TPU v7x, 32 devices: a whole 2x2x4 slice. The times are simulated.
32 devices in a mesh: frames: 8 (over y, x, core), pos: 4 (over z).
Axes of the slice: x: 2, y: 2, z: 4, core: 2. Of those that a mesh axis runs over, the one named last changes fastest.
Arguments:
- frames_in: bfloat16 [512, 16, 1024], P(('frames', 'pos')), may hold values from -6 to 6
- frame_valid: int32 [512], P(('frames', 'pos')), may hold values 0 or 1
- last_position: int32 [512], P(('frames', 'pos')), may hold values from 0 to 15
- weight_qkv: bfloat16 [16, 1024, 3072], P('pos', 'frames'), may hold values from -0.1875 to 0.1875
- weight_out: bfloat16 [16, 1024, 1024], P('pos', 'frames'), may hold values from -0.5 to 0.5
- weight_ffn: bfloat16 [16, 1024, 5632], P('pos', 'frames'), may hold values from -0.1875 to 0.1875
- weight_down: bfloat16 [16, 2816, 1024], P('pos', 'frames'), may hold values from -0.109375 to 0.109375
- gain_attn: bfloat16 [16, 1024], P('pos', 'frames'), may hold values from 0.5 to 1.5
- gain_ffn: bfloat16 [16, 1024], P('pos', 'frames'), may hold values from 0.5 to 1.5
- grad_out: bfloat16 [512, 16, 1024], P(('frames', 'pos')), may hold values from -6 to 6
Outputs:
- output: bfloat16 [512, 16, 1024], P(('frames', 'pos'))
- grad_input: bfloat16 [512, 16, 1024], P(('frames', 'pos'))
- grad_qkv: float32 [16, 1024, 3072], P('pos', 'frames')
- grad_wout: float32 [16, 1024, 1024], P('pos', 'frames')
- grad_ffn: float32 [16, 1024, 5632], P('pos', 'frames')
- grad_down: float32 [16, 2816, 1024], P('pos', 'frames')
- grad_gain_attn: float32 [16, 1024], P('pos', 'frames')
- grad_gain_ffn: float32 [16, 1024], P('pos', 'frames')
All inputs are finite; a program needn't handle non-finite values. No bound on the sum of `frame_valid` on one device may be relied on, other than what follows from the above.
Results may differ from a plain program's by a relative error of at most 0.015.
Values may be sent and summed in bfloat16 or wider, within the bound.
No kernel may reach another device: no remote copies, remote signals or barrier semaphores. Data moves between devices by JAX's collectives and lax.ppermute only.
A program may use at most 384 MiB of HBM per device.

v0:
```python
import jax
import jax.numpy as jnp
from jax import lax
from jax.sharding import PartitionSpec as P

HEADS = 16
HEAD = 64
FF = 2816


EPSILON = 1e-06
NEGATIVE = -1e30


def rms_forward(values, gain_row):
    inverse = lax.rsqrt(jnp.mean(values * values, axis=-1, keepdims=True) + EPSILON)
    normed = values * inverse
    return (normed * gain_row[None], normed, inverse)


def rms_backward(upstream, normed, inverse, gain_row):
    scaled = upstream * gain_row[None]
    row_inner = jnp.mean(scaled * normed, axis=-1, keepdims=True)
    return (inverse * (scaled - normed * row_inner), jnp.sum(upstream * normed, axis=0))


def project(pattern, left_side, right_side):
    return jnp.einsum(pattern, left_side, right_side, preferred_element_type=jnp.float32)


def split_heads(qkv_frames):
    frames = qkv_frames.shape[0]
    length = qkv_frames.shape[1]
    pieces = qkv_frames.reshape(frames, length, 3, HEADS, HEAD)
    return (pieces[:, :, 0], pieces[:, :, 1], pieces[:, :, 2])


def masked_scores(query, key_part):
    raw_scores = project("fqhe,fkhe->fhqk", query, key_part) * HEAD ** (-0.5)
    length = raw_scores.shape[-1]
    allowed = lax.broadcasted_iota(jnp.int32, (length, length), 0) >= lax.broadcasted_iota(
        jnp.int32, (length, length), 1
    )
    return jnp.where(allowed, raw_scores, NEGATIVE)


def on_device(
    frames_in,
    frame_valid,
    last_position,
    weight_qkv,
    weight_out,
    weight_ffn,
    weight_down,
    gain_attn,
    gain_ffn,
    grad_out,
):
    scale = HEAD ** (-0.5)
    slot_index = lax.broadcasted_iota(jnp.int32, (frames_in.shape[0], frames_in.shape[1]), 1)
    live_mask = (frame_valid[:, None] > 0) & (slot_index <= last_position[:, None])
    pos_rows = lax.all_to_all(frames_in, "pos", split_axis=1, concat_axis=0, tiled=True)
    full_qkv, full_out, full_gain_a = (
        lax.all_gather(weight_qkv, "frames", axis=1, tiled=True),
        lax.all_gather(weight_out, "frames", axis=1, tiled=True),
        lax.all_gather(gain_attn, "frames", axis=1, tiled=True),
    )
    gain_one = full_gain_a.astype(jnp.float32)
    residual = pos_rows.astype(jnp.float32)
    scaled_one, normed_one, inverse_one = rms_forward(residual, gain_one)
    normed_one_low = scaled_one.astype(jnp.bfloat16)
    qkv_rows = project("rpd,pde->rpe", normed_one_low, full_qkv).astype(jnp.bfloat16)
    qkv_frames = lax.all_to_all(qkv_rows, "pos", split_axis=0, concat_axis=1, tiled=True)
    query, key_part, value_part = split_heads(qkv_frames)
    scores = masked_scores(query, key_part)
    row_top = jnp.max(scores, axis=-1, keepdims=True)
    exponent = jnp.exp(scores - row_top)
    row_total = jnp.sum(exponent, axis=-1, keepdims=True)
    log_total = row_top + jnp.log(row_total)
    attend_low = (exponent / row_total).astype(jnp.bfloat16)
    mixed_heads = project("fhqk,fkhe->fqhe", attend_low, value_part)
    mixed_low = mixed_heads.reshape(frames_in.shape).astype(jnp.bfloat16)
    mixed_rows = lax.all_to_all(mixed_low, "pos", split_axis=1, concat_axis=0, tiled=True)
    middle = residual + project("rpd,pde->rpe", mixed_rows, full_out)
    full_ffn, full_down, full_gain_f = (
        lax.all_gather(weight_ffn, "frames", axis=1, tiled=True),
        lax.all_gather(weight_down, "frames", axis=1, tiled=True),
        lax.all_gather(gain_ffn, "frames", axis=1, tiled=True),
    )
    gain_two = full_gain_f.astype(jnp.float32)
    scaled_two, normed_two, inverse_two = rms_forward(middle, gain_two)
    normed_two_low = scaled_two.astype(jnp.bfloat16)
    gate_up = project("rpd,pde->rpe", normed_two_low, full_ffn)
    gate = gate_up[..., :FF]
    upward = gate_up[..., FF:]
    gate_sig = jax.nn.sigmoid(gate)
    hidden = (gate * gate_sig * upward).astype(jnp.bfloat16)
    result = middle + project("rpf,pfd->rpd", hidden, full_down)
    result_frames = lax.all_to_all(
        result.astype(jnp.bfloat16), "pos", split_axis=0, concat_axis=1, tiled=True
    )
    output = jnp.where(live_mask[:, :, None], result_frames, jnp.zeros_like(result_frames))
    upstream = jnp.where(live_mask[:, :, None], grad_out, jnp.zeros_like(grad_out))
    upstream_rows = lax.all_to_all(upstream, "pos", split_axis=1, concat_axis=0, tiled=True)
    back_ffn, back_down = (
        lax.all_gather(weight_ffn, "frames", axis=1, tiled=True),
        lax.all_gather(weight_down, "frames", axis=1, tiled=True),
    )
    grad_hidden = project("rpd,pfd->rpf", upstream_rows, back_down)
    term_down = project("rpf,rpd->pfd", hidden, upstream_rows)
    grad_upward = grad_hidden * gate * gate_sig
    grad_gate = grad_hidden * upward * gate_sig * (1.0 + gate * (1.0 - gate_sig))
    grad_gate_up = jnp.concatenate([grad_gate, grad_upward], axis=-1).astype(jnp.bfloat16)
    grad_normed_two = project("rpe,pde->rpd", grad_gate_up, back_ffn)
    term_ffn = project("rpd,rpe->pde", normed_two_low, grad_gate_up)
    grad_middle_norm, term_gain_f = rms_backward(grad_normed_two, normed_two, inverse_two, gain_two)
    grad_middle = upstream_rows.astype(jnp.float32) + grad_middle_norm
    sum_ffn, sum_down, sum_gain_f = (
        lax.psum_scatter(
            term_ffn.astype(jnp.bfloat16), "frames", scatter_dimension=1, tiled=True
        ).astype(jnp.float32),
        lax.psum_scatter(
            term_down.astype(jnp.bfloat16), "frames", scatter_dimension=1, tiled=True
        ).astype(jnp.float32),
        lax.psum_scatter(
            term_gain_f.astype(jnp.bfloat16), "frames", scatter_dimension=1, tiled=True
        ).astype(jnp.float32),
    )
    back_qkv, back_out = (
        lax.all_gather(weight_qkv, "frames", axis=1, tiled=True),
        lax.all_gather(weight_out, "frames", axis=1, tiled=True),
    )
    grad_branch = grad_middle.astype(jnp.bfloat16)
    grad_mixed = project("rpe,pde->rpd", grad_branch, back_out).astype(jnp.bfloat16)
    term_out = project("rpd,rpe->pde", mixed_rows, grad_branch)
    grad_mixed_frames = lax.all_to_all(grad_mixed, "pos", split_axis=0, concat_axis=1, tiled=True)
    grad_heads = grad_mixed_frames.reshape(query.shape)
    again_scores = masked_scores(query, key_part)
    attend = jnp.exp(again_scores - log_total)
    grad_value = project("fhqk,fqhe->fkhe", attend.astype(jnp.bfloat16), grad_heads)
    grad_attend = project("fqhe,fkhe->fhqk", grad_heads, value_part)
    row_inner = jnp.sum(attend * grad_attend, axis=-1, keepdims=True)
    grad_scores = (attend * (grad_attend - row_inner)).astype(jnp.bfloat16)
    grad_query = project("fhqk,fkhe->fqhe", grad_scores, key_part) * scale
    grad_key = project("fhqk,fqhe->fkhe", grad_scores, query) * scale
    grad_qkv_frames = (
        jnp.stack([grad_query, grad_key, grad_value], axis=2)
        .reshape(qkv_frames.shape)
        .astype(jnp.bfloat16)
    )
    grad_qkv_rows = lax.all_to_all(grad_qkv_frames, "pos", split_axis=1, concat_axis=0, tiled=True)
    grad_normed_one = project("rpe,pde->rpd", grad_qkv_rows, back_qkv)
    term_qkv = project("rpd,rpe->pde", normed_one_low, grad_qkv_rows)
    grad_input_norm, term_gain_a = rms_backward(grad_normed_one, normed_one, inverse_one, gain_one)
    grad_rows = (grad_middle + grad_input_norm).astype(jnp.bfloat16)
    grad_frames = lax.all_to_all(grad_rows, "pos", split_axis=0, concat_axis=1, tiled=True)
    sum_qkv, sum_out, sum_gain_a = (
        lax.psum_scatter(
            term_qkv.astype(jnp.bfloat16), "frames", scatter_dimension=1, tiled=True
        ).astype(jnp.float32),
        lax.psum_scatter(
            term_out.astype(jnp.bfloat16), "frames", scatter_dimension=1, tiled=True
        ).astype(jnp.float32),
        lax.psum_scatter(
            term_gain_a.astype(jnp.bfloat16), "frames", scatter_dimension=1, tiled=True
        ).astype(jnp.float32),
    )
    return (output, grad_frames, sum_qkv, sum_out, sum_ffn, sum_down, sum_gain_a, sum_gain_f)


def solution(mesh):
    placed = (
        P(("frames", "pos"), None, None),
        P(("frames", "pos")),
        P(("frames", "pos")),
        P("pos", "frames", None),
        P("pos", "frames", None),
        P("pos", "frames", None),
        P("pos", "frames", None),
        P("pos", "frames"),
        P("pos", "frames"),
        P(("frames", "pos"), None, None),
    )
    return jax.shard_map(
        on_device,
        mesh=mesh,
        in_specs=placed,
        out_specs=(
            P(("frames", "pos"), None, None),
            P(("frames", "pos"), None, None),
            P("pos", "frames", None),
            P("pos", "frames", None),
            P("pos", "frames", None),
            P("pos", "frames", None),
            P("pos", "frames"),
            P("pos", "frames"),
        ),
        check_vma=False,
    )
```

profile of v0, /device:TPU:0, one launch (start us, length us, event | category | flops | bytes accessed | tf_op | source)
XLA Modules:
  0.0 1377.5 jit_solution(14971009679618732410)
XLA Ops:
  11.1 6.3 all-to-all-start
  17.4 8.9 all_gather.22
  26.3 5.6 all-to-all-done
  32.6 105.4 %all-gather.5.cloned.1.call-done = bf16[4,1024,3072]{2,1,0:T(8,128)(2,1)} async-done(((bf16[4,128,3072]{2,1,0:T(8,128)(2,1)}), bf16[4,1024,3072]{2,1,0:T(8,128)(2,1)}) %all-gather.5.cloned.1.call-update) | async-done | bytes 25165840 | tf_op jit(solution)/shard_map/all_gather | solution.py:64
  138.0 12.6 fusion
  158.8 36.3 %all-to-all-done.1 = bf16[64,4,3072]{2,1,0:T(4,128)(2,1)} async-done(((bf16[64,4,3072]{2,1,0:T(4,128)(2,1)}), bf16[64,4,3072]{2,1,0:T(4,128)(2,1)}, u32[]{:S(2)}, u32[]{:S(2)}) %all-to-all-start.1) | async-done | bytes 1572896 | tf_op jit(solution)/shard_map/all_to_all | solution.py:73
  202.5 5.2 reshape.117
  216.0 5.0 all-to-all-start.2
  221.1 9.2 all_gather.25
  235.5 5.2 multiply_reduce_fusion.5
  240.8 169.6 %all-gather.9.cloned.1.call-done = bf16[4,1024,5632]{2,1,0:T(8,128)(2,1)} async-done(((bf16[4,128,5632]{2,1,0:T(8,128)(2,1)}), bf16[4,1024,5632]{2,1,0:T(8,128)(2,1)}) %all-gather.9.cloned.1.call-update) | async-done | bytes 46137360 | tf_op jit(solution)/shard_map/all_gather | solution.py:86
  410.4 23.7 %convolution_bitcast_fusion = f32[64,4,5632]{2,0,1:T(8,128)} fusion(bf16[4,1024,5632]{2,1,0:T(8,128)(2,1)} %all-gather.9.cloned.1.call-done, f32[64,4,1024]{2,0,1:T(8,128)S(1)} %get-tuple-element.29, f32[4,1024]{1,0:T(4,128)S(1)} %convert_element_type.128, f32[64,4]{0,1:T(4,128)S(1)} %add_rsqrt_fusion.1), kind=kOutput, calls=%fused_computation.3 | convolution fusion | flops 2953576448 | bytes 52970496 | tf_op jit(solution)/shard_map/rpd,pde->rpe/dot_general | solution.py:28
  434.1 94.5 %all-gather.11.cloned.1.call-done = bf16[4,2816,1024]{2,1,0:T(8,128)(2,1)} async-done(((bf16[4,352,1024]{2,1,0:T(8,128)(2,1)}), bf16[4,2816,1024]{2,1,0:T(8,128)(2,1)}) %all-gather.11.cloned.1.call-update) | async-done | bytes 23068688 | tf_op jit(solution)/shard_map/all_gather | solution.py:87
  528.7 14.3 %multiply_convert_fusion.1 = (bf16[64,4,2816]{2,0,1:T(8,128)(2,1)}, bf16[64,4,2816]{2,0,1:T(8,128)(2,1)}, bf16[64,4,2816]{2,0,1:T(8,128)(2,1)S(1)}) fusion(f32[64,4,5632]{2,0,1:T(8,128)} %convolution_bitcast_fusion, bf16[64,4,1024]{2,0,1:T(8,128)(2,1)} %bitcast.141, bf16[4,2816,1024]{2,1,0:T(8,128)(2,1)} %all-gather.11.cloned.1.call-done), kind=kOutput, calls=%fused_computation.11 | convolution fusion | flops 1487929344 | bytes 33685504 | tf_op jit(solution)/shard_map/rpd,pfd->rpf/dot_general | solution.py:28
  542.9 21.8 %multiply_reduce_fusion.1 = (bf16[4,1024]{1,0:T(4,128)(2,1)}, f32[64,4]{0,1:T(4,128)}, f32[64,4,1024]{2,0,1:T(8,128)}) fusion(f32[64,4,1024]{2,0,1:T(8,128)S(1)} %get-tuple-element.29, f32[64,4]{0,1:T(4,128)} %copy-done.15, f32[4,1024]{1,0:T(4,128)S(1)} %convert_element_type.128, bf16[4,1024,5632]{2,1,0:T(8,128)(2,1)} %all-gather.9.cloned.1.call-done, ...), kind=kOutput, calls=%fused_computation.45 | convolution fusion | flops 2960125696 | bytes 51144704 | tf_op jit(solution)/shard_map/rpe,pde->rpd/dot_general | solution.py:28
  567.2 6.4 fusion.12
  581.2 13.4 all-to-all-done.5
  621.5 34.9 %all-to-all-done.6 = bf16[16,16,3072]{2,0,1:T(8,128)(2,1)} async-done(((bf16[16,16,3072]{2,0,1:T(8,128)(2,1)}), bf16[16,16,3072]{2,0,1:T(8,128)(2,1)}, u32[]{:S(2)}, u32[]{:S(2)}) %all-to-all-start.6) | async-done | bytes 1572896 | tf_op jit(solution)/shard_map/all_to_all | solution.py:151
  659.1 14.5 %multiply_reduce_fusion.2 = (bf16[4,1024]{1,0:T(4,128)(2,1)}, f32[64,4]{0,1:T(4,128)}, f32[64,4,1024]{2,0,1:T(8,128)}) fusion(f32[64,4,1024]{2,0,1:T(8,128)S(1)} %bitcast_multiply_fusion, f32[4,1024]{1,0:T(4,128)} %copy-done.12, bf16[64,4,3072]{2,0,1:T(8,128)(2,1)} %bitcast.135, bf16[4,1024,3072]{2,1,0:T(8,128)(2,1)} %all-gather.5.cloned.1.call-done), kind=kOutput, calls=%fused_computation.46 | convolution fusion | flops 1611919104 | bytes 28861440 | tf_op jit(solution)/shard_map/rpe,pde->rpd/dot_general | solution.py:28
  675.4 7.2 convolution_convert_fusion.3
  682.7 12.0 convolution_convert_fusion.2
  694.8 13.3 convolution_convert_fusion.1
  708.8 24.2 %convolution_convert_fusion = bf16[4,1024,5632]{2,1,0:T(8,128)(2,1)} fusion(bf16[64,4,2816]{2,0,1:T(8,128)(2,1)} %get-tuple-element.21, bf16[64,4,2816]{2,0,1:T(8,128)(2,1)} %get-tuple-element.20, f32[64,4,1024]{2,0,1:T(8,128)S(1)} %get-tuple-element.29, f32[4,1024]{1,0:T(4,128)S(1)} %convert_element_type.128, f32[64,4]{0,1:T(4,128)S(1)} %copy-done.16), kind=kOutput, calls=%fused_computation | convolution fusion | flops 2982412288 | bytes 50086912 | tf_op jit(solution)/shard_map/rpd,rpe->pde/dot_general | solution.py:28
  733.0 12.4 fusion.11
  754.0 10.1 all-to-all-done.3
  771.9 9.7 all-to-all-done.7
  785.5 146.9 %reduce-scatter.17.cloned.1.call-done = bf16[4,352,1024]{2,1,0:T(8,128)(2,1)} async-done(((bf16[4,2816,1024]{2,1,0:T(8,128)(2,1)}), bf16[4,352,1024]{2,1,0:T(8,128)(2,1)}) %reduce-scatter.17.cloned.1.call-update) | async-done | bytes 2883600 | tf_op jit(solution)/shard_map/reduce_scatter | solution.py:122
  932.4 5.1 convert_element_type.147
  937.5 155.9 %reduce-scatter.11.cloned.1.call-done = bf16[4,128,3072]{2,1,0:T(8,128)(2,1)} async-done(((bf16[4,1024,3072]{2,1,0:T(8,128)(2,1)}), bf16[4,128,3072]{2,1,0:T(8,128)(2,1)}) %reduce-scatter.11.cloned.1.call-update) | async-done | bytes 3145744 | tf_op jit(solution)/shard_map/reduce_scatter | solution.py:158
  1093.4 5.4 convert_element_type.141
  1098.8 262.9 %reduce-scatter.15.cloned.1.call-done = bf16[4,128,5632]{2,1,0:T(8,128)(2,1)} async-done(((bf16[4,1024,5632]{2,1,0:T(8,128)(2,1)}), bf16[4,128,5632]{2,1,0:T(8,128)(2,1)}) %reduce-scatter.15.cloned.1.call-update) | async-done | bytes 5767184 | tf_op jit(solution)/shard_map/reduce_scatter | solution.py:119
  1361.7 8.6 convert_element_type.145
  (145 shorter events, 95.8 us)
Async XLA Ops:
  7.2 130.8 %all-gather.5.cloned.1.call-start = ((), (), s32[]{:S(2)}) async-start(), calls=%async_computation.14 | async-start | bytes 28311552 | tf_op jit(solution)/shard_map/all_gather | solution.py:64
  7.9 227.6 %all-gather.7.cloned.1.call-start = ((), (), s32[]{:S(2)}) async-start(), calls=%async_computation.15 | async-start | bytes 9437184 | tf_op jit(solution)/shard_map/all_gather | solution.py:65
  8.7 401.7 %all-gather.9.cloned.1.call-start = ((), (), s32[]{:S(2)}) async-start(), calls=%async_computation.16 | async-start | bytes 51904512 | tf_op jit(solution)/shard_map/all_gather | solution.py:86
  9.4 8.0 copy-start.24
  9.4 519.3 %all-gather.11.cloned.1.call-start = ((), (), s32[]{:S(2)}) async-start(), calls=%async_computation.17 | async-start | bytes 25952256 | tf_op jit(solution)/shard_map/all_gather | solution.py:87
  11.1 20.8 %all-to-all-start = ((bf16[16,16,1024]{2,0,1:T(8,128)(2,1)}), bf16[16,16,1024]{2,0,1:T(8,128)(2,1)S(1)}, u32[]{:S(2)}, u32[]{:S(2)}) async-start(bf16[16,16,1024]{2,0,1:T(8,128)(2,1)} %copy.63), calls=%async_computation | async-start | bytes 1048576 | tf_op jit(solution)/shard_map/all_to_all | solution.py:62
  26.3 124.3 %copy-start.12 = (f32[4,1024]{1,0:T(4,128)}, f32[4,1024]{1,0:T(4,128)S(1)}, u32[]{:S(2)}) copy-start(f32[4,1024]{1,0:T(4,128)S(1)} %convert_element_type.120) | copy-start | bytes 49156
  32.3 105.7 %copy-start.21 = (f32[64,4]{0,1:T(4,128)}, f32[64,4]{0,1:T(4,128)S(1)}, u32[]{:S(2)}) copy-start(f32[64,4]{0,1:T(4,128)S(1)} %rsqrt.20) | copy-start | bytes 3076
  32.4 203.1 %copy-start.2 = (f32[16,4,4,1024]{3,0,1,2:T(8,128)}, f32[16,4,4,1024]{3,0,1,2:T(8,128)S(1)}, u32[]{:S(2)}) copy-start(f32[16,4,4,1024]{3,0,1,2:T(8,128)S(1)} %copy.64) | copy-start | bytes 3145732
  150.6 7.0 copy-start.27
  150.6 7.0 copy-start.26
  150.6 7.0 copy-start.20
  153.0 42.1 %all-to-all-start.1 = ((bf16[64,4,3072]{2,1,0:T(4,128)(2,1)}), bf16[64,4,3072]{2,1,0:T(4,128)(2,1)}, u32[]{:S(2)}, u32[]{:S(2)}) async-start(bf16[64,4,3072]{2,1,0:T(4,128)(2,1)} %copy.68), calls=%async_computation.1 | async-start | bytes 3145728 | tf_op jit(solution)/shard_map/all_to_all | solution.py:73
  157.7 50.1 %copy-start.22 = (pred[16,16]{0,1:T(8,128)(4,1)}, pred[16,16]{0,1:T(8,128)(4,1)S(1)}, u32[]{:S(2)}) copy-start(pred[16,16]{0,1:T(8,128)(4,1)S(1)} %fusion.21) | copy-start | bytes 772
  195.1 20.9 %all-to-all-start.4 = ((bf16[16,16,1024]{2,0,1:T(8,128)(2,1)}), bf16[16,16,1024]{2,0,1:T(8,128)(2,1)}, u32[]{:S(2)}, u32[]{:S(2)}) async-start(bf16[16,16,1024]{2,0,1:T(8,128)(2,1)} %copy_select_fusion), calls=%async_computation.4 | async-start | bytes 1048576 | tf_op jit(solution)/shard_map/all_to_all | solution.py:104
  214.2 6.8 copy-start.25
  216.0 18.7 %all-to-all-start.2 = ((bf16[16,16,1024]{2,0,1:T(8,128)(2,1)}), bf16[16,16,1024]{2,0,1:T(8,128)(2,1)S(1)}, u32[]{:S(2)}, u32[]{:S(2)}) async-start(bf16[16,16,1024]{2,0,1:T(8,128)(2,1)} %reshape.126), calls=%async_computation.2 | async-start | bytes 1048576 | tf_op jit(solution)/shard_map/all_to_all | solution.py:83
  240.8 193.3 %copy-start.15 = (f32[64,4]{0,1:T(4,128)}, f32[64,4]{0,1:T(4,128)S(1)}, u32[]{:S(2)}) copy-start(f32[64,4]{0,1:T(4,128)S(1)} %add_rsqrt_fusion.1) | copy-start | bytes 3076
  567.1 6.4 copy-start.4
  574.8 19.8 %all-to-all-start.5 = ((bf16[64,4,1024]{2,1,0:T(4,128)(2,1)}), bf16[64,4,1024]{2,1,0:T(4,128)(2,1)}, u32[]{:S(2)}, u32[]{:S(2)}) async-start(bf16[64,4,1024]{2,1,0:T(4,128)(2,1)} %copy.81), calls=%async_computation.5 | async-start | bytes 1048576 | tf_op jit(solution)/shard_map/all_to_all | solution.py:136
  615.4 41.0 %all-to-all-start.6 = ((bf16[16,16,3072]{2,0,1:T(8,128)(2,1)}), bf16[16,16,3072]{2,0,1:T(8,128)(2,1)}, u32[]{:S(2)}, u32[]{:S(2)}) async-start(bf16[16,16,3072]{2,0,1:T(8,128)(2,1)} %reshape.127), calls=%async_computation.6 | async-start | bytes 3145728 | tf_op jit(solution)/shard_map/all_to_all | solution.py:151
  619.8 147.8 %reduce-scatter.21.cloned.1.call-start = ((), (), s32[]{:S(2)}) async-start(), calls=%async_computation.23 | async-start | bytes 294912
  621.4 149.0 %reduce-scatter.19.cloned.1.call-start = ((), (), s32[]{:S(2)}) async-start(), calls=%async_computation.22 | async-start | bytes 294912
  675.2 107.5 %reduce-scatter.13.cloned.1.call-start = ((), (), s32[]{:S(2)}) async-start(), calls=%async_computation.19 | async-start | bytes 9437184 | tf_op jit(solution)/shard_map/reduce_scatter | solution.py:161
  682.6 249.8 %reduce-scatter.17.cloned.1.call-start = ((), (), s32[]{:S(2)}) async-start(), calls=%async_computation.21 | async-start | bytes 25952256 | tf_op jit(solution)/shard_map/reduce_scatter | solution.py:122
  694.7 398.6 %reduce-scatter.11.cloned.1.call-start = ((), (), s32[]{:S(2)}) async-start(), calls=%async_computation.18 | async-start | bytes 28311552 | tf_op jit(solution)/shard_map/reduce_scatter | solution.py:158
  708.1 653.6 %reduce-scatter.15.cloned.1.call-start = ((), (), s32[]{:S(2)}) async-start(), calls=%async_computation.20 | async-start | bytes 51904512 | tf_op jit(solution)/shard_map/reduce_scatter | solution.py:119
  733.0 17.8 %copy-start.3 = (f32[16,4,4,1024]{3,0,1,2:T(8,128)S(1)}, f32[16,4,4,1024]{3,0,1,2:T(8,128)}, u32[]{:S(2)}) copy-start(f32[16,4,4,1024]{3,0,1,2:T(8,128)} %copy-done.2) | copy-start | bytes 3145732
  733.0 17.8 %copy-start.13 = (f32[4,1024]{1,0:T(4,128)S(1)}, f32[4,1024]{1,0:T(4,128)}, u32[]{:S(2)}) copy-start(f32[4,1024]{1,0:T(4,128)} %copy-done.12) | copy-start | bytes 49156
  746.6 17.5 %all-to-all-start.3 = ((bf16[64,4,1024]{2,1,0:T(4,128)(2,1)}), bf16[64,4,1024]{2,1,0:T(4,128)(2,1)S(1)}, u32[]{:S(2)}, u32[]{:S(2)}) async-start(bf16[64,4,1024]{2,1,0:T(4,128)(2,1)} %copy.77), calls=%async_computation.3 | async-start | bytes 1048576 | tf_op jit(solution)/shard_map/all_to_all | solution.py:99
  750.8 18.4 %copy-start.23 = (pred[16,16]{0,1:T(8,128)(4,1)S(1)}, pred[16,16]{0,1:T(8,128)(4,1)}, u32[]{:S(2)}) copy-start(pred[16,16]{0,1:T(8,128)(4,1)} %copy-done.22) | copy-start | bytes 772
  764.1 17.4 %all-to-all-start.7 = ((bf16[64,4,1024]{2,1,0:T(4,128)(2,1)}), bf16[64,4,1024]{2,1,0:T(4,128)(2,1)S(1)}, u32[]{:S(2)}, u32[]{:S(2)}) async-start(bf16[64,4,1024]{2,1,0:T(4,128)(2,1)} %copy.89), calls=%async_computation.7 | async-start | bytes 1048576 | tf_op jit(solution)/shard_map/all_to_all | solution.py:156
  (14 other events, 28.7 us)
Sparse Core Ops, SparseCore 0:
  9.9 128.0 all-gather.4
  139.9 54.3 all-gather.6
  196.2 214.1 all-gather.8
  412.2 116.4 all-gather.10
  623.3 34.0 reduce-scatter.20
  675.3 31.7 reduce-scatter.18
  711.1 71.2 reduce-scatter.12
  786.5 145.8 reduce-scatter.16
  936.5 156.8 reduce-scatter.10
  1097.3 264.3 reduce-scatter.14
where the time goes:
time: 1380 us
  waiting for transfers between devices  1050 us (76%)
  matrix products  177 us (13%)
  local copies, waits for them, and re-layouts  46.6 us (3%)
  starting transfers between devices  37.2 us (3%)
  other arithmetic  33.2 us (2%)
  blocking collectives  18.1 us (1%)
  between operations  15.1 us (1%)
    reduce_scatter x1, waiting for transfers between devices, on_device(): lax.psum_scatter(term_ffn.astype(jnp.bfloat16), 'frames', scatter_dimensi...  263 us
    dot_general x18, matrix products, project(): jnp.einsum(pattern, left_side, right_side, preferred_element_type=jnp.flo...  177 us
    all_gather x1, waiting for transfers between devices, on_device(): lax.all_gather(weight_ffn, 'frames', axis=1, tiled=True)  170 us
    reduce_scatter x1, waiting for transfers between devices, on_device(): lax.psum_scatter(term_qkv.astype(jnp.bfloat16), 'frames', scatter_dimensi...  156 us
    reduce_scatter x1, waiting for transfers between devices, on_device(): lax.psum_scatter(term_down.astype(jnp.bfloat16), 'frames', scatter_dimens...  147 us
    all_gather x1, waiting for transfers between devices, on_device(): lax.all_gather(weight_qkv, 'frames', axis=1, tiled=True)  105 us
    all_gather x1, waiting for transfers between devices, on_device(): lax.all_gather(weight_down, 'frames', axis=1, tiled=True)  94.5 us
    all_to_all x1, waiting for transfers between devices, on_device(): lax.all_to_all(qkv_rows, 'pos', split_axis=0, concat_axis=1, tiled=True)  36.3 us
  transfers between devices with their start and end apart: 18, of which 13 were waited for; matrix products, arithmetic and copies ran while one was open for 13% of the time, Pallas kernels for 0%

commit v1 on v0

v1 whole, which is shorter than its diff:
```python
import jax
import jax.numpy as jnp
from jax import lax
from jax.sharding import Mesh, PartitionSpec as P

HEAD = 64
EPSILON = 1e-06
NEGATIVE = -1e30

ROWS = ("pos", "spot")
PLANE = ("spot", "half")


def project(left, right, contract):
    return lax.dot_general(left, right, (contract, ((), ())), preferred_element_type=jnp.float32)


def plain(left, right):
    return project(left, right, ((1,), (0,)))


def by_columns(left, right):
    return project(left, right, ((1,), (1,)))


def over_rows(left, right):
    return project(left, right, ((0,), (0,)))


def rms(values):
    inverse = lax.rsqrt(jnp.mean(values * values, axis=-1, keepdims=True) + EPSILON)
    return values * inverse, inverse


def rms_backward(upstream, normed, inverse, gain):
    scaled = upstream * gain
    inner = jnp.mean(scaled * normed, axis=-1, keepdims=True)
    return inverse * (scaled - normed * inner)


def shift(value, step, size):
    return lax.ppermute(value, "half", [(u, (u + step) % size) for u in range(size)])


def gather_halves(own, size):
    return jnp.stack([own] + [shift(own, step, size) for step in range(1, size)])


def sum_own(partial, size):
    total = partial[0]
    for step in range(1, size):
        total = total + shift(partial[step], -step, size)
    return total


def sum_all(partial, size):
    if size == 2:
        return partial + shift(partial, 1, size)[::-1]
    return gather_halves(sum_own(partial, size), size)


def to_spots(weight, local, halves, plane):
    mine = lax.axis_index("spot")
    index = lax.axis_index(PLANE)
    out = jnp.zeros((local,) + weight.shape[1:], weight.dtype)
    for step in range(local):
        pairs = [(f, (f % local + step) % local * halves + f // local) for f in range(plane)]
        piece = lax.dynamic_index_in_dim(weight, (index + step) % local, 0, keepdims=False)
        piece = lax.ppermute(piece, PLANE, pairs)
        out = lax.dynamic_update_index_in_dim(out, piece, (mine - step) % local, 0)
    return out.reshape(-1, weight.shape[-1])


def from_spots(grad, local, halves, plane):
    mine = lax.axis_index("spot")
    index = lax.axis_index(PLANE)
    grad = grad.reshape(local, -1, grad.shape[-1])
    pieces = []
    for step in range(local):
        pairs = [((f % local + step) % local * halves + f // local, f) for f in range(plane)]
        piece = lax.dynamic_index_in_dim(grad, (mine - step) % local, 0, keepdims=False)
        pieces.append(lax.ppermute(piece, PLANE, pairs))
    pieces = jnp.stack(pieces)
    placed = [
        lax.dynamic_index_in_dim(pieces, (position - index) % local, 0, keepdims=False)
        for position in range(local)
    ]
    return jnp.stack(placed).astype(jnp.float32)


def columns_to_spots(weight, groups, halves):
    local, depth, width = weight.shape
    split = weight.reshape(local, depth, groups, halves, width // groups // halves)
    split = jnp.transpose(split, (0, 3, 1, 2, 4)).reshape(local * halves, depth, width // halves)
    moved = lax.all_to_all(split, PLANE, split_axis=0, concat_axis=0, tiled=True)
    return moved.reshape(-1, width // halves)


def columns_from_spots(grad, groups, halves, plane):
    depth = grad.shape[0] // plane
    width = grad.shape[1] * halves
    moved = lax.all_to_all(
        grad.reshape(plane, depth, grad.shape[1]), PLANE, split_axis=0, concat_axis=0, tiled=True
    )
    moved = moved.reshape(plane // halves, halves, depth, groups, width // groups // halves)
    return jnp.transpose(moved, (0, 2, 3, 1, 4)).reshape(-1, depth, width).astype(jnp.float32)


def rows_to_spots(values):
    moved = lax.all_to_all(values, ROWS, split_axis=1, concat_axis=0, tiled=True)
    return moved.reshape(moved.shape[0], moved.shape[2])


def rows_from_spots(values):
    return lax.all_to_all(values[:, None], ROWS, split_axis=0, concat_axis=1, tiled=True)


def swap(values, blocks):
    return lax.all_to_all(
        values.reshape(blocks, -1, values.shape[-1]), ROWS, split_axis=0, concat_axis=0, tiled=True
    )


def scores_of(query, key_part):
    raw = jnp.einsum("qfhe,kfhe->fhqk", query, key_part, preferred_element_type=jnp.float32)
    length = raw.shape[-1]
    allowed = lax.broadcasted_iota(jnp.int32, (length, length), 0) >= lax.broadcasted_iota(
        jnp.int32, (length, length), 1
    )
    return jnp.where(allowed, raw * HEAD ** (-0.5), NEGATIVE)


def pieces_of(qkv):
    positions, frames, width = qkv.shape
    pieces = qkv.reshape(positions, frames, 3, width // 3 // HEAD, HEAD)
    return pieces[:, :, 0], pieces[:, :, 1], pieces[:, :, 2]


def attend(qkv):
    query, key_part, value_part = pieces_of(qkv)
    scores = scores_of(query, key_part)
    top = jnp.max(scores, axis=-1, keepdims=True)
    exponent = jnp.exp(scores - top)
    total = jnp.sum(exponent, axis=-1, keepdims=True)
    low = (exponent / total).astype(jnp.bfloat16)
    mixed = jnp.einsum("fhqk,kfhe->qfhe", low, value_part, preferred_element_type=jnp.float32)
    return mixed.reshape(qkv.shape[0], qkv.shape[1], -1).astype(jnp.bfloat16), top + jnp.log(total)


def attend_backward(qkv, log_total, grad_mixed):
    query, key_part, value_part = pieces_of(qkv)
    grad_heads = grad_mixed.reshape(query.shape)
    f32 = jnp.float32
    probs = jnp.exp(scores_of(query, key_part) - log_total)
    grad_value = jnp.einsum(
        "fhqk,qfhe->kfhe", probs.astype(jnp.bfloat16), grad_heads, preferred_element_type=f32
    )
    grad_probs = jnp.einsum("qfhe,kfhe->fhqk", grad_heads, value_part, preferred_element_type=f32)
    inner = jnp.sum(probs * grad_probs, axis=-1, keepdims=True)
    grad_scores = (probs * (grad_probs - inner)).astype(jnp.bfloat16)
    scale = HEAD ** (-0.5)
    grad_query = jnp.einsum("fhqk,kfhe->qfhe", grad_scores, key_part, preferred_element_type=f32)
    grad_key = jnp.einsum("fhqk,qfhe->kfhe", grad_scores, query, preferred_element_type=f32)
    stacked = jnp.stack([grad_query * scale, grad_key * scale, grad_value], axis=2)
    return stacked.reshape(qkv.shape).astype(jnp.bfloat16)


def on_device(
    frames_in,
    frame_valid,
    last_position,
    weight_qkv,
    weight_out,
    weight_ffn,
    weight_down,
    gain_attn,
    gain_ffn,
    grad_out,
):
    f32, bf16 = jnp.float32, jnp.bfloat16
    frames, positions, depth = frames_in.shape
    local = weight_qkv.shape[0]
    plane = depth // weight_qkv.shape[1]
    halves = plane // local
    slot = lax.broadcasted_iota(jnp.int32, (frames, positions), 1)
    live = ((frame_valid[:, None] > 0) & (slot <= last_position[:, None]))[:, :, None]

    gains = jnp.stack([gain_attn, gain_ffn], axis=1)
    gains = jnp.repeat(gains, halves, axis=0)
    gains = lax.all_to_all(gains, PLANE, split_axis=0, concat_axis=0, tiled=True)
    gain_one, gain_two = jnp.transpose(gains, (1, 0, 2)).reshape(2, 1, depth).astype(f32)
    own_rows = rows_to_spots(frames_in)
    full_qkv = columns_to_spots(weight_qkv, 3, halves)
    full_out = to_spots(weight_out, local, halves, plane)
    upstream_own = rows_to_spots(jnp.where(live, grad_out, jnp.zeros_like(grad_out)))
    full_ffn = columns_to_spots(weight_ffn, 2, halves)
    full_down = to_spots(weight_down, local, halves, plane)

    own_count = own_rows.shape[0]
    count = own_count * halves
    rows = gather_halves(own_rows, halves).reshape(count, depth)
    residual = rows.astype(f32)
    unit_one, _ = rms(residual)
    normed_one = (unit_one * gain_one).astype(bf16)
    qkv_rows = plain(normed_one, full_qkv).astype(bf16)
    qkv = swap(qkv_rows, positions)
    mixed_frames, log_total = attend(qkv)
    mixed = swap(mixed_frames, positions).reshape(count, -1)
    branch = sum_all(plain(mixed, full_out).reshape(halves, own_count, depth), halves)
    middle = residual + branch.reshape(count, depth)

    unit_two, inverse_two = rms(middle)
    normed_two = (unit_two * gain_two).astype(bf16)
    gate_up = plain(normed_two, full_ffn)
    width = gate_up.shape[1] // 2
    gate, upward = gate_up[:, :width], gate_up[:, width:]
    gate_sig = jax.nn.sigmoid(gate)
    hidden = (gate * gate_sig * upward).astype(bf16)
    down = plain(hidden, full_down).reshape(halves, own_count, depth)
    result = middle[:own_count] + sum_own(down, halves)
    result = rows_from_spots(result.astype(bf16))
    output = jnp.where(live, result, jnp.zeros_like(result))

    upstream = gather_halves(upstream_own, halves).reshape(count, depth)
    sum_down = from_spots(over_rows(hidden, upstream).astype(bf16), local, halves, plane)
    grad_hidden = by_columns(upstream, full_down)
    grad_upward = grad_hidden * gate * gate_sig
    grad_gate = grad_hidden * upward * gate_sig * (1.0 + gate * (1.0 - gate_sig))
    grad_gate_up = jnp.concatenate([grad_gate, grad_upward], axis=-1).astype(bf16)
    sum_ffn = columns_from_spots(over_rows(normed_two, grad_gate_up).astype(bf16), 2, halves, plane)
    grad_normed_two = by_columns(grad_gate_up, full_ffn).reshape(halves, own_count, depth)
    grad_normed_two = sum_all(grad_normed_two, halves).reshape(count, depth)
    term_two = jnp.sum((grad_normed_two * unit_two)[:own_count], axis=0)
    grad_middle = upstream.astype(f32) + rms_backward(
        grad_normed_two, unit_two, inverse_two, gain_two
    )

    grad_branch = grad_middle.astype(bf16)
    grad_mixed = by_columns(grad_branch, full_out).astype(bf16)
    grad_qkv_frames = attend_backward(qkv, log_total, swap(grad_mixed, positions))
    sum_out = from_spots(over_rows(mixed, grad_branch).astype(bf16), local, halves, plane)
    grad_qkv_rows = swap(grad_qkv_frames, positions).reshape(count, -1)
    sum_qkv = columns_from_spots(
        over_rows(normed_one, grad_qkv_rows).astype(bf16), 3, halves, plane
    )
    grad_normed_one = by_columns(grad_qkv_rows, full_qkv).reshape(halves, own_count, depth)
    grad_normed_one = sum_own(grad_normed_one, halves)
    own_unit, own_inverse = rms(own_rows.astype(f32))
    term_one = jnp.sum(grad_normed_one * own_unit, axis=0)
    grad_rows = grad_middle[:own_count] + rms_backward(
        grad_normed_one, own_unit, own_inverse, gain_one
    )
    grad_input = rows_from_spots(grad_rows.astype(bf16))

    terms = jnp.stack([term_one, term_two]).reshape(2, plane, depth // plane)
    terms = lax.all_to_all(
        jnp.transpose(terms, (1, 0, 2)), PLANE, split_axis=0, concat_axis=0, tiled=True
    )
    terms = jnp.sum(terms.reshape(local, halves, 2, depth // plane), axis=1)
    return (output, grad_input, sum_qkv, sum_out, sum_ffn, sum_down, terms[:, 0], terms[:, 1])


def solution(mesh):
    plane, lines = mesh.shape["frames"], mesh.shape["pos"]

    def run(*arrays):
        local = arrays[0].shape[1] // lines
        inner = Mesh(
            mesh.devices.reshape(local, plane // local, lines), ("spot", "half", "pos")
        )
        by_frame = P(("spot", "half", "pos"))
        weight = P("pos", ("spot", "half"))
        return jax.shard_map(
            on_device,
            mesh=inner,
            in_specs=(by_frame,) * 3 + (weight,) * 6 + (by_frame,),
            out_specs=(by_frame,) * 2 + (weight,) * 6,
            check_vma=False,
        )(*arrays)

    return run
```

time: 1380 us -> 674 us (0.49)
  the two profiles are of different devices: /device:TPU:0 before, /device:TPU:13 now
where the time goes in v1:
time: 674 us; the launch traced here: 662 us
  waiting for transfers between devices  257 us (38%)
  starting transfers between devices  161 us (24%)
  local copies, waits for them, and re-layouts  156 us (23%)
  matrix products  52.6 us (8%)
  other arithmetic  33.4 us (5%)
    ppermute x8, waiting for transfers between devices, to_spots(): piece = lax.ppermute(piece, PLANE, pairs)  78.9 us
    all_to_all x4, waiting for transfers between devices, swap(): lax.all_to_all(values.reshape(blocks, -1, values.shape[-1]), ROWS, split_...  71 us
    convert_element_type x4, local copies, waits for them, and re-layouts, columns_from_spots(): jnp.transpose(moved, (0, 2, 3, 1, 4)).reshape(-1, depth, width)  51.7 us
    ppermute x8, starting transfers between devices, from_spots(): pieces.append(lax.ppermute(piece, PLANE, pairs))  48.2 us
    all_to_all x2, waiting for transfers between devices, columns_from_spots(): lax.all_to_all(grad.reshape(plane, depth, grad.shape[1]), PLANE, split_ax...  46.6 us
    dot_general x12, matrix products, project(): lax.dot_general(left, right, (contract, ((), ())), preferred_element_type...  43.1 us
    all_to_all x2, waiting for transfers between devices, columns_to_spots(): lax.all_to_all(split, PLANE, split_axis=0, concat_axis=0, tiled=True)  30.7 us
    unnamed x98, local copies, waits for them, and re-layouts  30.3 us
  transfers between devices with their start and end apart: 36, of which 19 were waited for; matrix products, arithmetic and copies ran while one was open for 29% of the time, Pallas kernels for 0%

profile of v1, /device:TPU:13, one launch (start us, length us, event | category | flops | bytes accessed | tf_op | source)
XLA Modules:
  0.0 662.4 jit_solution(14465733667736237669)
XLA Ops:
  9.3 5.9 all-to-all-start
  28.6 6.8 %all-to-all-start.2 = ((bf16[8,128,1536]{1,2,0:T(8,128)(2,1)}), bf16[8,128,1536]{1,2,0:T(8,128)(2,1)}, u32[]{:S(2)}, u32[]{:S(2)}) async-start(bf16[8,128,1536]{1,2,0:T(8,128)(2,1)} %bitcast.223), calls=%async_computation.2 | async-start | bytes 6291456 | tf_op jit(solution)/shard_map/all_to_all | solution.py:95
  38.9 30.7 %all-to-all-done.2 = bf16[8,128,1536]{1,2,0:T(8,128)(2,1)} async-done(((bf16[8,128,1536]{1,2,0:T(8,128)(2,1)}), bf16[8,128,1536]{1,2,0:T(8,128)(2,1)}, u32[]{:S(2)}, u32[]{:S(2)}) %all-to-all-start.2) | async-done | bytes 3145760 | tf_op jit(solution)/shard_map/all_to_all | solution.py:95
  79.1 6.4 all-to-all-start.3
  86.6 36.0 %all-to-all-done.3 = bf16[16,32,1536]{2,1,0:T(8,128)(2,1)S(1)} async-done(((bf16[16,32,1536]{2,1,0:T(8,128)(2,1)}), bf16[16,32,1536]{2,1,0:T(8,128)(2,1)S(1)}, u32[]{:S(2)}, u32[]{:S(2)}) %all-to-all-start.3) | async-done | bytes 1572896 | tf_op jit(solution)/shard_map/all_to_all | solution.py:119
  144.8 12.7 %reshape.429 = bf16[4,128,2,2,1408]{4,3,2,1,0:T(2,128)(2,1)} reshape(bf16[4,128,5632]{2,1,0:T(8,128)(2,1)} %param.15) | data formatting | bytes 11534336 | tf_op jit(solution)/shard_map/reshape | solution.py:93
  157.5 9.4 %copy.134 = bf16[4,2,128,2,1408]{4,3,2,1,0:T(2,128)(2,1)} copy(bf16[4,2,128,2,1408]{4,1,3,2,0:T(2,128)(2,1)} %bitcast.221) | data formatting | bytes 11534336 | tf_op jit(solution)/shard_map/transpose | solution.py:94
  166.9 13.4 %reshape.430 = bf16[8,128,2816]{2,1,0:T(8,128)(2,1)} reshape(bf16[4,2,128,2,1408]{4,3,2,1,0:T(2,128)(2,1)} %copy.134) | data formatting | bytes 11534336 | tf_op jit(solution)/shard_map/reshape | solution.py:94
  180.3 7.1 %all-to-all-start.5 = ((bf16[8,128,2816]{2,1,0:T(8,128)(2,1)}), bf16[8,128,2816]{2,1,0:T(8,128)(2,1)}, u32[]{:S(2)}, u32[]{:S(2)}) async-start(bf16[8,128,2816]{2,1,0:T(8,128)(2,1)} %reshape.430), calls=%async_computation.5 | async-start | bytes 11534336 | tf_op jit(solution)/shard_map/all_to_all | solution.py:95
  197.1 60.9 %collective-permute-done.1 = bf16[128,1024]{1,0:T(8,128)(2,1)S(1)} collective-permute-done((bf16[128,1024]{1,0:T(8,128)(2,1)}, bf16[128,1024]{1,0:T(8,128)(2,1)S(1)}, u32[]{:S(2)}, u32[]{:S(2)}) %collective-permute-start.1) | collective-permute-done | bytes 262176 | tf_op jit(solution)/shard_map/ppermute | solution.py:69
  274.6 8.5 %collective-permute-done.6 = bf16[352,1024]{1,0:T(8,128)(2,1)S(1)} collective-permute-done((bf16[352,1024]{1,0:T(8,128)(2,1)S(1)}, bf16[352,1024]{1,0:T(8,128)(2,1)S(1)}, u32[]{:S(2)}, u32[]{:S(2)}) %collective-permute-start.6) | collective-permute-done | bytes 720928 | tf_op jit(solution)/shard_map/ppermute | solution.py:69
  283.6 12.5 %collective-permute-start.11 = (bf16[256,1024]{1,0:T(8,128)(2,1)S(1)}, bf16[256,1024]{1,0:T(8,128)(2,1)S(1)}, u32[]{:S(2)}, u32[]{:S(2)}) collective-permute-start(bf16[256,1024]{1,0:T(8,128)(2,1)S(1)} %bitcast.226), channel_id=1, source_target_pairs={{0,4},{4,0},{1,5},{5,1},{2,6},{6,2},{3,7},{7,3},{8,12},{12,8},{9,1... | collective-permute-start | bytes 1572872 | tf_op jit(solution)/shard_map/ppermute | solution.py:42
  305.2 6.3 fusion.37
  314.8 6.8 %fusion = f32[2,256,1024]{2,1,0:T(8,128)S(1)} fusion(bf16[1024,2816,1]{1,0,2:T(8,128)(2,1)} %bitcast.58, bf16[2,256,1408]{2,1,0:T(8,128)(2,1)S(1)} %bitcast.275, bf16[2,256,1408]{2,1,0:T(8,128)(2,1)S(1)} %bitcast.274), kind=kOutput, calls=%fused_computation.10 | convolution fusion | flops 2958557184 | bytes 10747904 | tf_op jit(solution)/shard_map/dot_general | solution.py:15
  331.5 5.5 all-to-all-start.8
  345.0 5.4 all-to-all-done.8
  351.2 5.1 all-to-all-start.6
  370.7 5.3 convert_element_type.183
  376.1 6.4 all-to-all-start.9
  385.0 5.1 convolution_convert_fusion
  390.0 29.6 %all-to-all-done.9 = bf16[16,32,1536]{2,1,0:T(8,128)(2,1)} async-done(((bf16[16,32,1536]{2,1,0:T(8,128)(2,1)}), bf16[16,32,1536]{2,1,0:T(8,128)(2,1)}, u32[]{:S(2)}, u32[]{:S(2)}) %all-to-all-start.9) | async-done | bytes 1572896 | tf_op jit(solution)/shard_map/all_to_all | solution.py:119
  419.7 6.4 all-to-all-start.12
  441.7 46.6 %all-to-all-done.12 = bf16[8,128,2816]{2,1,0:T(8,128)(2,1)} async-done(((bf16[8,128,2816]{2,1,0:T(8,128)(2,1)}), bf16[8,128,2816]{2,1,0:T(8,128)(2,1)}, u32[]{:S(2)}, u32[]{:S(2)}) %all-to-all-start.12) | async-done | bytes 5767200 | tf_op jit(solution)/shard_map/all_to_all | solution.py:102
  488.3 7.1 %all-to-all-start.13 = ((f32[8,2,128]{2,1,0:T(2,128)}), f32[8,2,128]{2,1,0:T(2,128)S(1)}, u32[]{:S(2)}, u32[]{:S(2)}) async-start(f32[8,2,128]{2,1,0:T(2,128)} %maximum_bitcast_fusion), calls=%async_computation.13 | async-start | bytes 16384 | tf_op jit(solution)/shard_map/all_to_all | solution.py:256
  511.2 6.8 %collective-permute-start.19 = (bf16[352,1024]{1,0:T(8,128)(2,1)}, bf16[352,1024]{1,0:T(8,128)(2,1)}, u32[]{:S(2)}, u32[]{:S(2)}) collective-permute-start(bf16[352,1024]{1,0:T(8,128)(2,1)} %get-tuple-element.61), channel_id=1, source_target_pairs={{8,0},{16,4},{24,8},{0,12},{12,16},{20,20},{28,24},{4,28},{9,1},{1... | collective-permute-start | bytes 2162696 | tf_op jit(solution)/shard_map/ppermute | solution.py:82
  535.2 10.8 %collective-permute-done.20 = bf16[352,1024]{1,0:T(8,128)(2,1)} collective-permute-done((bf16[352,1024]{1,0:T(8,128)(2,1)}, bf16[352,1024]{1,0:T(8,128)(2,1)}, u32[]{:S(2)}, u32[]{:S(2)}) %collective-permute-start.20) | collective-permute-done | bytes 720928 | tf_op jit(solution)/shard_map/ppermute | solution.py:82
  550.9 15.8 %collective-permute-start.17 = (bf16[128,1024]{1,0:T(8,128)(2,1)}, bf16[128,1024]{1,0:T(8,128)(2,1)}, u32[]{:S(2)}, u32[]{:S(2)}) collective-permute-start(bf16[128,1024]{1,0:T(8,128)(2,1)} %get-tuple-element.71), channel_id=1, source_target_pairs={{24,0},{0,4},{8,8},{16,12},{28,16},{4,20},{12,24},{20,28},{25,1},{... | collective-permute-start | bytes 786440 | tf_op jit(solution)/shard_map/ppermute | solution.py:82
  566.7 14.6 %collective-permute-start.16 = (bf16[128,1024]{1,0:T(8,128)(2,1)S(1)}, bf16[128,1024]{1,0:T(8,128)(2,1)}, u32[]{:S(2)}, u32[]{:S(2)}) collective-permute-start(bf16[128,1024]{1,0:T(8,128)(2,1)S(1)} %get-tuple-element.72), channel_id=1, source_target_pairs={{16,0},{24,4},{0,8},{8,12},{20,16},{28,20},{4,24},{12,28},{17,1},{... | collective-permute-start | bytes 786440 | tf_op jit(solution)/shard_map/ppermute | solution.py:82
  598.7 13.0 %reshape.448 = f32[4,2,128,2,1408]{4,3,2,1,0:T(2,128)} reshape(bf16[8,128,2816]{2,1,0:T(8,128)(2,1)} %all-to-all-done.12) | data formatting | bytes 17301504 | tf_op jit(solution)/shard_map/convert_element_type | solution.py:106
  611.7 20.4 %copy.183 = f32[4,2,128,2,1408]{4,1,3,2,0:T(2,128)} copy(f32[4,2,128,2,1408]{4,3,2,1,0:T(2,128)} %reshape.448) | data formatting | bytes 23068672 | tf_op jit(solution)/shard_map/convert_element_type | solution.py:106
  632.1 15.3 %reshape.446 = f32[4,128,5632]{2,1,0:T(8,128)} reshape(f32[4,128,2,2,1408]{4,3,2,1,0:T(2,128)} %bitcast.215) | data formatting | bytes 23068672 | tf_op jit(solution)/shard_map/convert_element_type | solution.py:106
  655.4 6.6 copy.149
  (237 shorter events, 211.4 us)
Async XLA Ops:
  9.3 19.4 %all-to-all-start = ((bf16[16,16,1024]{2,0,1:T(8,128)(2,1)}), bf16[16,16,1024]{2,0,1:T(8,128)(2,1)S(1)}, u32[]{:S(2)}, u32[]{:S(2)}) async-start(bf16[16,16,1024]{2,0,1:T(8,128)(2,1)} %copy.124), calls=%async_computation | async-start | bytes 1048576 | tf_op jit(solution)/shard_map/all_to_all | solution.py:110
  28.6 41.0 %all-to-all-start.2 = ((bf16[8,128,1536]{1,2,0:T(8,128)(2,1)}), bf16[8,128,1536]{1,2,0:T(8,128)(2,1)}, u32[]{:S(2)}, u32[]{:S(2)}) async-start(bf16[8,128,1536]{1,2,0:T(8,128)(2,1)} %bitcast.223), calls=%async_computation.2 | async-start | bytes 6291456 | tf_op jit(solution)/shard_map/all_to_all | solution.py:95
  79.1 43.5 %all-to-all-start.3 = ((bf16[16,32,1536]{2,1,0:T(8,128)(2,1)}), bf16[16,32,1536]{2,1,0:T(8,128)(2,1)S(1)}, u32[]{:S(2)}, u32[]{:S(2)}) async-start(bf16[16,32,1536]{2,1,0:T(8,128)(2,1)} %bitcast.249), calls=%async_computation.3 | async-start | bytes 3145728 | tf_op jit(solution)/shard_map/all_to_all | solution.py:119
  122.6 17.2 %all-to-all-start.7 = ((bf16[16,16,1024]{2,0,1:T(8,128)(2,1)}), bf16[16,16,1024]{2,0,1:T(8,128)(2,1)S(1)}, u32[]{:S(2)}, u32[]{:S(2)}) async-start(bf16[16,16,1024]{2,0,1:T(8,128)(2,1)} %copy_select_fusion), calls=%async_computation.7 | async-start | bytes 1048576 | tf_op jit(solution)/shard_map/all_to_all | solution.py:110
  139.8 40.6 %all-to-all-start.4 = ((bf16[16,32,512]{2,1,0:T(8,128)(2,1)}), bf16[16,32,512]{2,1,0:T(8,128)(2,1)S(1)}, u32[]{:S(2)}, u32[]{:S(2)}) async-start(bf16[16,32,512]{2,1,0:T(8,128)(2,1)} %convert_element_type.170), calls=%async_computation.4 | async-start | bytes 1048576 | tf_op jit(solution)/shard_map/all_to_all | solution.py:119
  180.3 124.9 %all-to-all-start.5 = ((bf16[8,128,2816]{2,1,0:T(8,128)(2,1)}), bf16[8,128,2816]{2,1,0:T(8,128)(2,1)}, u32[]{:S(2)}, u32[]{:S(2)}) async-start(bf16[8,128,2816]{2,1,0:T(8,128)(2,1)} %reshape.430), calls=%async_computation.5 | async-start | bytes 11534336 | tf_op jit(solution)/shard_map/all_to_all | solution.py:95
  188.3 69.7 %collective-permute-start.1 = (bf16[128,1024]{1,0:T(8,128)(2,1)}, bf16[128,1024]{1,0:T(8,128)(2,1)S(1)}, u32[]{:S(2)}, u32[]{:S(2)}) collective-permute-start(bf16[128,1024]{1,0:T(8,128)(2,1)} %get-tuple-element.76), channel_id=1, source_target_pairs={{0,0},{4,8},{8,16},{12,24},{16,4},{20,12},{24,20},{28,28},{1,1},{5... | collective-permute-start | bytes 786440 | tf_op jit(solution)/shard_map/ppermute | solution.py:69
  191.4 66.8 %collective-permute-start.2 = (bf16[128,1024]{1,0:T(8,128)(2,1)}, bf16[128,1024]{1,0:T(8,128)(2,1)S(1)}, u32[]{:S(2)}, u32[]{:S(2)}) collective-permute-start(bf16[128,1024]{1,0:T(8,128)(2,1)} %get-tuple-element.75), channel_id=1, source_target_pairs={{0,8},{4,16},{8,24},{12,0},{16,12},{20,20},{24,28},{28,4},{1,9},{5... | collective-permute-start | bytes 786440 | tf_op jit(solution)/shard_map/ppermute | solution.py:69
  193.0 67.8 %collective-permute-start.3 = (bf16[128,1024]{1,0:T(8,128)(2,1)S(1)}, bf16[128,1024]{1,0:T(8,128)(2,1)S(1)}, u32[]{:S(2)}, u32[]{:S(2)}) collective-permute-start(bf16[128,1024]{1,0:T(8,128)(2,1)S(1)} %get-tuple-element.77), channel_id=1, source_target_pairs={{0,16},{4,24},{8,0},{12,8},{16,20},{20,28},{24,4},{28,12},{1,17},{... | collective-permute-start | bytes 786440 | tf_op jit(solution)/shard_map/ppermute | solution.py:69
  195.1 67.6 %collective-permute-start.4 = (bf16[128,1024]{1,0:T(8,128)(2,1)S(1)}, bf16[128,1024]{1,0:T(8,128)(2,1)S(1)}, u32[]{:S(2)}, u32[]{:S(2)}) collective-permute-start(bf16[128,1024]{1,0:T(8,128)(2,1)S(1)} %get-tuple-element.74), channel_id=1, source_target_pairs={{0,24},{4,0},{8,8},{12,16},{16,28},{20,4},{24,12},{28,20},{1,25},{... | collective-permute-start | bytes 786440 | tf_op jit(solution)/shard_map/ppermute | solution.py:69
  264.4 39.1 %collective-permute-start.5 = (f32[2,256,1024]{2,1,0:T(8,128)S(1)}, f32[2,256,1024]{2,1,0:T(8,128)S(1)}, u32[]{:S(2)}, u32[]{:S(2)}) collective-permute-start(f32[2,256,1024]{2,1,0:T(8,128)S(1)} %fusion.36), channel_id=1, source_target_pairs={{0,4},{4,0},{1,5},{5,1},{2,6},{6,2},{3,7},{7,3},{8,12},{12,8},{9,1... | collective-permute-start | bytes 6291464 | tf_op jit(solution)/shard_map/ppermute | solution.py:42
  265.2 17.9 %collective-permute-start.6 = (bf16[352,1024]{1,0:T(8,128)(2,1)S(1)}, bf16[352,1024]{1,0:T(8,128)(2,1)S(1)}, u32[]{:S(2)}, u32[]{:S(2)}) collective-permute-start(bf16[352,1024]{1,0:T(8,128)(2,1)S(1)} %get-tuple-element.64), channel_id=1, source_target_pairs={{0,0},{4,8},{8,16},{12,24},{16,4},{20,12},{24,20},{28,28},{1,1},{5... | collective-permute-start | bytes 2162696 | tf_op jit(solution)/shard_map/ppermute | solution.py:69
  268.4 27.7 %collective-permute-start.7 = (bf16[352,1024]{1,0:T(8,128)(2,1)S(1)}, bf16[352,1024]{1,0:T(8,128)(2,1)S(1)}, u32[]{:S(2)}, u32[]{:S(2)}) collective-permute-start(bf16[352,1024]{1,0:T(8,128)(2,1)S(1)} %get-tuple-element.63), channel_id=1, source_target_pairs={{0,8},{4,16},{8,24},{12,0},{16,12},{20,20},{24,28},{28,4},{1,9},{5... | collective-permute-start | bytes 2162696 | tf_op jit(solution)/shard_map/ppermute | solution.py:69
  269.1 27.6 %collective-permute-start.8 = (bf16[352,1024]{1,0:T(8,128)(2,1)S(1)}, bf16[352,1024]{1,0:T(8,128)(2,1)S(1)}, u32[]{:S(2)}, u32[]{:S(2)}) collective-permute-start(bf16[352,1024]{1,0:T(8,128)(2,1)S(1)} %get-tuple-element.65), channel_id=1, source_target_pairs={{0,16},{4,24},{8,0},{12,8},{16,20},{20,28},{24,4},{28,12},{1,17},{... | collective-permute-start | bytes 2162696 | tf_op jit(solution)/shard_map/ppermute | solution.py:69
  271.9 29.5 %collective-permute-start.9 = (bf16[352,1024]{1,0:T(8,128)(2,1)S(1)}, bf16[352,1024]{1,0:T(8,128)(2,1)S(1)}, u32[]{:S(2)}, u32[]{:S(2)}) collective-permute-start(bf16[352,1024]{1,0:T(8,128)(2,1)S(1)} %get-tuple-element.62), channel_id=1, source_target_pairs={{0,24},{4,0},{8,8},{12,16},{16,28},{20,4},{24,12},{28,20},{1,25},{... | collective-permute-start | bytes 2162696 | tf_op jit(solution)/shard_map/ppermute | solution.py:69
  283.6 17.8 %collective-permute-start.11 = (bf16[256,1024]{1,0:T(8,128)(2,1)S(1)}, bf16[256,1024]{1,0:T(8,128)(2,1)S(1)}, u32[]{:S(2)}, u32[]{:S(2)}) collective-permute-start(bf16[256,1024]{1,0:T(8,128)(2,1)S(1)} %bitcast.226), channel_id=1, source_target_pairs={{0,4},{4,0},{1,5},{5,1},{2,6},{6,2},{3,7},{7,3},{8,12},{12,8},{9,1... | collective-permute-start | bytes 1572872 | tf_op jit(solution)/shard_map/ppermute | solution.py:42
  326.6 10.4 %collective-permute-start.10 = (f32[256,1024]{1,0:T(8,128)}, f32[256,1024]{1,0:T(8,128)}, u32[]{:S(2)}, u32[]{:S(2)}) collective-permute-start(f32[256,1024]{1,0:T(8,128)} %slice.76), channel_id=1, source_target_pairs={{0,4},{4,0},{1,5},{5,1},{2,6},{6,2},{3,7},{7,3},{8,12},{12,8},{9,1... | collective-permute-start | bytes 3145736 | tf_op jit(solution)/shard_map/ppermute | solution.py:42
  331.5 18.9 %all-to-all-start.8 = ((bf16[16,32,512]{2,1,0:T(8,128)(2,1)}), bf16[16,32,512]{2,1,0:T(8,128)(2,1)S(1)}, u32[]{:S(2)}, u32[]{:S(2)}) async-start(bf16[16,32,512]{2,1,0:T(8,128)(2,1)} %bitcast.256), calls=%async_computation.8 | async-start | bytes 1048576 | tf_op jit(solution)/shard_map/all_to_all | solution.py:119
  351.2 24.8 %all-to-all-start.6 = ((bf16[16,2,8192]{2,1,0:T(2,128)(2,1)}), bf16[16,2,8192]{2,1,0:T(2,128)(2,1)S(1)}, u32[]{:S(2)}, u32[]{:S(2)}) async-start(bf16[16,2,8192]{2,1,0:T(2,128)(2,1)} %reshape.451), calls=%async_computation.6 | async-start | bytes 1048576 | tf_op jit(solution)/shard_map/all_to_all | solution.py:115
  376.1 43.6 %all-to-all-start.9 = ((bf16[16,32,1536]{2,1,0:T(8,128)(2,1)}), bf16[16,32,1536]{2,1,0:T(8,128)(2,1)}, u32[]{:S(2)}, u32[]{:S(2)}) async-start(bf16[16,32,1536]{2,1,0:T(8,128)(2,1)} %convert_element_type.183), calls=%async_computation.9 | async-start | bytes 3145728 | tf_op jit(solution)/shard_map/all_to_all | solution.py:119
  419.7 68.6 %all-to-all-start.12 = ((bf16[8,128,2816]{2,1,0:T(8,128)(2,1)}), bf16[8,128,2816]{2,1,0:T(8,128)(2,1)}, u32[]{:S(2)}, u32[]{:S(2)}) async-start(bf16[8,128,2816]{2,1,0:T(8,128)(2,1)} %bitcast.225), calls=%async_computation.12 | async-start | bytes 11534336 | tf_op jit(solution)/shard_map/all_to_all | solution.py:102
  488.3 10.3 %all-to-all-start.13 = ((f32[8,2,128]{2,1,0:T(2,128)}), f32[8,2,128]{2,1,0:T(2,128)S(1)}, u32[]{:S(2)}, u32[]{:S(2)}) async-start(f32[8,2,128]{2,1,0:T(2,128)} %maximum_bitcast_fusion), calls=%async_computation.13 | async-start | bytes 16384 | tf_op jit(solution)/shard_map/all_to_all | solution.py:256
  498.6 31.9 %all-to-all-start.10 = ((bf16[16,2,8192]{2,1,0:T(2,128)(2,1)}), bf16[16,2,8192]{2,1,0:T(2,128)(2,1)S(1)}, u32[]{:S(2)}, u32[]{:S(2)}) async-start(bf16[16,2,8192]{2,1,0:T(2,128)(2,1)} %reshape.453), calls=%async_computation.10 | async-start | bytes 1048576 | tf_op jit(solution)/shard_map/all_to_all | solution.py:115
  507.7 27.6 %collective-permute-start.21 = (bf16[352,1024]{1,0:T(8,128)(2,1)}, bf16[352,1024]{1,0:T(8,128)(2,1)}, u32[]{:S(2)}, u32[]{:S(2)}) collective-permute-start(bf16[352,1024]{1,0:T(8,128)(2,1)} %get-tuple-element.59), channel_id=1, source_target_pairs={{24,0},{0,4},{8,8},{16,12},{28,16},{4,20},{12,24},{20,28},{25,1},{... | collective-permute-start | bytes 2162696 | tf_op jit(solution)/shard_map/ppermute | solution.py:82
  510.7 35.2 %collective-permute-start.20 = (bf16[352,1024]{1,0:T(8,128)(2,1)}, bf16[352,1024]{1,0:T(8,128)(2,1)}, u32[]{:S(2)}, u32[]{:S(2)}) collective-permute-start(bf16[352,1024]{1,0:T(8,128)(2,1)} %get-tuple-element.60), channel_id=1, source_target_pairs={{16,0},{24,4},{0,8},{8,12},{20,16},{28,20},{4,24},{12,28},{17,1},{... | collective-permute-start | bytes 2162696 | tf_op jit(solution)/shard_map/ppermute | solution.py:82
  511.2 34.8 %collective-permute-start.19 = (bf16[352,1024]{1,0:T(8,128)(2,1)}, bf16[352,1024]{1,0:T(8,128)(2,1)}, u32[]{:S(2)}, u32[]{:S(2)}) collective-permute-start(bf16[352,1024]{1,0:T(8,128)(2,1)} %get-tuple-element.61), channel_id=1, source_target_pairs={{8,0},{16,4},{24,8},{0,12},{12,16},{20,20},{28,24},{4,28},{9,1},{1... | collective-permute-start | bytes 2162696 | tf_op jit(solution)/shard_map/ppermute | solution.py:82
  518.0 28.0 %collective-permute-start.18 = (bf16[352,1024]{1,0:T(8,128)(2,1)S(1)}, bf16[352,1024]{1,0:T(8,128)(2,1)}, u32[]{:S(2)}, u32[]{:S(2)}) collective-permute-start(bf16[352,1024]{1,0:T(8,128)(2,1)S(1)} %get-tuple-element.58), channel_id=1, source_target_pairs={{0,0},{8,4},{16,8},{24,12},{4,16},{12,20},{20,24},{28,28},{1,1},{9... | collective-permute-start | bytes 2162696 | tf_op jit(solution)/shard_map/ppermute | solution.py:82
  530.4 119.3 %all-to-all-start.11 = ((bf16[8,128,1536]{1,2,0:T(8,128)(2,1)}), bf16[8,128,1536]{1,2,0:T(8,128)(2,1)}, u32[]{:S(2)}, u32[]{:S(2)}) async-start(bf16[8,128,1536]{1,2,0:T(8,128)(2,1)} %copy.144), calls=%async_computation.11 | async-start | bytes 6291456 | tf_op jit(solution)/shard_map/all_to_all | solution.py:102
  550.9 40.0 %collective-permute-start.17 = (bf16[128,1024]{1,0:T(8,128)(2,1)}, bf16[128,1024]{1,0:T(8,128)(2,1)}, u32[]{:S(2)}, u32[]{:S(2)}) collective-permute-start(bf16[128,1024]{1,0:T(8,128)(2,1)} %get-tuple-element.71), channel_id=1, source_target_pairs={{24,0},{0,4},{8,8},{16,12},{28,16},{4,20},{12,24},{20,28},{25,1},{... | collective-permute-start | bytes 786440 | tf_op jit(solution)/shard_map/ppermute | solution.py:82
  566.7 24.2 %collective-permute-start.16 = (bf16[128,1024]{1,0:T(8,128)(2,1)S(1)}, bf16[128,1024]{1,0:T(8,128)(2,1)}, u32[]{:S(2)}, u32[]{:S(2)}) collective-permute-start(bf16[128,1024]{1,0:T(8,128)(2,1)S(1)} %get-tuple-element.72), channel_id=1, source_target_pairs={{16,0},{24,4},{0,8},{8,12},{20,16},{28,20},{4,24},{12,28},{17,1},{... | collective-permute-start | bytes 786440 | tf_op jit(solution)/shard_map/ppermute | solution.py:82
  581.3 9.6 %collective-permute-start.15 = (bf16[128,1024]{1,0:T(8,128)(2,1)S(1)}, bf16[128,1024]{1,0:T(8,128)(2,1)}, u32[]{:S(2)}, u32[]{:S(2)}) collective-permute-start(bf16[128,1024]{1,0:T(8,128)(2,1)S(1)} %get-tuple-element.73), channel_id=1, source_target_pairs={{8,0},{16,4},{24,8},{0,12},{12,16},{20,20},{28,24},{4,28},{9,1},{1... | collective-permute-start | bytes 786440 | tf_op jit(solution)/shard_map/ppermute | solution.py:82
  582.6 13.2 %collective-permute-start.14 = (bf16[128,1024]{1,0:T(8,128)(2,1)S(1)}, bf16[128,1024]{1,0:T(8,128)(2,1)}, u32[]{:S(2)}, u32[]{:S(2)}) collective-permute-start(bf16[128,1024]{1,0:T(8,128)(2,1)S(1)} %get-tuple-element.70), channel_id=1, source_target_pairs={{0,0},{8,4},{16,8},{24,12},{4,16},{12,20},{20,24},{28,28},{1,1},{9... | collective-permute-start | bytes 786440 | tf_op jit(solution)/shard_map/ppermute | solution.py:82
  (46 other events, 337.0 us)

commit v2 on v0

--- a/solution.py
+++ b/solution.py
@@ -1,13 +1,15 @@
+import functools
+
 import jax
 import jax.numpy as jnp
 from jax import lax
-from jax.sharding import PartitionSpec as P
+from jax.experimental import pallas as pl
+from jax.experimental.pallas import tpu as pltpu
+from jax.sharding import Mesh, PartitionSpec as P
 
 HEADS = 16
 HEAD = 64
-FF = 2816
-
-
+LANES = 128
 EPSILON = 1e-06
 NEGATIVE = -1e30
 
@@ -44,7 +46,7 @@
     return jnp.where(allowed, raw_scores, NEGATIVE)
 
 
-def on_device(
+def gathered_plan(
     frames_in,
     frame_valid,
     last_position,
@@ -91,8 +93,9 @@
     scaled_two, normed_two, inverse_two = rms_forward(middle, gain_two)
     normed_two_low = scaled_two.astype(jnp.bfloat16)
     gate_up = project("rpd,pde->rpe", normed_two_low, full_ffn)
-    gate = gate_up[..., :FF]
-    upward = gate_up[..., FF:]
+    width = gate_up.shape[-1] // 2
+    gate = gate_up[..., :width]
+    upward = gate_up[..., width:]
     gate_sig = jax.nn.sigmoid(gate)
     hidden = (gate * gate_sig * upward).astype(jnp.bfloat16)
     result = middle + project("rpf,pfd->rpd", hidden, full_down)
@@ -168,32 +171,580 @@
     return (output, grad_frames, sum_qkv, sum_out, sum_ffn, sum_down, sum_gain_a, sum_gain_f)
 
 
+ROWS = ("pos", "spot")
+PLANE = ("spot", "half")
+
+
+def plain(left, right):
+    return lax.dot_general(left, right, (((1,), (0,)), ((), ())), preferred_element_type=jnp.float32)
+
+
+def by_columns(left, right):
+    return lax.dot_general(left, right, (((1,), (1,)), ((), ())), preferred_element_type=jnp.float32)
+
+
+def over_rows(left, right):
+    return lax.dot_general(left, right, (((0,), (0,)), ((), ())), preferred_element_type=jnp.float32)
+
+
+def tie(*values):
+    return lax.optimization_barrier(values)
+
+
+def pick(stack, index):
+    return lax.dynamic_index_in_dim(stack, index, 0, keepdims=False)
+
+
+def hop(value, k, spots):
+    return value if k == 0 else lax.ppermute(value, "spot", [(i, i ^ k) for i in range(spots)])
+
+
+def trade(value):
+    return lax.ppermute(value, "half", [(0, 1), (1, 0)])
+
+
+def rows_to_spots(values):
+    moved = lax.all_to_all(values, ROWS, split_axis=1, concat_axis=0, tiled=True)
+    return moved.reshape(moved.shape[0], moved.shape[2])
+
+
+def rows_from_spots(values):
+    return lax.all_to_all(values[:, None], ROWS, split_axis=0, concat_axis=1, tiled=True)
+
+
+def swap(values, blocks):
+    return lax.all_to_all(
+        values.reshape(blocks, -1, values.shape[-1]), ROWS, split_axis=0, concat_axis=0, tiled=True
+    )
+
+
+def head_runs(width, groups, spots):
+    size = width // groups // spots // 2
+    return [((g * spots + a) * 2 * size, ((g * spots + a) * 2 + 1) * size) for g in range(groups) for a in range(spots)], size
+
+
+def unit_runs(width, groups):
+    size = width // groups // 2
+    return [(g * 2 * size, (g * 2 + 1) * size) for g in range(groups)], size
+
+
+def call(kernel, name, grid, inputs, outputs, scalars, scratch=()):
+    moved = sum(a.size * a.dtype.itemsize for a, _, _ in inputs)
+    return pl.pallas_call(
+        kernel,
+        grid_spec=pltpu.PrefetchScalarGridSpec(
+            num_scalar_prefetch=1,
+            grid=grid,
+            in_specs=[pl.BlockSpec(block, where) for _, block, where in inputs],
+            out_specs=[pl.BlockSpec(block, where) for _, _, block, where in outputs],
+            scratch_shapes=list(scratch),
+        ),
+        out_shape=[jax.ShapeDtypeStruct(shape, dtype) for shape, dtype, _, _ in outputs],
+        compiler_params=pltpu.CompilerParams(vmem_limit_bytes=48 << 20),
+        cost_estimate=pl.CostEstimate(flops=0, transcendentals=0, bytes_accessed=moved // 8),
+        name=name,
+    )(scalars, *[a for a, _, _ in inputs])
+
+
+def aligned(start, size):
+    return pl.ds(pl.multiple_of(start, LANES), size)
+
+
+def split_kernel(runs, count, per, rests, scalars, *refs):
+    starts, size = runs
+    pieces, outs = refs[: count * per], refs[count * per :]
+    half = scalars[0]
+    for k in range(count):
+        at = scalars[1 + k]
+        for i, (even, odd) in enumerate(starts):
+            piece, even, odd = (
+                (pieces[k * per + i], 0, size) if per > 1 else (pieces[k], even, odd)
+            )
+            for out, first, second in ((outs[0], even, odd), (outs[1], odd, even)):
+                columns = aligned(first + half * (second - first), size)
+                out[pl.ds(at, 1), :, i * size : (i + 1) * size] = piece[:, columns][None]
+        for out, (start, width) in zip(outs[2:], rests):
+            out[pl.ds(at, 1)] = pieces[k][:, start : start + width][None]
+
+
+def split_columns(pieces, runs, scalars, rests=()):
+    starts, size = runs
+    per = len(pieces[0])
+    rows, width = pieces[0][0].shape
+    count, step = len(pieces), rows // 4
+    widths = [len(starts) * size] * 2 + [n for _, n in rests]
+    outs = call(
+        functools.partial(split_kernel, runs, count, per, rests),
+        "split_columns",
+        (4,),
+        [(a, (step, width), lambda r, s: (r, 0)) for piece in pieces for a in piece],
+        [
+            ((count, rows, n), pieces[0][0].dtype, (count, step, n), lambda r, s: (0, r, 0))
+            for n in widths
+        ],
+        scalars,
+    )
+    return [out.reshape(count * rows, -1) for out in outs]
+
+
+def place_kernel(runs, parts, skip, scalars, *refs):
+    out = refs[-1]
+    half = scalars[0]
+    for k in range((len(refs) - 1) // parts):
+
+        @pl.when(pl.program_id(0) == k)
+        def _():
+            for p in range(parts):
+                ref = refs[k * parts + p]
+                if runs is None:
+                    out[0] = ref[:, skip:].astype(jnp.float32)
+                    continue
+                starts, size = runs
+                for i, pair in enumerate(starts):
+                    first, second = pair[::-1] if p else pair
+                    columns = aligned(first + half * (second - first), size)
+                    out[0, :, columns] = ref[:, i * size : (i + 1) * size].astype(jnp.float32)
+
+
+def place(pieces, scalars, rows, width, runs=None, skip=0):
+    count, parts = len(pieces), len(pieces[0])
+    cuts = 2 if rows * width > (1 << 19) else 1
+    step = rows // cuts
+
+    def spec(k, first):
+        base = first // step
+        return lambda j, r, s: (base + jnp.where(j == k, r, jnp.where(j < k, 0, cuts - 1)), 0)
+
+    return call(
+        functools.partial(place_kernel, runs, parts, skip),
+        "place",
+        (count, cuts),
+        [
+            (a, (step, a.shape[1]), spec(k, first))
+            for k, piece in enumerate(pieces)
+            for a, first in piece
+        ],
+        [
+            (
+                (count, rows, width),
+                jnp.float32,
+                (1, step, width),
+                lambda j, r, s: (s[1 + j], r, 0),
+            )
+        ],
+        scalars,
+    )[0]
+
+
+def halves_rows(step, own):
+    count = own.shape[0] // step
+    return (
+        lambda r, *s: (jnp.minimum(r, count - 1), 0),
+        lambda r, *s: (jnp.maximum(r - count, 0), 0),
+    )
+
+
+def unit_of(values):
+    inverse = lax.rsqrt(jnp.mean(values * values, axis=-1, keepdims=True) + EPSILON)
+    return values * inverse, inverse
+
+
+def spread(values, scratch, half, own, other):
+    scratch[...] = values.astype(scratch.dtype)
+    for a in range(own.shape[1] // LANES):
+        own[:, a * LANES : (a + 1) * LANES] = scratch[:, aligned((2 * a + half) * LANES, LANES)]
+        other[:, a * LANES : (a + 1) * LANES] = scratch[:, aligned((2 * a + 1 - half) * LANES, LANES)]
+
+
+def gather(own, other, scratch, half):
+    for a in range(own[0].shape[1] // LANES):
+        block = slice(a * LANES, (a + 1) * LANES)
+        scratch[:, aligned((2 * a + half) * LANES, LANES)] = own[0][:, block] + own[1][:, block]
+        scratch[:, aligned((2 * a + 1 - half) * LANES, LANES)] = other[0][:, block] + other[1][:, block]
+    return scratch[...]
+
+
+def either(own_ref, got_ref):
+    mine = pl.program_id(0) < pl.num_programs(0) // 2
+    return jnp.where(mine, own_ref[...].astype(jnp.float32), got_ref[...].astype(jnp.float32))
+
+
+def norm_kernel(scalars, own_rows, got_rows, gain, own, other, scratch):
+    unit, _ = unit_of(either(own_rows, got_rows))
+    spread(unit * gain[...], scratch, scalars[0], own, other)
+
+
+def middle_kernel(scalars, own_rows, got_rows, branch, got_branch, gain, middle, own, other, scratch):
+    values = either(own_rows, got_rows) + (branch[...] + got_branch[...])
+    middle[...] = values
+    unit, _ = unit_of(values)
+    spread(unit * gain[...], scratch, scalars[0], own, other)
+
+
+def pull(values, upstream, gain):
+    unit, inverse = unit_of(values)
+    scaled = upstream * gain
+    inner = jnp.mean(scaled * unit, axis=-1, keepdims=True)
+    return inverse * (scaled - unit * inner), jnp.sum(upstream * unit, axis=0, keepdims=True)
+
+
+def accumulate(term, value, when):
+    @pl.when(pl.program_id(0) == 0)
+    def _():
+        term[...] = jnp.zeros_like(term)
+
+    @pl.when(when)
+    def _():
+        term[...] += value
+
+
+def middle_back_kernel(
+    scalars, middle, own, other, got_own, got_other, own_up, got_up, gain, whole, low, term, scratch
+):
+    upstream = gather((own, got_other), (other, got_own), scratch, scalars[0])
+    grad, value = pull(middle[...], upstream, gain[...])
+    grad = grad + either(own_up, got_up)
+    whole[...] = grad
+    low[...] = grad.astype(low.dtype)
+    accumulate(term, value, pl.program_id(0) < pl.num_programs(0) // 2)
+
+
+def input_back_kernel(
+    scalars, rows, own, other, got_own, got_other, grad_middle, gain, out, term, scratch
+):
+    upstream = gather((own, got_other), (other, got_own), scratch, scalars[0])
+    grad, value = pull(rows[...].astype(jnp.float32), upstream, gain[...])
+    out[...] = (grad_middle[...] + grad).astype(out.dtype)
+    accumulate(term, value, True)
+
+
+def softmax_of(query, keys, allowed):
+    scores = jnp.where(allowed, by_columns(query, keys) * HEAD ** (-0.5), NEGATIVE)
+    exponent = jnp.exp(scores - jnp.max(scores, axis=-1, keepdims=True))
+    return exponent / jnp.sum(exponent, axis=-1, keepdims=True)
+
+
+def frame_mask(positions, frames):
+    count = positions * frames
+    row = lax.broadcasted_iota(jnp.int32, (count, count), 0)
+    column = lax.broadcasted_iota(jnp.int32, (count, count), 1)
+    return (row % frames == column % frames) & (row >= column)
+
+
+def attend_kernel(qkv_ref, mixed_ref):
+    positions, frames, width = qkv_ref.shape
+    count, third = positions * frames, width // 3
+    allowed = frame_mask(positions, frames)
+    lane = lax.broadcasted_iota(jnp.int32, (count, LANES), 1)
+    for first in range(0, third, LANES):
+        query, keys, values = (
+            qkv_ref[:, :, part * third + first : part * third + first + LANES].reshape(count, LANES)
+            for part in range(3)
+        )
+        mixed = jnp.zeros((count, LANES), jnp.float32)
+        for start in range(0, LANES, HEAD):
+            inside = (lane >= start) & (lane < start + HEAD)
+            probs = softmax_of(jnp.where(inside, query, jnp.zeros_like(query)), keys, allowed)
+            mixed = jnp.where(inside, plain(probs.astype(jnp.bfloat16), values), mixed)
+        mixed_ref[:, :, first : first + LANES] = mixed.astype(mixed_ref.dtype).reshape(
+            positions, frames, LANES
+        )
+
+
+def attend_back_kernel(qkv_ref, grad_ref, out_ref):
+    positions, frames, width = qkv_ref.shape
+    count, third = positions * frames, width // 3
+    scale = HEAD ** (-0.5)
+    allowed = frame_mask(positions, frames)
+    lane = lax.broadcasted_iota(jnp.int32, (count, LANES), 1)
+    for first in range(0, third, LANES):
+        query, keys, values = (
+            qkv_ref[:, :, part * third + first : part * third + first + LANES].reshape(count, LANES)
+            for part in range(3)
+        )
+        upstream = grad_ref[:, :, first : first + LANES].reshape(count, LANES)
+        grads = [jnp.zeros((count, LANES), jnp.float32)] * 3
+        for start in range(0, LANES, HEAD):
+            inside = (lane >= start) & (lane < start + HEAD)
+            probs = softmax_of(jnp.where(inside, query, jnp.zeros_like(query)), keys, allowed)
+            grad_probs = by_columns(jnp.where(inside, upstream, jnp.zeros_like(upstream)), values)
+            inner = jnp.sum(probs * grad_probs, axis=-1, keepdims=True)
+            grad_scores = (probs * (grad_probs - inner)).astype(jnp.bfloat16)
+            new = (
+                plain(grad_scores, keys) * scale,
+                over_rows(grad_scores, query) * scale,
+                over_rows(probs.astype(jnp.bfloat16), upstream),
+            )
+            grads = [jnp.where(inside, value, old) for value, old in zip(new, grads)]
+        for part, grad in enumerate(grads):
+            out_ref[:, :, part * third + first : part * third + first + LANES] = grad.astype(
+                out_ref.dtype
+            ).reshape(positions, frames, LANES)
+
+
+def over_frames(kernel, out_width, *arrays):
+    positions, frames, width = arrays[0].shape
+    step = min(frames, 256 // positions)
+    heads = width // 3 // HEAD
+    work = frames // step * heads * (step * positions) ** 2
+    return pl.pallas_call(
+        kernel,
+        grid=(frames // step,),
+        in_specs=[
+            pl.BlockSpec((positions, step, a.shape[2]), lambda i: (0, i, 0)) for a in arrays
+        ],
+        out_specs=pl.BlockSpec((positions, step, out_width), lambda i: (0, i, 0)),
+        out_shape=jax.ShapeDtypeStruct((positions, frames, out_width), arrays[0].dtype),
+        compiler_params=pltpu.CompilerParams(vmem_limit_bytes=48 << 20),
+        cost_estimate=pl.CostEstimate(
+            flops=4 * LANES * work,
+            transcendentals=work,
+            bytes_accessed=2 * positions * frames * (width + out_width),
+        ),
+        name=kernel.__name__,
+    )(*arrays)
+
+
+def spots_plan(
+    frames_in,
+    frame_valid,
+    last_position,
+    weight_qkv,
+    weight_out,
+    weight_ffn,
+    weight_down,
+    gain_attn,
+    gain_ffn,
+    grad_out,
+):
+    f32, bf16 = jnp.float32, jnp.bfloat16
+    frames, positions, depth = frames_in.shape
+    spots, slice_rows = weight_qkv.shape[:2]
+    plane, near = spots * 2, spots - 1
+    spot, half = lax.axis_index("spot"), lax.axis_index("half")
+    heads = head_runs(3 * depth, 3, spots)
+    units = unit_runs(weight_ffn.shape[2], 2)
+    hidden_units = weight_ffn.shape[2] // 2
+    down_index = lax.axis_index(PLANE) % spots
+    down_pairs = [
+        [(f, (f % spots ^ k) * 2 + f // spots) for f in range(plane)] for k in range(spots)
+    ]
+    early = spots // 2
+    by_spot = jnp.stack([half] + [spot ^ k for k in range(spots)]).astype(jnp.int32)
+    by_slice = jnp.stack([half] + [down_index ^ k for k in range(spots)]).astype(jnp.int32)
+    slot = lax.broadcasted_iota(jnp.int32, (frames, positions), 1)
+    live = ((frame_valid[:, None] > 0) & (slot <= last_position[:, None]))[:, :, None]
+
+    gains = jnp.stack([gain_attn, gain_ffn], axis=2)
+    gains = jnp.pad(gains, ((0, 0), (0, 0), (0, LANES - 2)))
+    first = [
+        jnp.concatenate([pick(part, spot ^ k) for part in (weight_qkv, weight_out, gains)], axis=1)
+        for k in range(spots)
+    ]
+    *first, rows_in = tie(*first, frames_in)
+    first = [hop(piece, k, spots) for k, piece in enumerate(first)]
+    own_rows = rows_to_spots(rows_in)
+    gates = [pick(weight_ffn, spot ^ k)[:, :hidden_units] for k in range(spots)]
+    ups = [pick(weight_ffn, spot ^ k)[:, hidden_units:] for k in range(spots)]
+    tied = tie(own_rows, *first, *gates)
+    own_rows, first, gates = tied[0], tied[1 : spots + 1], list(tied[spots + 1 :])
+    gates[:near] = [hop(piece, k, spots) for k, piece in enumerate(gates[:near])]
+    got_rows = trade(own_rows)
+
+    own_count = own_rows.shape[0]
+    count = own_count * 2
+    step = own_count // 2
+    qkv_own, qkv_sent, full_out, gains = split_columns(
+        [[piece] for piece in first], heads, by_spot, ((3 * depth, depth), (4 * depth, LANES))
+    )
+    qkv_other = trade(qkv_sent)
+    gains = gains[:, :2]
+    pair = [part.reshape(spots, slice_rows, 2) for part in (gains, trade(gains))]
+    even, odd = (jnp.where(half == h, *pair) for h in range(2))
+    gains = jnp.stack([even, odd], axis=1).reshape(depth, 2).T.astype(f32)
+    gain_one, gain_two = gains[:1], gains[1:]
+    qkv_other, *gates[:near] = tie(qkv_other, *gates[:near])
+    mine, theirs = halves_rows(step, own_rows)
+    straight = lambda r, *s: (r, 0)
+    crossed = lambda r, *s: ((r + 2) % 4, 0)
+    top = lambda r, *s: (0, 0)
+    rows = [(own_rows, (step, depth), mine), (got_rows, (step, depth), theirs)]
+    split_rows = [((count, depth // 2), bf16, (step, depth // 2), straight)] * 2
+    low_scratch, scratch = pltpu.VMEM((step, depth), bf16), pltpu.VMEM((step, depth), f32)
+    one_own, one_other = call(
+        norm_kernel, "norm", (4,), rows + [(gain_one, (1, depth), top)], split_rows, by_spot, [low_scratch]
+    )
+    qkv_rows = (plain(one_own, qkv_own) + plain(one_other, qkv_other)).astype(bf16)
+    tied = tie(*gates, *ups[:near])
+    gates, ups[:near] = list(tied[:spots]), tied[spots:]
+    ups[:near] = [hop(piece, k, spots) for k, piece in enumerate(ups[:near])]
+    gates[near] = hop(gates[near], near, spots)
+    qkv = swap(qkv_rows, positions)
+    mixed = over_frames(attend_kernel, depth // 2, qkv)
+    mixed, *ups[:near], gates[near] = tie(mixed, *ups[:near], gates[near])
+    ups[near], gates[near] = tie(ups[near], gates[near])
+    ups[near] = hop(ups[near], near, spots)
+    third = [pick(weight_down, down_index ^ k) for k in range(spots)]
+    gates[near], *third = tie(gates[near], *third)
+    third = [lax.ppermute(p, PLANE, down_pairs[k]) for k, p in enumerate(third)]
+    mixed = swap(mixed, positions).reshape(count, -1)
+    upstream = jnp.where(live, grad_out, jnp.zeros_like(grad_out))
+    mixed, upstream = tie(mixed, upstream)
+    own_up = rows_to_spots(upstream)
+    branch = plain(mixed, full_out)
+    branch, ups[near] = tie(branch, ups[near])
+    middle, two_own, two_other = call(
+        middle_kernel,
+        "middle",
+        (4,),
+        rows
+        + [(branch, (step, depth), straight), (trade(branch), (step, depth), crossed)]
+        + [(gain_two, (1, depth), top)],
+        [((count, depth), f32, (step, depth), straight)] + split_rows,
+        by_spot,
+        [low_scratch],
+    )
+
+    ffn_own, ffn_sent = split_columns(list(zip(gates, ups)), units, by_spot)
+    ffn_other = trade(ffn_sent)
+    ffn_other, *third[:early] = tie(ffn_other, *third[:early])
+    gate_up = plain(two_own, ffn_own) + plain(two_other, ffn_other)
+    gate_up, *third = tie(gate_up, *third)
+    width = gate_up.shape[1] // 2
+    gate, upward = gate_up[:, :width], gate_up[:, width:]
+    gate_sig = jax.nn.sigmoid(gate)
+    hidden = (gate * gate_sig * upward).astype(bf16)
+    got_up = trade(own_up)
+    upstream = jnp.concatenate([own_up, got_up])
+    down_grad = over_rows(hidden, upstream).astype(bf16).reshape(spots, -1, depth)
+    down_sent = [pick(down_grad, spot ^ k) for k in range(spots)]
+    hidden, *down_sent = tie(hidden, *down_sent)
+    down_back = [[(b, a) for a, b in pairs] for pairs in down_pairs]
+    for k in range(0, spots, 2):
+        down_sent[k] = lax.ppermute(down_sent[k], PLANE, down_back[k])
+    down_sent = list(tie(*down_sent))
+    for k in range(1, spots, 2):
+        down_sent[k] = lax.ppermute(down_sent[k], PLANE, down_back[k])
+    full_down = jnp.zeros((spots,) + third[0].shape, bf16)
+    for k, piece in enumerate(third):
+        full_down = lax.dynamic_update_index_in_dim(full_down, piece, spot ^ k, 0)
+    full_down = full_down.reshape(-1, depth)
+
+    grad_hidden = by_columns(upstream, full_down)
+    grad_upward = grad_hidden * gate * gate_sig
+    grad_gate = grad_hidden * upward * gate_sig * (1.0 + gate * (1.0 - gate_sig))
+    grad_gate_up = jnp.concatenate([grad_gate, grad_upward], axis=-1).astype(bf16)
+    back_own = by_columns(grad_gate_up, ffn_own)
+    back_other = by_columns(grad_gate_up, ffn_other)
+    got_own, got_other = trade(back_own), trade(back_other)
+    got_other, grad_gate_up, *down_sent[::2] = tie(got_other, grad_gate_up, *down_sent[::2])
+    wide, narrow = (step, depth), (step, depth // 2)
+    grad_middle, grad_branch, term_two = call(
+        middle_back_kernel,
+        "middle_back",
+        (4,),
+        [(middle, wide, straight), (back_own, narrow, straight), (back_other, narrow, straight)]
+        + [(got_own, narrow, crossed), (got_other, narrow, crossed)]
+        + [(own_up, wide, mine), (got_up, wide, theirs), (gain_two, (1, depth), top)],
+        [
+            ((count, depth), f32, wide, straight),
+            ((count, depth), bf16, wide, straight),
+            ((1, depth), f32, (1, depth), top),
+        ],
+        by_spot,
+        [scratch],
+    )
+
+    cut = lambda grad: [pick(grad.reshape(spots, slice_rows, -1), spot ^ k) for k in range(spots)]
+    grad_mixed = by_columns(grad_branch, full_out).astype(bf16)
+    grad_mixed, *down_sent = tie(grad_mixed, *down_sent)
+    grad_mixed_frames = swap(grad_mixed, positions)
+    ffn_grad_own = cut(over_rows(two_own, grad_gate_up).astype(bf16))
+    ffn_grad_got = cut(trade(over_rows(two_other, grad_gate_up).astype(bf16)))
+    tied = tie(*down_sent, *ffn_grad_own)
+    down_sent, ffn_grad_own = tied[:spots], list(tied[spots:])
+    ffn_grad_own = [hop(piece, k, spots) for k, piece in enumerate(ffn_grad_own)]
+    grad_mixed_frames, *ffn_grad_own[:near] = tie(grad_mixed_frames, *ffn_grad_own[:near])
+    grad_qkv = over_frames(attend_back_kernel, 3 * depth // 2, qkv, grad_mixed_frames)
+    late = [
+        jnp.concatenate(pair, axis=1)
+        for pair in zip(ffn_grad_got, cut(over_rows(mixed, grad_branch).astype(bf16)))
+    ]
+    grad_qkv, ffn_grad_own[near], *late = tie(grad_qkv, ffn_grad_own[near], *late)
+    late[:near] = [hop(piece, k, spots) for k, piece in enumerate(late[:near])]
+    result = plain(hidden, full_down)
+    result = (middle[:own_count] + result[:own_count] + trade(result[own_count:])).astype(bf16)
+    sum_down = place([[(piece, 0)] for piece in down_sent], by_slice, *weight_down.shape[1:])
+    grad_qkv_rows = swap(grad_qkv, positions).reshape(count, -1)
+    grad_qkv_rows, result, sum_down, *late = tie(grad_qkv_rows, result, sum_down, *late)
+    late[near] = hop(late[near], near, spots)
+    result = rows_from_spots(result)
+    qkv_grad_got = trade(over_rows(one_other, grad_qkv_rows).astype(bf16))
+    qkv_grad_own = over_rows(one_own, grad_qkv_rows).astype(bf16)
+    qkv_sent = [jnp.concatenate(pair) for pair in zip(cut(qkv_grad_own), cut(qkv_grad_got))]
+    *qkv_sent, grad_qkv_rows = tie(*qkv_sent, grad_qkv_rows)
+    qkv_sent = [hop(piece, k, spots) for k, piece in enumerate(qkv_sent)]
+    back_own = by_columns(grad_qkv_rows, qkv_own)
+    back_other = by_columns(grad_qkv_rows, qkv_other)
+    got_own, got_other = trade(back_own[own_count:]), trade(back_other[own_count:])
+    got_other, result, late[near] = tie(got_other, result, late[near])
+    grad_rows, term_one = call(
+        input_back_kernel,
+        "input_back",
+        (2,),
+        [(own_rows, wide, straight), (back_own, narrow, straight), (back_other, narrow, straight)]
+        + [(got_own, narrow, straight), (got_other, narrow, straight)]
+        + [(grad_middle, wide, straight), (gain_one, (1, depth), top)],
+        [((own_count, depth), bf16, wide, straight), ((1, depth), f32, (1, depth), top)],
+        by_spot,
+        [scratch],
+    )
+    grad_rows, *qkv_sent[:near] = tie(grad_rows, *qkv_sent[:near])
+    grad_input = rows_from_spots(grad_rows)
+    grad_input, term_one = tie(grad_input, term_one)
+    output = jnp.where(live, result, jnp.zeros_like(result))
+
+    sum_ffn = place(
+        [[(own, 0), (got, 0)] for own, got in zip(ffn_grad_own, late)],
+        by_spot,
+        slice_rows,
+        2 * hidden_units,
+        units,
+    )
+    sum_out = place([[(piece, 0)] for piece in late], by_spot, slice_rows, depth, skip=hidden_units)
+    sum_qkv = place(
+        [[(piece, 0), (piece, slice_rows)] for piece in qkv_sent], by_spot, slice_rows, 3 * depth, heads
+    )
+    terms = jnp.stack([term_one, term_two]).reshape(2, plane, depth // plane)
+    terms = lax.all_to_all(
+        jnp.transpose(terms, (1, 0, 2)), PLANE, split_axis=0, concat_axis=0, tiled=True
+    )
+    terms = jnp.sum(terms.reshape(spots, 2, 2, depth // plane), axis=1)
+    return (output, grad_input, sum_qkv, sum_out, sum_ffn, sum_down, terms[:, 0], terms[:, 1])
+
+
 def solution(mesh):
-    placed = (
-        P(("frames", "pos"), None, None),
-        P(("frames", "pos")),
-        P(("frames", "pos")),
-        P("pos", "frames", None),
-        P("pos", "frames", None),
-        P("pos", "frames", None),
-        P("pos", "frames", None),
-        P("pos", "frames"),
-        P("pos", "frames"),
-        P(("frames", "pos"), None, None),
-    )
-    return jax.shard_map(
-        on_device,
-        mesh=mesh,
-        in_specs=placed,
-        out_specs=(
-            P(("frames", "pos"), None, None),
-            P(("frames", "pos"), None, None),
-            P("pos", "frames", None),
-            P("pos", "frames", None),
-            P("pos", "frames", None),
-            P("pos", "frames", None),
-            P("pos", "frames"),
-            P("pos", "frames"),
-        ),
-        check_vma=False,
-    )
+    plane, lines = mesh.shape["frames"], mesh.shape["pos"]
+
+    def run(*arrays):
+        positions, depth = arrays[0].shape[1:]
+        spots = positions // lines
+        slice_rows = depth // plane
+        shares = arrays[5].shape[2] // 4
+        fits = plane == 2 * spots and spots & (spots - 1) == 0
+        fits = fits and slice_rows % LANES == 0 and shares % LANES == 0
+        if fits:
+            inner = Mesh(mesh.devices.reshape(spots, 2, lines), PLANE + ("pos",))
+            by_frame, weight, plan = P(PLANE + ("pos",)), P("pos", PLANE), spots_plan
+        else:
+            inner, plan = mesh, gathered_plan
+            by_frame, weight = P(("frames", "pos")), P("pos", "frames")
+        return jax.shard_map(
+            plan,
+            mesh=inner,
+            in_specs=(by_frame,) * 3 + (weight,) * 6 + (by_frame,),
+            out_specs=(by_frame,) * 2 + (weight,) * 6,
+            check_vma=False,
+        )(*arrays)
+
+    return run

time: 1380 us -> 524 us (0.38)
  waiting for transfers between devices: 1050 us -> 223 us
  matrix products: 177 us -> 51.6 us
  starting transfers between devices: 37.2 us -> 100 us
  Pallas kernels: 0 us -> 58.2 us
  blocking collectives: 18.1 us -> 0 us
  other arithmetic: 33.2 us -> 19.4 us
    reduce_scatter x4 -> x0, waiting for transfers between devices: 566 us -> none  [the longest x1 263 us: on_device(): lax.psum_scatter(term_ffn.astype(jnp.bfloat16), 'frames', scatter_dimensi...]
    all_gather x4 -> x0, waiting for transfers between devices: 369 us -> none  [the longest x1 170 us: on_device(): lax.all_gather(weight_ffn, 'frames', axis=1, tiled=True)]
    ppermute x0 -> x39, waiting for transfers between devices: none -> 171 us  [the longest x18 136 us: hop(): lax.ppermute(value, 'spot', [(i, i ^ k) for i in range(spots)])]
    dot_general x18, matrix products: 177 us -> 51.6 us  [the longest x6 17.5 us: over_rows(): lax.dot_general(left, right, (((0,), (0,)), ((), ())), preferred_element_...]
    all_to_all x8 -> x9, waiting for transfers between devices: 112 us -> 51.7 us  [the longest x4 36.9 us: swap(): lax.all_to_all(values.reshape(blocks, -1, values.shape[-1]), ROWS, split_...]
    pallas_call x0 -> x12, Pallas kernels: none -> 58.2 us  [the longest x10 45.6 us: call(): pl.pallas_call(kernel, grid_spec=pltpu.PrefetchScalarGridSpec(num_scalar_...]
    ppermute x0 -> x39, starting transfers between devices: none -> 51.9 us  [the longest x18 24.7 us: hop(): lax.ppermute(value, 'spot', [(i, i ^ k) for i in range(spots)])]
    convert_element_type x10 -> x2, other arithmetic: 25.5 us -> 3.04 us  [the longest x1 3.03 us: spots_plan(): (middle[:own_count] + result[:own_count] + trade(result[own_count:])).ast...]
  transfers between devices with their start and end apart: 18 -> 48, of which waited for: 13 -> 23; matrix products, arithmetic and copies ran while one was open for 13% -> 18% of each run, Pallas kernels for 0% -> 9%
where the time goes in v2:
time: 524 us; the launch traced here: 514 us
  waiting for transfers between devices  223 us (43%)
  starting transfers between devices  100 us (19%)
  local copies, waits for them, and re-layouts  59.9 us (11%)
  Pallas kernels  58.2 us (11%)
  matrix products  51.6 us (10%)
  other arithmetic  19.4 us (4%)
    ppermute x18, waiting for transfers between devices, hop(): lax.ppermute(value, 'spot', [(i, i ^ k) for i in range(spots)])  136 us
    pallas_call x10, Pallas kernels, call(): pl.pallas_call(kernel, grid_spec=pltpu.PrefetchScalarGridSpec(num_scalar_...  45.6 us
    all_to_all x4, waiting for transfers between devices, swap(): lax.all_to_all(values.reshape(blocks, -1, values.shape[-1]), ROWS, split_...  36.9 us
    ppermute x18, starting transfers between devices, hop(): lax.ppermute(value, 'spot', [(i, i ^ k) for i in range(spots)])  24.7 us
    unnamed x111, local copies, waits for them, and re-layouts  24.5 us
    ppermute x4, waiting for transfers between devices, spots_plan(): down_sent[k] = lax.ppermute(down_sent[k], PLANE, down_back[k])  21.1 us
    all_to_all x4, starting transfers between devices, swap(): lax.all_to_all(values.reshape(blocks, -1, values.shape[-1]), ROWS, split_...  20.2 us
    squeeze x10, local copies, waits for them, and re-layouts, pick(): return lax.dynamic_index_in_dim(stack, index, 0, keepdims=False)  19 us
  transfers between devices with their start and end apart: 48, of which 23 were waited for; matrix products, arithmetic and copies ran while one was open for 18% of the time, Pallas kernels for 9%

profile of v2, /device:TPU:0, one launch (start us, length us, event | category | flops | bytes accessed | tf_op | source)
XLA Modules:
  0.0 513.9 jit_solution(8700704776153054549)
XLA Ops:
  8.7 8.3 %all-to-all-start = ((bf16[16,16,1024]{2,0,1:T(8,128)(2,1)}), bf16[16,16,1024]{2,0,1:T(8,128)(2,1)S(1)}, u32[]{:S(2)}, u32[]{:S(2)}) async-start(bf16[16,16,1024]{2,0,1:T(8,128)(2,1)} %copy.70), calls=%async_computation | async-start | bytes 1048576 | tf_op jit(solution)/shard_map/all_to_all | solution.py:207
  20.6 4.6 dynamic-slice_bitcast_fusion
  32.2 17.5 %collective-permute-done.refs_1_ = bf16[128,4224]{1,0:T(8,128)(2,1)} collective-permute-done((bf16[128,4224]{1,0:T(8,128)(2,1)}, bf16[128,4224]{1,0:T(8,128)(2,1)}, u32[]{:S(2)}, u32[]{:S(2)}) %collective-permute-start) | collective-permute-done | bytes 1081376 | tf_op jit(solution)/shard_map/ppermute | solution.py:199
  49.8 22.4 %collective-permute-done.2.refs_3_ = bf16[128,4224]{1,0:T(8,128)(2,1)} collective-permute-done((bf16[128,4224]{1,0:T(8,128)(2,1)}, bf16[128,4224]{1,0:T(8,128)(2,1)}, u32[]{:S(2)}, u32[]{:S(2)}) %collective-permute-start.2) | collective-permute-done | bytes 1081376 | tf_op jit(solution)/shard_map/ppermute | solution.py:199
  72.3 5.1 split_columns.2
  84.1 13.1 %collective-permute-done.6.refs_2_ = bf16[128,2816]{1,0:T(8,128)(2,1)} collective-permute-done((bf16[128,2816]{1,0:T(8,128)(2,1)}, bf16[128,2816]{1,0:T(8,128)(2,1)}, u32[]{:S(2)}, u32[]{:S(2)}) %collective-permute-start.6) | collective-permute-done | bytes 720928 | tf_op jit(solution)/shard_map/ppermute | solution.py:199
  102.6 5.1 all-to-all-start.1
  111.3 30.5 %all-to-all-done.1.qkv_ref = bf16[16,32,1536]{2,1,0:T(8,128)(2,1)S(1)} async-done(((bf16[16,32,1536]{2,1,0:T(8,128)(2,1)}), bf16[16,32,1536]{2,1,0:T(8,128)(2,1)S(1)}, u32[]{:S(2)}, u32[]{:S(2)}) %all-to-all-start.1) | async-done | bytes 1572896 | tf_op jit(solution)/shard_map/all_to_all | solution.py:216
  145.8 12.6 %collective-permute-done.10.refs_6_ = bf16[128,2816]{1,0:T(8,128)(2,1)} collective-permute-done((bf16[128,2816]{1,0:T(8,128)(2,1)}, bf16[128,2816]{1,0:T(8,128)(2,1)}, u32[]{:S(2)}, u32[]{:S(2)}) %collective-permute-start.10) | collective-permute-done | bytes 720928 | tf_op jit(solution)/shard_map/ppermute | solution.py:199
  158.4 4.6 all-to-all-start.2
  171.1 6.4 %all-to-all-done.2 = bf16[16,32,512]{2,1,0:T(8,128)(2,1)} async-done(((bf16[16,32,512]{2,1,0:T(8,128)(2,1)}), bf16[16,32,512]{2,1,0:T(8,128)(2,1)}, u32[]{:S(2)}, u32[]{:S(2)}) %all-to-all-start.2) | async-done | bytes 524320 | tf_op jit(solution)/shard_map/all_to_all | solution.py:216
  180.9 6.3 %collective-permute-done.11.refs_7_ = bf16[128,2816]{1,0:T(8,128)(2,1)} collective-permute-done((bf16[128,2816]{1,0:T(8,128)(2,1)}, bf16[128,2816]{1,0:T(8,128)(2,1)}, u32[]{:S(2)}, u32[]{:S(2)}) %collective-permute-start.11) | collective-permute-done | bytes 720928 | tf_op jit(solution)/shard_map/ppermute | solution.py:199
  187.3 5.9 %split_columns.3 = (bf16[4,128,2816]{2,1,0:T(8,128)(2,1)}, bf16[4,128,2816]{2,1,0:T(8,128)(2,1)}) custom-call(s32[5]{0:T(128)S(1)} %stack.62.scalars, bf16[128,2816]{1,0:T(8,128)(2,1)S(1)} %get-tuple-element.166.refs_0_, bf16[128,2816]{1,0:T(8,128)(2,1)S(1)} %get-tuple-element.167.refs_1_, bf16[128,2816]{1,0:T(8,128)(2,1)} %collective-permute-done.6.refs_2_, ...), custom_call_target="tpu_custom_call" | custom-call | bytes 720896 | tf_op jit(solution)/shard_map/split_columns/pallas_call | solution.py:233
  193.7 5.2 %all-to-all-start.3 = ((bf16[16,16,1024]{2,0,1:T(8,128)(2,1)}), bf16[16,16,1024]{2,0,1:T(8,128)(2,1)}, u32[]{:S(2)}, u32[]{:S(2)}) async-start(bf16[16,16,1024]{2,0,1:T(8,128)(2,1)} %copy_select_fusion), calls=%async_computation.3 | async-start | bytes 1048576 | tf_op jit(solution)/shard_map/all_to_all | solution.py:207
  198.9 6.9 %collective-permute-start.15 = (bf16[352,1024]{1,0:T(8,128)(2,1)}, bf16[352,1024]{1,0:T(8,128)(2,1)}, u32[]{:S(2)}, u32[]{:S(2)}) collective-permute-start(bf16[352,1024]{1,0:T(8,128)(2,1)} %get-tuple-element.178), channel_id=1, source_target_pairs={{0,0},{4,8},{8,16},{12,24},{16,4},{20,12},{24,20},{28,28},{1,1},{5... | collective-permute-start | bytes 2162696 | tf_op jit(solution)/shard_map/ppermute | solution.py:589
  205.8 5.1 collective-permute-start.18
  217.3 4.8 collective-permute-start.13
  230.0 10.0 %collective-permute-done.17 = bf16[352,1024]{1,0:T(8,128)(2,1)} collective-permute-done((bf16[352,1024]{1,0:T(8,128)(2,1)}, bf16[352,1024]{1,0:T(8,128)(2,1)}, u32[]{:S(2)}, u32[]{:S(2)}) %collective-permute-start.17) | collective-permute-done | bytes 720928 | tf_op jit(solution)/shard_map/ppermute | solution.py:589
  263.8 13.2 %collective-permute-done.22.refs_2_ = bf16[352,1024]{1,0:T(8,128)(2,1)S(1)} collective-permute-done((bf16[352,1024]{1,0:T(8,128)(2,1)S(1)}, bf16[352,1024]{1,0:T(8,128)(2,1)S(1)}, u32[]{:S(2)}, u32[]{:S(2)}) %collective-permute-start.22) | collective-permute-done | bytes 720928 | tf_op jit(solution)/shard_map/ppermute | solution.py:624
  285.3 5.3 %middle_back.1 = (f32[512,1024]{1,0:T(8,128)}, bf16[512,1024]{1,0:T(8,128)(2,1)S(1)}, f32[1,1024]{1,0:T(1,128)S(1)}) custom-call(s32[5]{0:T(128)S(1)} %stack.62.scalars, f32[512,1024]{1,0:T(8,128)} %copy-done.1, f32[512,512]{1,0:T(8,128)S(1)} %fusion.11.own, f32[512,512]{1,0:T(8,128)S(1)} %fusion.10.other, f32[512,512]{1,0:T(8,128)S(1)} %collective-permute-done.19.got_own, ...), custom_call_target="tpu_custom_call" | custom-call | bytes 918016 | tf_op jit(solution)/shard_map/middle_back/pallas_call | solution.py:233
  295.4 4.9 collective-permute-done.23.refs_1_
  318.8 15.9 %collective-permute-done.25.refs_2_ = bf16[128,2816]{1,0:T(8,128)(2,1)S(1)} collective-permute-done((bf16[128,2816]{1,0:T(8,128)(2,1)S(1)}, bf16[128,2816]{1,0:T(8,128)(2,1)S(1)}, u32[]{:S(2)}, u32[]{:S(2)}) %collective-permute-start.25) | collective-permute-done | bytes 720928 | tf_op jit(solution)/shard_map/ppermute | solution.py:199
  335.6 9.4 %attend_back_kernel.1 = bf16[16,32,1536]{2,1,0:T(8,128)(2,1)S(1)} custom-call(bf16[16,32,1536]{2,1,0:T(8,128)(2,1)S(1)} %all-to-all-done.1.qkv_ref, bf16[16,32,512]{2,1,0:T(8,128)(2,1)S(1)} %all-to-all-done.4.grad_ref), custom_call_target="tpu_custom_call" | custom-call | flops 536870912 | bytes 3145728 | tf_op jit(solution)/shard_map/attend_back_kernel/pallas_call | solution.py:490
  350.8 6.1 %all-to-all-start.5 = ((bf16[16,32,1536]{2,1,0:T(8,128)(2,1)}), bf16[16,32,1536]{2,1,0:T(8,128)(2,1)}, u32[]{:S(2)}, u32[]{:S(2)}) async-start(bf16[16,32,1536]{2,1,0:T(8,128)(2,1)} %copy-done), calls=%async_computation.5 | async-start | bytes 3145728 | tf_op jit(solution)/shard_map/all_to_all | solution.py:216
  371.7 27.1 %collective-permute-done.30.refs_1_.refs_3_ = bf16[128,3840]{1,0:T(8,128)(2,1)S(1)} collective-permute-done((bf16[128,3840]{1,0:T(8,128)(2,1)}, bf16[128,3840]{1,0:T(8,128)(2,1)S(1)}, u32[]{:S(2)}, u32[]{:S(2)}) %collective-permute-start.30) | collective-permute-done | bytes 983072 | tf_op jit(solution)/shard_map/ppermute | solution.py:199
  406.6 6.0 %all-to-all-start.6 = ((bf16[16,2,8192]{2,1,0:T(2,128)(2,1)}), bf16[16,2,8192]{2,1,0:T(2,128)(2,1)}, u32[]{:S(2)}, u32[]{:S(2)}) async-start(bf16[16,2,8192]{2,1,0:T(2,128)(2,1)} %reshape.198), calls=%async_computation.6 | async-start | bytes 1048576 | tf_op jit(solution)/shard_map/all_to_all | solution.py:212
  436.4 8.2 %collective-permute-done.34.refs_3_.refs_7_ = bf16[128,3840]{1,0:T(8,128)(2,1)} collective-permute-done((bf16[128,3840]{1,0:T(8,128)(2,1)}, bf16[128,3840]{1,0:T(8,128)(2,1)}, u32[]{:S(2)}, u32[]{:S(2)}) %collective-permute-start.34) | collective-permute-done | bytes 983072 | tf_op jit(solution)/shard_map/ppermute | solution.py:199
  449.2 10.6 %collective-permute-done.36.refs_2_.refs_3_ = bf16[256,1536]{1,0:T(8,128)(2,1)} collective-permute-done((bf16[256,1536]{1,0:T(8,128)(2,1)}, bf16[256,1536]{1,0:T(8,128)(2,1)}, u32[]{:S(2)}, u32[]{:S(2)}) %collective-permute-start.36) | collective-permute-done | bytes 786464 | tf_op jit(solution)/shard_map/ppermute | solution.py:199
  464.0 5.1 all-to-all-start.7
  471.8 12.7 %all-to-all-done.7 = bf16[16,2,8192]{2,1,0:T(2,128)(2,1)} async-done(((bf16[16,2,8192]{2,1,0:T(2,128)(2,1)}), bf16[16,2,8192]{2,1,0:T(2,128)(2,1)}, u32[]{:S(2)}, u32[]{:S(2)}) %all-to-all-start.7) | async-done | bytes 524320 | tf_op jit(solution)/shard_map/all_to_all | solution.py:212
  498.0 8.5 %place.7 = f32[4,128,5632]{2,1,0:T(8,128)} custom-call(s32[5]{0:T(128)S(1)} %stack.62.scalars, bf16[128,2816]{1,0:T(8,128)(2,1)S(1)} %copy-done.4, bf16[128,3840]{1,0:T(8,128)(2,1)S(1)} %pad_maximum_fusion.6.refs_0_.refs_1_, bf16[128,2816]{1,0:T(8,128)(2,1)S(1)} %copy-done.23, bf16[128,3840]{1,0:T(8,128)(2,1)S(1)} %copy-done.3, ...), custom_call_target="tpu_custom_call" | custom-call | bytes 851968 | tf_op jit(solution)/shard_map/place/pallas_call | solution.py:233
  506.5 5.3 %place.5 = f32[4,128,3072]{2,1,0:T(8,128)} custom-call(s32[5]{0:T(128)S(1)} %stack.62.scalars, bf16[256,1536]{1,0:T(8,128)(2,1)S(1)} %pad_maximum_fusion.10.refs_0_.refs_1_, bf16[256,1536]{1,0:T(8,128)(2,1)S(1)} %pad_maximum_fusion.10.refs_0_.refs_1_, bf16[256,1536]{1,0:T(8,128)(2,1)} %collective-permute-done.36.refs_2_.refs_3_, ...), custom_call_target="tpu_custom_call" | custom-call | bytes 786432 | tf_op jit(solution)/shard_map/place/pallas_call | solution.py:233
  (264 shorter events, 199.3 us)
Async XLA Ops:
  8.7 23.5 %all-to-all-start = ((bf16[16,16,1024]{2,0,1:T(8,128)(2,1)}), bf16[16,16,1024]{2,0,1:T(8,128)(2,1)S(1)}, u32[]{:S(2)}, u32[]{:S(2)}) async-start(bf16[16,16,1024]{2,0,1:T(8,128)(2,1)} %copy.70), calls=%async_computation | async-start | bytes 1048576 | tf_op jit(solution)/shard_map/all_to_all | solution.py:207
  17.0 32.6 %collective-permute-start = (bf16[128,4224]{1,0:T(8,128)(2,1)}, bf16[128,4224]{1,0:T(8,128)(2,1)}, u32[]{:S(2)}, u32[]{:S(2)}) collective-permute-start(bf16[128,4224]{1,0:T(8,128)(2,1)} %get-tuple-element.132), channel_id=1, source_target_pairs={{0,8},{8,0},{16,24},{24,16},{1,9},{9,1},{17,25},{25,17},{2,10},{10... | collective-permute-start | bytes 3244040 | tf_op jit(solution)/shard_map/ppermute | solution.py:199
  19.0 30.9 %collective-permute-start.1 = (bf16[128,4224]{1,0:T(8,128)(2,1)}, bf16[128,4224]{1,0:T(8,128)(2,1)}, u32[]{:S(2)}, u32[]{:S(2)}) collective-permute-start(bf16[128,4224]{1,0:T(8,128)(2,1)} %get-tuple-element.133), channel_id=1, source_target_pairs={{0,16},{8,24},{16,0},{24,8},{1,17},{9,25},{17,1},{25,9},{2,18},{10... | collective-permute-start | bytes 3244040 | tf_op jit(solution)/shard_map/ppermute | solution.py:199
  20.4 51.8 %collective-permute-start.2 = (bf16[128,4224]{1,0:T(8,128)(2,1)}, bf16[128,4224]{1,0:T(8,128)(2,1)}, u32[]{:S(2)}, u32[]{:S(2)}) collective-permute-start(bf16[128,4224]{1,0:T(8,128)(2,1)} %get-tuple-element.134), channel_id=1, source_target_pairs={{0,24},{8,16},{16,8},{24,0},{1,25},{9,17},{17,9},{25,1},{2,26},{10... | collective-permute-start | bytes 3244040 | tf_op jit(solution)/shard_map/ppermute | solution.py:199
  102.6 39.1 %all-to-all-start.1 = ((bf16[16,32,1536]{2,1,0:T(8,128)(2,1)}), bf16[16,32,1536]{2,1,0:T(8,128)(2,1)S(1)}, u32[]{:S(2)}, u32[]{:S(2)}) async-start(bf16[16,32,1536]{2,1,0:T(8,128)(2,1)} %bitcast.205), calls=%async_computation.1 | async-start | bytes 3145728 | tf_op jit(solution)/shard_map/all_to_all | solution.py:216
  107.7 38.1 %collective-permute-start.8 = (bf16[128,2816]{1,0:T(8,128)(2,1)}, bf16[128,2816]{1,0:T(8,128)(2,1)}, u32[]{:S(2)}, u32[]{:S(2)}) collective-permute-start(bf16[128,2816]{1,0:T(8,128)(2,1)} %get-tuple-element.154), channel_id=1, source_target_pairs={{0,8},{8,0},{16,24},{24,16},{1,9},{9,1},{17,25},{25,17},{2,10},{10... | collective-permute-start | bytes 2162696 | tf_op jit(solution)/shard_map/ppermute | solution.py:199
  109.7 36.1 %collective-permute-start.9 = (bf16[128,2816]{1,0:T(8,128)(2,1)}, bf16[128,2816]{1,0:T(8,128)(2,1)}, u32[]{:S(2)}, u32[]{:S(2)}) collective-permute-start(bf16[128,2816]{1,0:T(8,128)(2,1)} %get-tuple-element.155), channel_id=1, source_target_pairs={{0,16},{8,24},{16,0},{24,8},{1,17},{9,25},{17,1},{25,9},{2,18},{10... | collective-permute-start | bytes 2162696 | tf_op jit(solution)/shard_map/ppermute | solution.py:199
  111.2 47.3 %collective-permute-start.10 = (bf16[128,2816]{1,0:T(8,128)(2,1)}, bf16[128,2816]{1,0:T(8,128)(2,1)}, u32[]{:S(2)}, u32[]{:S(2)}) collective-permute-start(bf16[128,2816]{1,0:T(8,128)(2,1)} %get-tuple-element.156), channel_id=1, source_target_pairs={{0,24},{8,16},{16,8},{24,0},{1,25},{9,17},{17,9},{25,1},{2,26},{10... | collective-permute-start | bytes 2162696 | tf_op jit(solution)/shard_map/ppermute | solution.py:199
  163.8 23.5 %collective-permute-start.11 = (bf16[128,2816]{1,0:T(8,128)(2,1)}, bf16[128,2816]{1,0:T(8,128)(2,1)}, u32[]{:S(2)}, u32[]{:S(2)}) collective-permute-start(bf16[128,2816]{1,0:T(8,128)(2,1)} %get-tuple-element.161), channel_id=1, source_target_pairs={{0,24},{8,16},{16,8},{24,0},{1,25},{9,17},{17,9},{25,1},{2,26},{10... | collective-permute-start | bytes 2162696 | tf_op jit(solution)/shard_map/ppermute | solution.py:199
  193.2 31.4 %collective-permute-start.14 = (bf16[512,2816]{1,0:T(8,128)(2,1)}, bf16[512,2816]{1,0:T(8,128)(2,1)}, u32[]{:S(2)}, u32[]{:S(2)}) collective-permute-start(bf16[512,2816]{1,0:T(8,128)(2,1)} %bitcast.227), channel_id=1, source_target_pairs={{0,4},{4,0},{1,5},{5,1},{2,6},{6,2},{3,7},{7,3},{8,12},{12,8},{9,1... | collective-permute-start | bytes 8650760 | tf_op jit(solution)/shard_map/ppermute | solution.py:203
  193.7 23.6 %all-to-all-start.3 = ((bf16[16,16,1024]{2,0,1:T(8,128)(2,1)}), bf16[16,16,1024]{2,0,1:T(8,128)(2,1)}, u32[]{:S(2)}, u32[]{:S(2)}) async-start(bf16[16,16,1024]{2,0,1:T(8,128)(2,1)} %copy_select_fusion), calls=%async_computation.3 | async-start | bytes 1048576 | tf_op jit(solution)/shard_map/all_to_all | solution.py:207
  205.8 34.3 %collective-permute-start.17 = (bf16[352,1024]{1,0:T(8,128)(2,1)}, bf16[352,1024]{1,0:T(8,128)(2,1)}, u32[]{:S(2)}, u32[]{:S(2)}) collective-permute-start(bf16[352,1024]{1,0:T(8,128)(2,1)} %get-tuple-element.183), channel_id=1, source_target_pairs={{0,16},{4,24},{8,0},{12,8},{16,20},{20,28},{24,4},{28,12},{1,17},{... | collective-permute-start | bytes 2162696 | tf_op jit(solution)/shard_map/ppermute | solution.py:589
  205.8 34.3 %collective-permute-start.18 = (bf16[352,1024]{1,0:T(8,128)(2,1)}, bf16[352,1024]{1,0:T(8,128)(2,1)}, u32[]{:S(2)}, u32[]{:S(2)}) collective-permute-start(bf16[352,1024]{1,0:T(8,128)(2,1)} %get-tuple-element.184), channel_id=1, source_target_pairs={{0,24},{4,16},{8,8},{12,0},{16,28},{20,20},{24,12},{28,4},{1,25},{... | collective-permute-start | bytes 2162696 | tf_op jit(solution)/shard_map/ppermute | solution.py:589
  217.3 27.8 %collective-permute-start.13 = (bf16[256,1024]{1,0:T(8,128)(2,1)}, bf16[256,1024]{1,0:T(8,128)(2,1)S(1)}, u32[]{:S(2)}, u32[]{:S(2)}) collective-permute-start(bf16[256,1024]{1,0:T(8,128)(2,1)} %bitcast.35.own_up), channel_id=1, source_target_pairs={{0,4},{4,0},{1,5},{5,1},{2,6},{6,2},{3,7},{7,3},{8,12},{12,8},{9,1... | collective-permute-start | bytes 1572872 | tf_op jit(solution)/shard_map/ppermute | solution.py:203
  253.5 23.5 %collective-permute-start.20 = (f32[512,512]{1,0:T(8,128)S(1)}, f32[512,512]{1,0:T(8,128)S(1)}, u32[]{:S(2)}, u32[]{:S(2)}) collective-permute-start(f32[512,512]{1,0:T(8,128)S(1)} %fusion.10.other), channel_id=1, source_target_pairs={{0,4},{4,0},{1,5},{5,1},{2,6},{6,2},{3,7},{7,3},{8,12},{12,8},{9,1... | collective-permute-start | bytes 3145736 | tf_op jit(solution)/shard_map/ppermute | solution.py:203
  263.5 21.8 %collective-permute-start.19 = (f32[512,512]{1,0:T(8,128)S(1)}, f32[512,512]{1,0:T(8,128)S(1)}, u32[]{:S(2)}, u32[]{:S(2)}) collective-permute-start(f32[512,512]{1,0:T(8,128)S(1)} %fusion.11.own), channel_id=1, source_target_pairs={{0,4},{4,0},{1,5},{5,1},{2,6},{6,2},{3,7},{7,3},{8,12},{12,8},{9,1... | collective-permute-start | bytes 3145736 | tf_op jit(solution)/shard_map/ppermute | solution.py:203
  280.3 64.8 %collective-permute-start.28 = (bf16[512,2816]{1,0:T(8,128)(2,1)}, bf16[512,2816]{1,0:T(8,128)(2,1)}, u32[]{:S(2)}, u32[]{:S(2)}) collective-permute-start(bf16[512,2816]{1,0:T(8,128)(2,1)} %convolution_convert_fusion), channel_id=1, source_target_pairs={{0,4},{4,0},{1,5},{5,1},{2,6},{6,2},{3,7},{7,3},{8,12},{12,8},{9,1... | collective-permute-start | bytes 8650760 | tf_op jit(solution)/shard_map/ppermute | solution.py:203
  282.4 21.8 %collective-permute-start.24 = (bf16[352,1024]{1,0:T(8,128)(2,1)S(1)}, bf16[352,1024]{1,0:T(8,128)(2,1)S(1)}, u32[]{:S(2)}, u32[]{:S(2)}) collective-permute-start(bf16[352,1024]{1,0:T(8,128)(2,1)S(1)} %get-tuple-element.201), channel_id=1, source_target_pairs={{24,0},{16,4},{8,8},{0,12},{28,16},{20,20},{12,24},{4,28},{25,1},{... | collective-permute-start | bytes 2162696 | tf_op jit(solution)/shard_map/ppermute | solution.py:627
  305.0 30.6 %all-to-all-start.4 = ((bf16[16,32,512]{2,1,0:T(8,128)(2,1)}), bf16[16,32,512]{2,1,0:T(8,128)(2,1)S(1)}, u32[]{:S(2)}, u32[]{:S(2)}) async-start(bf16[16,32,512]{2,1,0:T(8,128)(2,1)} %bitcast.54), calls=%async_computation.4 | async-start | bytes 1048576 | tf_op jit(solution)/shard_map/all_to_all | solution.py:216
  312.6 22.2 %collective-permute-start.25 = (bf16[128,2816]{1,0:T(8,128)(2,1)S(1)}, bf16[128,2816]{1,0:T(8,128)(2,1)S(1)}, u32[]{:S(2)}, u32[]{:S(2)}) collective-permute-start(bf16[128,2816]{1,0:T(8,128)(2,1)S(1)} %get-tuple-element.209), channel_id=1, source_target_pairs={{0,8},{8,0},{16,24},{24,16},{1,9},{9,1},{17,25},{25,17},{2,10},{10... | collective-permute-start | bytes 2162696 | tf_op jit(solution)/shard_map/ppermute | solution.py:199
  314.5 20.3 %collective-permute-start.26 = (bf16[128,2816]{1,0:T(8,128)(2,1)S(1)}, bf16[128,2816]{1,0:T(8,128)(2,1)S(1)}, u32[]{:S(2)}, u32[]{:S(2)}) collective-permute-start(bf16[128,2816]{1,0:T(8,128)(2,1)S(1)} %get-tuple-element.210), channel_id=1, source_target_pairs={{0,16},{8,24},{16,0},{24,8},{1,17},{9,25},{17,1},{25,9},{2,18},{10... | collective-permute-start | bytes 2162696 | tf_op jit(solution)/shard_map/ppermute | solution.py:199
  318.7 32.1 %collective-permute-start.27 = (bf16[128,2816]{1,0:T(8,128)(2,1)}, bf16[128,2816]{1,0:T(8,128)(2,1)}, u32[]{:S(2)}, u32[]{:S(2)}) collective-permute-start(bf16[128,2816]{1,0:T(8,128)(2,1)} %get-tuple-element.212), channel_id=1, source_target_pairs={{0,24},{8,16},{16,8},{24,0},{1,25},{9,17},{17,9},{25,1},{2,26},{10... | collective-permute-start | bytes 2162696 | tf_op jit(solution)/shard_map/ppermute | solution.py:199
  350.8 48.0 %all-to-all-start.5 = ((bf16[16,32,1536]{2,1,0:T(8,128)(2,1)}), bf16[16,32,1536]{2,1,0:T(8,128)(2,1)}, u32[]{:S(2)}, u32[]{:S(2)}) async-start(bf16[16,32,1536]{2,1,0:T(8,128)(2,1)} %copy-done), calls=%async_computation.5 | async-start | bytes 3145728 | tf_op jit(solution)/shard_map/all_to_all | solution.py:216
  361.8 37.0 %collective-permute-start.30 = (bf16[128,3840]{1,0:T(8,128)(2,1)}, bf16[128,3840]{1,0:T(8,128)(2,1)S(1)}, u32[]{:S(2)}, u32[]{:S(2)}) collective-permute-start(bf16[128,3840]{1,0:T(8,128)(2,1)} %pad_maximum_fusion.7), channel_id=1, source_target_pairs={{0,8},{8,0},{16,24},{24,16},{1,9},{9,1},{17,25},{25,17},{2,10},{10... | collective-permute-start | bytes 2949128 | tf_op jit(solution)/shard_map/ppermute | solution.py:199
  363.7 35.2 %collective-permute-start.31 = (bf16[128,3840]{1,0:T(8,128)(2,1)}, bf16[128,3840]{1,0:T(8,128)(2,1)}, u32[]{:S(2)}, u32[]{:S(2)}) collective-permute-start(bf16[128,3840]{1,0:T(8,128)(2,1)} %pad_maximum_fusion.8), channel_id=1, source_target_pairs={{0,16},{8,24},{16,0},{24,8},{1,17},{9,25},{17,1},{25,9},{2,18},{10... | collective-permute-start | bytes 2949128 | tf_op jit(solution)/shard_map/ppermute | solution.py:199
  406.6 24.0 %all-to-all-start.6 = ((bf16[16,2,8192]{2,1,0:T(2,128)(2,1)}), bf16[16,2,8192]{2,1,0:T(2,128)(2,1)}, u32[]{:S(2)}, u32[]{:S(2)}) async-start(bf16[16,2,8192]{2,1,0:T(2,128)(2,1)} %reshape.198), calls=%async_computation.6 | async-start | bytes 1048576 | tf_op jit(solution)/shard_map/all_to_all | solution.py:212
  412.6 32.0 %collective-permute-start.34 = (bf16[128,3840]{1,0:T(8,128)(2,1)}, bf16[128,3840]{1,0:T(8,128)(2,1)}, u32[]{:S(2)}, u32[]{:S(2)}) collective-permute-start(bf16[128,3840]{1,0:T(8,128)(2,1)} %pad_maximum_fusion.9), channel_id=1, source_target_pairs={{0,24},{8,16},{16,8},{24,0},{1,25},{9,17},{17,9},{25,1},{2,26},{10... | collective-permute-start | bytes 2949128 | tf_op jit(solution)/shard_map/ppermute | solution.py:199
  426.3 33.6 %collective-permute-start.36 = (bf16[256,1536]{1,0:T(8,128)(2,1)}, bf16[256,1536]{1,0:T(8,128)(2,1)}, u32[]{:S(2)}, u32[]{:S(2)}) collective-permute-start(bf16[256,1536]{1,0:T(8,128)(2,1)} %pad_maximum_fusion.11), channel_id=1, source_target_pairs={{0,8},{8,0},{16,24},{24,16},{1,9},{9,1},{17,25},{25,17},{2,10},{10... | collective-permute-start | bytes 2359304 | tf_op jit(solution)/shard_map/ppermute | solution.py:199
  426.8 33.9 %collective-permute-start.37 = (bf16[256,1536]{1,0:T(8,128)(2,1)}, bf16[256,1536]{1,0:T(8,128)(2,1)}, u32[]{:S(2)}, u32[]{:S(2)}) collective-permute-start(bf16[256,1536]{1,0:T(8,128)(2,1)} %pad_maximum_fusion.12), channel_id=1, source_target_pairs={{0,16},{8,24},{16,0},{24,8},{1,17},{9,25},{17,1},{25,9},{2,18},{10... | collective-permute-start | bytes 2359304 | tf_op jit(solution)/shard_map/ppermute | solution.py:199
  464.0 20.6 %all-to-all-start.7 = ((bf16[16,2,8192]{2,1,0:T(2,128)(2,1)}), bf16[16,2,8192]{2,1,0:T(2,128)(2,1)}, u32[]{:S(2)}, u32[]{:S(2)}) async-start(bf16[16,2,8192]{2,1,0:T(2,128)(2,1)} %reshape.200), calls=%async_computation.7 | async-start | bytes 1048576 | tf_op jit(solution)/shard_map/all_to_all | solution.py:212
  469.1 37.4 %collective-permute-start.38 = (bf16[256,1536]{1,0:T(8,128)(2,1)}, bf16[256,1536]{1,0:T(8,128)(2,1)}, u32[]{:S(2)}, u32[]{:S(2)}) collective-permute-start(bf16[256,1536]{1,0:T(8,128)(2,1)} %pad_maximum_fusion.13), channel_id=1, source_target_pairs={{0,24},{8,16},{16,8},{24,0},{1,25},{9,17},{17,9},{25,1},{2,26},{10... | collective-permute-start | bytes 2359304 | tf_op jit(solution)/shard_map/ppermute | solution.py:199
  488.3 24.6 %all-to-all-start.8 = ((f32[8,2,128]{2,1,0:T(2,128)}), f32[8,2,128]{2,1,0:T(2,128)S(1)}, u32[]{:S(2)}, u32[]{:S(2)}) async-start(f32[8,2,128]{2,1,0:T(2,128)} %maximum_bitcast_fusion), calls=%async_computation.8 | async-start | bytes 16384 | tf_op jit(solution)/shard_map/all_to_all | solution.py:719
  (67 other events, 537.6 us)

commit v3 on v2

--- a/solution.py
+++ b/solution.py
@@ -203,19 +203,14 @@
     return lax.ppermute(value, "half", [(0, 1), (1, 0)])
 
 
-def rows_to_spots(values):
-    moved = lax.all_to_all(values, ROWS, split_axis=1, concat_axis=0, tiled=True)
-    return moved.reshape(moved.shape[0], moved.shape[2])
-
-
-def rows_from_spots(values):
-    return lax.all_to_all(values[:, None], ROWS, split_axis=0, concat_axis=1, tiled=True)
-
-
 def swap(values, blocks):
     return lax.all_to_all(
         values.reshape(blocks, -1, values.shape[-1]), ROWS, split_axis=0, concat_axis=0, tiled=True
     )
+
+
+def rows_from_spots(values, blocks):
+    return swap(values, blocks).swapaxes(0, 1)
 
 
 def head_runs(width, groups, spots):
@@ -250,34 +245,67 @@
     return pl.ds(pl.multiple_of(start, LANES), size)
 
 
-def split_kernel(runs, count, per, rests, scalars, *refs):
+def collect_kernel(widths, scalars, *refs):
+    parts, outs = refs[: len(widths)], refs[len(widths) :]
+    for k, out in enumerate(outs):
+
+        @pl.when(pl.program_id(0) == k)
+        def _():
+            start = 0
+            for part, width in zip(parts, widths):
+                out[:, start : start + width] = part[0]
+                start += width
+
+
+def collect(parts, widths, scalars):
+    count, rows = scalars.shape[0] - 1, parts[0].shape[1]
+    cuts = 2
+    step, width = rows // cuts, sum(widths)
+
+    def spec(k):
+        return lambda j, r, s: (jnp.where(j == k, r, jnp.where(j < k, 0, cuts - 1)), 0)
+
+    return call(
+        functools.partial(collect_kernel, widths),
+        "collect",
+        (count, cuts),
+        [(a, (1, step, n), lambda j, r, s: (s[1 + j], r, 0)) for a, n in zip(parts, widths)],
+        [((rows, width), parts[0].dtype, (step, width), spec(k)) for k in range(count)],
+        scalars,
+    )
+
+
+def split_kernel(runs, count, per, whose, rests, scalars, *refs):
     starts, size = runs
     pieces, outs = refs[: count * per], refs[count * per :]
     half = scalars[0]
     for k in range(count):
         at = scalars[1 + k]
-        for i, (even, odd) in enumerate(starts):
-            piece, even, odd = (
-                (pieces[k * per + i], 0, size) if per > 1 else (pieces[k], even, odd)
-            )
-            for out, first, second in ((outs[0], even, odd), (outs[1], odd, even)):
+        for i, pair in enumerate(starts):
+            piece = pieces[k * per + (i if per > 1 else 0)]
+            for out, other in zip(outs, whose):
+                first, second = pair[::-1] if other else pair
                 columns = aligned(first + half * (second - first), size)
                 out[pl.ds(at, 1), :, i * size : (i + 1) * size] = piece[:, columns][None]
-        for out, (start, width) in zip(outs[2:], rests):
+        for out, (start, width) in zip(outs[len(whose) :], rests):
             out[pl.ds(at, 1)] = pieces[k][:, start : start + width][None]
 
 
-def split_columns(pieces, runs, scalars, rests=()):
+def split_columns(pieces, runs, scalars, whose=(False, True), width=None, rests=()):
     starts, size = runs
     per = len(pieces[0])
-    rows, width = pieces[0][0].shape
-    count, step = len(pieces), rows // 4
-    widths = [len(starts) * size] * 2 + [n for _, n in rests]
+    rows = pieces[0][0].shape[0]
+    count, step = len(pieces), rows // 2
+    widths = [len(starts) * size] * len(whose) + [n for _, n in rests]
     outs = call(
-        functools.partial(split_kernel, runs, count, per, rests),
+        functools.partial(split_kernel, runs, count, per, whose, rests),
         "split_columns",
-        (4,),
-        [(a, (step, width), lambda r, s: (r, 0)) for piece in pieces for a in piece],
+        (2,),
+        [
+            (a, (step, width or a.shape[1]), lambda r, s: (r, 0))
+            for piece in pieces
+            for a in piece
+        ],
         [
             ((count, rows, n), pieces[0][0].dtype, (count, step, n), lambda r, s: (0, r, 0))
             for n in widths
@@ -287,26 +315,30 @@
     return [out.reshape(count * rows, -1) for out in outs]
 
 
-def place_kernel(runs, parts, skip, scalars, *refs):
-    out = refs[-1]
+def place_kernel(runs, parts, skip, count, weighted, scalars, *refs):
+    pieces, out = refs[: count * parts], refs[count * parts + weighted]
     half = scalars[0]
-    for k in range((len(refs) - 1) // parts):
+    for k in range(count):
 
         @pl.when(pl.program_id(0) == k)
         def _():
             for p in range(parts):
-                ref = refs[k * parts + p]
+                ref = pieces[k * parts + p]
                 if runs is None:
-                    out[0] = ref[:, skip:].astype(jnp.float32)
+                    out[0] = ref[:, skip:].astype(out.dtype)
                     continue
                 starts, size = runs
                 for i, pair in enumerate(starts):
                     first, second = pair[::-1] if p else pair
                     columns = aligned(first + half * (second - first), size)
-                    out[0, :, columns] = ref[:, i * size : (i + 1) * size].astype(jnp.float32)
-
-
-def place(pieces, scalars, rows, width, runs=None, skip=0):
+                    out[0, :, columns] = ref[:, i * size : (i + 1) * size].astype(out.dtype)
+
+    if weighted:
+        products = out[0] * refs[count * parts][0].astype(jnp.float32)
+        refs[-1][0] = jnp.sum(products, axis=-1, keepdims=True)
+
+
+def place(pieces, scalars, rows, width, runs=None, skip=0, dtype=jnp.float32, weight=None):
     count, parts = len(pieces), len(pieces[0])
     cuts = 2 if rows * width > (1 << 19) else 1
     step = rows // cuts
@@ -315,25 +347,25 @@
         base = first // step
         return lambda j, r, s: (base + jnp.where(j == k, r, jnp.where(j < k, 0, cuts - 1)), 0)
 
-    return call(
-        functools.partial(place_kernel, runs, parts, skip),
+    entry = lambda j, r, s: (s[1 + j], r, 0)
+    inputs = [
+        (a, (step, a.shape[1]), spec(k, first))
+        for k, piece in enumerate(pieces)
+        for a, first in piece
+    ]
+    outputs = [((count, rows, width), dtype, (1, step, width), entry)]
+    if weight is not None:
+        inputs.append((weight, (1, step, width), entry))
+        outputs.append(((count, rows, 1), jnp.float32, (1, step, 1), entry))
+    outs = call(
+        functools.partial(place_kernel, runs, parts, skip, count, int(weight is not None)),
         "place",
         (count, cuts),
-        [
-            (a, (step, a.shape[1]), spec(k, first))
-            for k, piece in enumerate(pieces)
-            for a, first in piece
-        ],
-        [
-            (
-                (count, rows, width),
-                jnp.float32,
-                (1, step, width),
-                lambda j, r, s: (s[1 + j], r, 0),
-            )
-        ],
+        inputs,
+        outputs,
         scalars,
-    )[0]
+    )
+    return outs[0] if weight is None else outs
 
 
 def halves_rows(step, own):
@@ -385,37 +417,24 @@
     unit, inverse = unit_of(values)
     scaled = upstream * gain
     inner = jnp.mean(scaled * unit, axis=-1, keepdims=True)
-    return inverse * (scaled - unit * inner), jnp.sum(upstream * unit, axis=0, keepdims=True)
-
-
-def accumulate(term, value, when):
-    @pl.when(pl.program_id(0) == 0)
-    def _():
-        term[...] = jnp.zeros_like(term)
-
-    @pl.when(when)
-    def _():
-        term[...] += value
+    return inverse * (scaled - unit * inner)
 
 
 def middle_back_kernel(
-    scalars, middle, own, other, got_own, got_other, own_up, got_up, gain, whole, low, term, scratch
+    scalars, middle, own, other, got_own, got_other, own_up, got_up, gain, whole, low, scratch
 ):
     upstream = gather((own, got_other), (other, got_own), scratch, scalars[0])
-    grad, value = pull(middle[...], upstream, gain[...])
-    grad = grad + either(own_up, got_up)
+    grad = pull(middle[...], upstream, gain[...]) + either(own_up, got_up)
     whole[...] = grad
     low[...] = grad.astype(low.dtype)
-    accumulate(term, value, pl.program_id(0) < pl.num_programs(0) // 2)
 
 
 def input_back_kernel(
-    scalars, rows, own, other, got_own, got_other, grad_middle, gain, out, term, scratch
+    scalars, rows, own, other, got_own, got_other, grad_middle, gain, out, scratch
 ):
     upstream = gather((own, got_other), (other, got_own), scratch, scalars[0])
-    grad, value = pull(rows[...].astype(jnp.float32), upstream, gain[...])
+    grad = pull(rows[...].astype(jnp.float32), upstream, gain[...])
     out[...] = (grad_middle[...] + grad).astype(out.dtype)
-    accumulate(term, value, True)
 
 
 def softmax_of(query, keys, allowed):
@@ -535,39 +554,44 @@
     slot = lax.broadcasted_iota(jnp.int32, (frames, positions), 1)
     live = ((frame_valid[:, None] > 0) & (slot <= last_position[:, None]))[:, :, None]
 
-    gains = jnp.stack([gain_attn, gain_ffn], axis=2)
-    gains = jnp.pad(gains, ((0, 0), (0, 0), (0, LANES - 2)))
-    first = [
-        jnp.concatenate([pick(part, spot ^ k) for part in (weight_qkv, weight_out, gains)], axis=1)
-        for k in range(spots)
-    ]
-    *first, rows_in = tie(*first, frames_in)
-    first = [hop(piece, k, spots) for k, piece in enumerate(first)]
-    own_rows = rows_to_spots(rows_in)
-    gates = [pick(weight_ffn, spot ^ k)[:, :hidden_units] for k in range(spots)]
+    gains = jnp.pad(jnp.stack([gain_attn, gain_ffn], axis=2), ((0, 0), (0, 0), (0, LANES - 2)))
+    parts = (weight_qkv, weight_out, gains, weight_ffn)
+    widths = (3 * depth, depth, LANES, hidden_units)
+    first = collect(parts, widths, jnp.concatenate([by_spot[:1], by_spot[2:]]))
+    first = list(collect(parts, widths, by_spot[:2])) + [hop(p, k + 1, spots) for k, p in enumerate(first)]
+    upstream = jnp.where(live, grad_out, jnp.zeros_like(grad_out))
+    rows_in = jnp.concatenate([frames_in.swapaxes(0, 1), upstream.swapaxes(0, 1)], axis=1)
+    own_rows = swap(rows_in, positions)
     ups = [pick(weight_ffn, spot ^ k)[:, hidden_units:] for k in range(spots)]
-    tied = tie(own_rows, *first, *gates)
-    own_rows, first, gates = tied[0], tied[1 : spots + 1], list(tied[spots + 1 :])
-    gates[:near] = [hop(piece, k, spots) for k, piece in enumerate(gates[:near])]
-    got_rows = trade(own_rows)
+    third = [pick(weight_down, down_index ^ k) for k in range(spots)]
+    tied = tie(*first, *ups, *third)
+    first, ups, third = tied[:spots], tied[spots : 2 * spots], tied[2 * spots :]
+    ups = [hop(piece, k, spots) for k, piece in enumerate(ups)]
+    own_rows, own_up = (
+        own_rows[:, part * frames : (part + 1) * frames].reshape(-1, depth) for part in range(2)
+    )
+    got_rows, got_up = trade(own_rows), trade(own_up)
 
     own_count = own_rows.shape[0]
     count = own_count * 2
     step = own_count // 2
-    qkv_own, qkv_sent, full_out, gains = split_columns(
-        [[piece] for piece in first], heads, by_spot, ((3 * depth, depth), (4 * depth, LANES))
-    )
+    pieces = [[piece] for piece in first]
+    (qkv_sent,) = split_columns(pieces, heads, by_spot, (True,), 3 * depth)
     qkv_other = trade(qkv_sent)
+    whole = 4 * depth + LANES
+    qkv_own, full_out, gains = split_columns(
+        pieces, heads, by_spot, (False,), whole, ((3 * depth, depth), (4 * depth, LANES))
+    )
     gains = gains[:, :2]
     pair = [part.reshape(spots, slice_rows, 2) for part in (gains, trade(gains))]
     even, odd = (jnp.where(half == h, *pair) for h in range(2))
     gains = jnp.stack([even, odd], axis=1).reshape(depth, 2).T.astype(f32)
     gain_one, gain_two = gains[:1], gains[1:]
-    qkv_other, *gates[:near] = tie(qkv_other, *gates[:near])
     mine, theirs = halves_rows(step, own_rows)
     straight = lambda r, *s: (r, 0)
     crossed = lambda r, *s: ((r + 2) % 4, 0)
     top = lambda r, *s: (0, 0)
+    lower = lambda blocks, where: lambda *r: (where(*r)[0] + blocks, 0)
     rows = [(own_rows, (step, depth), mine), (got_rows, (step, depth), theirs)]
     split_rows = [((count, depth // 2), bf16, (step, depth // 2), straight)] * 2
     low_scratch, scratch = pltpu.VMEM((step, depth), bf16), pltpu.VMEM((step, depth), f32)
@@ -575,81 +599,64 @@
         norm_kernel, "norm", (4,), rows + [(gain_one, (1, depth), top)], split_rows, by_spot, [low_scratch]
     )
     qkv_rows = (plain(one_own, qkv_own) + plain(one_other, qkv_other)).astype(bf16)
-    tied = tie(*gates, *ups[:near])
-    gates, ups[:near] = list(tied[:spots]), tied[spots:]
-    ups[:near] = [hop(piece, k, spots) for k, piece in enumerate(ups[:near])]
-    gates[near] = hop(gates[near], near, spots)
+    qkv_rows, *ups[:near] = tie(qkv_rows, *ups[:near])
     qkv = swap(qkv_rows, positions)
     mixed = over_frames(attend_kernel, depth // 2, qkv)
-    mixed, *ups[:near], gates[near] = tie(mixed, *ups[:near], gates[near])
-    ups[near], gates[near] = tie(ups[near], gates[near])
-    ups[near] = hop(ups[near], near, spots)
-    third = [pick(weight_down, down_index ^ k) for k in range(spots)]
-    gates[near], *third = tie(gates[near], *third)
     third = [lax.ppermute(p, PLANE, down_pairs[k]) for k, p in enumerate(third)]
+    mixed, *third[:early] = tie(mixed, *third[:early])
     mixed = swap(mixed, positions).reshape(count, -1)
-    upstream = jnp.where(live, grad_out, jnp.zeros_like(grad_out))
-    mixed, upstream = tie(mixed, upstream)
-    own_up = rows_to_spots(upstream)
     branch = plain(mixed, full_out)
-    branch, ups[near] = tie(branch, ups[near])
+    got_branch = trade(branch)
     middle, two_own, two_other = call(
         middle_kernel,
         "middle",
         (4,),
         rows
-        + [(branch, (step, depth), straight), (trade(branch), (step, depth), crossed)]
+        + [(branch, (step, depth), straight), (got_branch, (step, depth), crossed)]
         + [(gain_two, (1, depth), top)],
         [((count, depth), f32, (step, depth), straight)] + split_rows,
         by_spot,
         [low_scratch],
     )
 
-    ffn_own, ffn_sent = split_columns(list(zip(gates, ups)), units, by_spot)
+    gate_run = tuple(start + whole for start in units[0][0])
+    up_run = tuple(start - hidden_units for start in units[0][1])
+    ffn_own, ffn_sent = split_columns(
+        list(zip(first, ups)), ([gate_run, up_run], units[1]), by_spot
+    )
     ffn_other = trade(ffn_sent)
-    ffn_other, *third[:early] = tie(ffn_other, *third[:early])
     gate_up = plain(two_own, ffn_own) + plain(two_other, ffn_other)
-    gate_up, *third = tie(gate_up, *third)
+    gate_up, *third[early:] = tie(gate_up, *third[early:])
     width = gate_up.shape[1] // 2
     gate, upward = gate_up[:, :width], gate_up[:, width:]
     gate_sig = jax.nn.sigmoid(gate)
     hidden = (gate * gate_sig * upward).astype(bf16)
-    got_up = trade(own_up)
     upstream = jnp.concatenate([own_up, got_up])
     down_grad = over_rows(hidden, upstream).astype(bf16).reshape(spots, -1, depth)
     down_sent = [pick(down_grad, spot ^ k) for k in range(spots)]
-    hidden, *down_sent = tie(hidden, *down_sent)
     down_back = [[(b, a) for a, b in pairs] for pairs in down_pairs]
-    for k in range(0, spots, 2):
-        down_sent[k] = lax.ppermute(down_sent[k], PLANE, down_back[k])
-    down_sent = list(tie(*down_sent))
-    for k in range(1, spots, 2):
-        down_sent[k] = lax.ppermute(down_sent[k], PLANE, down_back[k])
-    full_down = jnp.zeros((spots,) + third[0].shape, bf16)
-    for k, piece in enumerate(third):
-        full_down = lax.dynamic_update_index_in_dim(full_down, piece, spot ^ k, 0)
+    down_sent = [lax.ppermute(p, PLANE, pairs) for p, pairs in zip(down_sent, down_back)]
+    full_down = place([[(piece, 0)] for piece in third], by_spot, *weight_down.shape[1:], dtype=bf16)
     full_down = full_down.reshape(-1, depth)
 
     grad_hidden = by_columns(upstream, full_down)
     grad_upward = grad_hidden * gate * gate_sig
     grad_gate = grad_hidden * upward * gate_sig * (1.0 + gate * (1.0 - gate_sig))
     grad_gate_up = jnp.concatenate([grad_gate, grad_upward], axis=-1).astype(bf16)
-    back_own = by_columns(grad_gate_up, ffn_own)
-    back_other = by_columns(grad_gate_up, ffn_other)
-    got_own, got_other = trade(back_own), trade(back_other)
-    got_other, grad_gate_up, *down_sent[::2] = tie(got_other, grad_gate_up, *down_sent[::2])
+    back = jnp.concatenate([by_columns(grad_gate_up, ffn_own), by_columns(grad_gate_up, ffn_other)])
+    back, *down_sent[::2] = tie(back, *down_sent[::2])
+    got_back, grad_gate_up = tie(trade(back), grad_gate_up)
     wide, narrow = (step, depth), (step, depth // 2)
-    grad_middle, grad_branch, term_two = call(
+    grad_middle, grad_branch = call(
         middle_back_kernel,
         "middle_back",
         (4,),
-        [(middle, wide, straight), (back_own, narrow, straight), (back_other, narrow, straight)]
-        + [(got_own, narrow, crossed), (got_other, narrow, crossed)]
+        [(middle, wide, straight), (back, narrow, straight), (back, narrow, lower(4, straight))]
+        + [(got_back, narrow, crossed), (got_back, narrow, lower(4, crossed))]
         + [(own_up, wide, mine), (got_up, wide, theirs), (gain_two, (1, depth), top)],
         [
             ((count, depth), f32, wide, straight),
             ((count, depth), bf16, wide, straight),
-            ((1, depth), f32, (1, depth), top),
         ],
         by_spot,
         [scratch],
@@ -661,24 +668,22 @@
     grad_mixed_frames = swap(grad_mixed, positions)
     ffn_grad_own = cut(over_rows(two_own, grad_gate_up).astype(bf16))
     ffn_grad_got = cut(trade(over_rows(two_other, grad_gate_up).astype(bf16)))
-    tied = tie(*down_sent, *ffn_grad_own)
-    down_sent, ffn_grad_own = tied[:spots], list(tied[spots:])
     ffn_grad_own = [hop(piece, k, spots) for k, piece in enumerate(ffn_grad_own)]
-    grad_mixed_frames, *ffn_grad_own[:near] = tie(grad_mixed_frames, *ffn_grad_own[:near])
     grad_qkv = over_frames(attend_back_kernel, 3 * depth // 2, qkv, grad_mixed_frames)
     late = [
         jnp.concatenate(pair, axis=1)
         for pair in zip(ffn_grad_got, cut(over_rows(mixed, grad_branch).astype(bf16)))
     ]
-    grad_qkv, ffn_grad_own[near], *late = tie(grad_qkv, ffn_grad_own[near], *late)
-    late[:near] = [hop(piece, k, spots) for k, piece in enumerate(late[:near])]
+    grad_qkv, *ffn_grad_own[:near] = tie(grad_qkv, *ffn_grad_own[:near])
+    late = [hop(piece, k, spots) for k, piece in enumerate(late)]
     result = plain(hidden, full_down)
     result = (middle[:own_count] + result[:own_count] + trade(result[own_count:])).astype(bf16)
     sum_down = place([[(piece, 0)] for piece in down_sent], by_slice, *weight_down.shape[1:])
     grad_qkv_rows = swap(grad_qkv, positions).reshape(count, -1)
-    grad_qkv_rows, result, sum_down, *late = tie(grad_qkv_rows, result, sum_down, *late)
-    late[near] = hop(late[near], near, spots)
-    result = rows_from_spots(result)
+    grad_qkv_rows, result, sum_down, ffn_grad_own[near], *late[:near] = tie(
+        grad_qkv_rows, result, sum_down, ffn_grad_own[near], *late[:near]
+    )
+    result = rows_from_spots(result, positions)
     qkv_grad_got = trade(over_rows(one_other, grad_qkv_rows).astype(bf16))
     qkv_grad_own = over_rows(one_own, grad_qkv_rows).astype(bf16)
     qkv_sent = [jnp.concatenate(pair) for pair in zip(cut(qkv_grad_own), cut(qkv_grad_got))]
@@ -686,41 +691,47 @@
     qkv_sent = [hop(piece, k, spots) for k, piece in enumerate(qkv_sent)]
     back_own = by_columns(grad_qkv_rows, qkv_own)
     back_other = by_columns(grad_qkv_rows, qkv_other)
-    got_own, got_other = trade(back_own[own_count:]), trade(back_other[own_count:])
-    got_other, result, late[near] = tie(got_other, result, late[near])
-    grad_rows, term_one = call(
+    back_own, back_other, result, late[near], *qkv_sent[:near] = tie(
+        back_own, back_other, result, late[near], *qkv_sent[:near]
+    )
+    got_back = trade(jnp.concatenate([back_own[own_count:], back_other[own_count:]]))
+    (grad_rows,) = call(
         input_back_kernel,
         "input_back",
         (2,),
         [(own_rows, wide, straight), (back_own, narrow, straight), (back_other, narrow, straight)]
-        + [(got_own, narrow, straight), (got_other, narrow, straight)]
+        + [(got_back, narrow, straight), (got_back, narrow, lower(2, straight))]
         + [(grad_middle, wide, straight), (gain_one, (1, depth), top)],
-        [((own_count, depth), bf16, wide, straight), ((1, depth), f32, (1, depth), top)],
+        [((own_count, depth), bf16, wide, straight)],
         by_spot,
         [scratch],
     )
-    grad_rows, *qkv_sent[:near] = tie(grad_rows, *qkv_sent[:near])
-    grad_input = rows_from_spots(grad_rows)
-    grad_input, term_one = tie(grad_input, term_one)
+    grad_input = rows_from_spots(grad_rows, positions)
     output = jnp.where(live, result, jnp.zeros_like(result))
 
-    sum_ffn = place(
+    sum_ffn, term_ffn = place(
         [[(own, 0), (got, 0)] for own, got in zip(ffn_grad_own, late)],
         by_spot,
         slice_rows,
         2 * hidden_units,
         units,
+        weight=weight_ffn,
     )
     sum_out = place([[(piece, 0)] for piece in late], by_spot, slice_rows, depth, skip=hidden_units)
-    sum_qkv = place(
-        [[(piece, 0), (piece, slice_rows)] for piece in qkv_sent], by_spot, slice_rows, 3 * depth, heads
-    )
-    terms = jnp.stack([term_one, term_two]).reshape(2, plane, depth // plane)
-    terms = lax.all_to_all(
-        jnp.transpose(terms, (1, 0, 2)), PLANE, split_axis=0, concat_axis=0, tiled=True
-    )
-    terms = jnp.sum(terms.reshape(spots, 2, 2, depth // plane), axis=1)
-    return (output, grad_input, sum_qkv, sum_out, sum_ffn, sum_down, terms[:, 0], terms[:, 1])
+    qkv_sent[near], sum_ffn, sum_out = tie(qkv_sent[near], sum_ffn, sum_out)
+    sum_qkv, term_attn = place(
+        [[(piece, 0), (piece, slice_rows)] for piece in qkv_sent],
+        by_spot,
+        slice_rows,
+        3 * depth,
+        heads,
+        weight=weight_qkv,
+    )
+    gain_terms = [
+        term.reshape(spots, slice_rows) / gain.astype(f32)
+        for term, gain in ((term_attn, gain_attn), (term_ffn, gain_ffn))
+    ]
+    return (output, grad_input, sum_qkv, sum_out, sum_ffn, sum_down, *gain_terms)
 
 
 def solution(mesh):

time: 524 us -> 490 us (0.935)
  waiting for transfers between devices: 223 us -> 191 us
  local copies, waits for them, and re-layouts: 59.9 us -> 41.1 us
  Pallas kernels: 58.2 us -> 73.3 us
  matrix products: 51.6 us -> 57.7 us
    all_to_all x5 -> x0, starting transfers between devices: 27.9 us -> none  [the longest x2 13.5 us: rows_to_spots(): lax.all_to_all(values, ROWS, split_axis=1, concat_axis=0, tiled=True)]
    all_to_all x4 -> x7, starting transfers between devices: 20.2 us -> 47.8 us  [swap(): lax.all_to_all(values.reshape(blocks, -1, values.shape[-1]), ROWS, split_...]
    all_to_all x5 -> x0, waiting for transfers between devices: 14.9 us -> none  [the longest x2 12.7 us: rows_from_spots(): lax.all_to_all(values[:, None], ROWS, split_axis=0, concat_axis=1, tiled=...]
    pallas_call x10 -> x14, Pallas kernels: 45.6 us -> 59.8 us  [call(): pl.pallas_call(kernel, grid_spec=pltpu.PrefetchScalarGridSpec(num_scalar_...]
    ppermute x4, waiting for transfers between devices: 12.6 us -> 1.85 us  [spots_plan(): third = [lax.ppermute(p, PLANE, down_pairs[k]) for k, p in enumerate(third)]]
    ppermute x4, waiting for transfers between devices: 21.1 us -> 12.9 us  [spots_plan(): lax.ppermute(p, PLANE, pairs)]
    unnamed x111 -> x119, local copies, waits for them, and re-layouts: 24.5 us -> 18.8 us
    ppermute x18 -> x15, starting transfers between devices: 24.7 us -> 20.5 us  [hop(): lax.ppermute(value, 'spot', [(i, i ^ k) for i in range(spots)])]
  transfers between devices with their start and end apart: 48 -> 41, of which waited for: 23 -> 19; matrix products, arithmetic and copies ran while one was open for 18% -> 17% of each run, Pallas kernels for 9% -> 14%
where the time goes in v3:
time: 490 us; the launch traced here: 481 us
  waiting for transfers between devices  191 us (39%)
  starting transfers between devices  101 us (21%)
  Pallas kernels  73.3 us (15%)
  matrix products  57.7 us (12%)
  local copies, waits for them, and re-layouts  41.1 us (8%)
  other arithmetic  15.2 us (3%)
    ppermute x15, waiting for transfers between devices, hop(): lax.ppermute(value, 'spot', [(i, i ^ k) for i in range(spots)])  138 us
    pallas_call x14, Pallas kernels, call(): pl.pallas_call(kernel, grid_spec=pltpu.PrefetchScalarGridSpec(num_scalar_...  59.8 us
    all_to_all x7, starting transfers between devices, swap(): lax.all_to_all(values.reshape(blocks, -1, values.shape[-1]), ROWS, split_...  47.8 us
    all_to_all x7, waiting for transfers between devices, swap(): lax.all_to_all(values.reshape(blocks, -1, values.shape[-1]), ROWS, split_...  34.7 us
    dot_general x6, matrix products, by_columns(): lax.dot_general(left, right, (((1,), (1,)), ((), ())), preferred_element_...  20.6 us
    ppermute x15, starting transfers between devices, hop(): lax.ppermute(value, 'spot', [(i, i ^ k) for i in range(spots)])  20.5 us
    dot_general x6, matrix products, plain(): lax.dot_general(left, right, (((1,), (0,)), ((), ())), preferred_element_...  19.2 us
    unnamed x119, local copies, waits for them, and re-layouts  18.8 us
  transfers between devices with their start and end apart: 41, of which 19 were waited for; matrix products, arithmetic and copies ran while one was open for 17% of the time, Pallas kernels for 14%

profile of v3, /device:TPU:0, one launch (start us, length us, event | category | flops | bytes accessed | tf_op | source)
XLA Modules:
  0.0 480.8 jit_solution(13104067947533493562)
XLA Ops:
  2.9 7.0 %collect.3 = (bf16[128,7040]{1,0:T(8,128)(2,1)}, bf16[128,7040]{1,0:T(8,128)(2,1)}, bf16[128,7040]{1,0:T(8,128)(2,1)}) custom-call(s32[4]{0:T(128)S(1)} %pad_add_fusion.1.scalars, bf16[4,128,3072]{2,1,0:T(8,128)(2,1)} %refs_8_.3, bf16[4,128,1024]{2,1,0:T(8,128)(2,1)S(1)} %copy-done.5, bf16[4,128,128]{2,1,0:T(8,128)(2,1)S(1)} %pad.4.refs_2_, ...), custom_call_target="tpu_custom_call" | custom-call | bytes 1261568 | tf_op jit(solution)/shard_map/collect/pallas_call | solution.py:228
  16.7 7.4 %all-to-all-start = ((bf16[16,32,1024]{2,1,0:T(8,128)(2,1)}), bf16[16,32,1024]{2,1,0:T(8,128)(2,1)}, u32[]{:S(2)}, u32[]{:S(2)}) async-start(bf16[16,32,1024]{2,1,0:T(8,128)(2,1)} %pad_maximum_fusion.2), calls=%async_computation | async-start | bytes 2097152 | tf_op jit(solution)/shard_map/all_to_all | solution.py:207
  38.0 23.7 %collective-permute-done.1.refs_1_.refs_2_ = bf16[128,7040]{1,0:T(8,128)(2,1)} collective-permute-done((bf16[128,7040]{1,0:T(8,128)(2,1)}, bf16[128,7040]{1,0:T(8,128)(2,1)}, u32[]{:S(2)}, u32[]{:S(2)}) %collective-permute-start.1) | collective-permute-done | bytes 1802272 | tf_op jit(solution)/shard_map/ppermute | solution.py:199
  61.7 41.4 %collective-permute-done.2.refs_2_.refs_4_ = bf16[128,7040]{1,0:T(8,128)(2,1)} collective-permute-done((bf16[128,7040]{1,0:T(8,128)(2,1)}, bf16[128,7040]{1,0:T(8,128)(2,1)}, u32[]{:S(2)}, u32[]{:S(2)}) %collective-permute-start.2) | collective-permute-done | bytes 1802272 | tf_op jit(solution)/shard_map/ppermute | solution.py:199
  123.9 6.3 %collective-permute-done.6.refs_3_ = bf16[128,2816]{1,0:T(8,128)(2,1)} collective-permute-done((bf16[128,2816]{1,0:T(8,128)(2,1)}, bf16[128,2816]{1,0:T(8,128)(2,1)}, u32[]{:S(2)}, u32[]{:S(2)}) %collective-permute-start.6) | collective-permute-done | bytes 720928 | tf_op jit(solution)/shard_map/ppermute | solution.py:199
  130.3 7.1 %all-to-all-start.1 = ((bf16[16,32,1536]{2,1,0:T(8,128)(2,1)}), bf16[16,32,1536]{2,1,0:T(8,128)(2,1)S(1)}, u32[]{:S(2)}, u32[]{:S(2)}) async-start(bf16[16,32,1536]{2,1,0:T(8,128)(2,1)} %bitcast.155), calls=%async_computation.1 | async-start | bytes 3145728 | tf_op jit(solution)/shard_map/all_to_all | solution.py:207
  137.4 6.8 %collective-permute-start.8 = (bf16[352,1024]{1,0:T(8,128)(2,1)}, bf16[352,1024]{1,0:T(8,128)(2,1)}, u32[]{:S(2)}, u32[]{:S(2)}) collective-permute-start(bf16[352,1024]{1,0:T(8,128)(2,1)} %get-tuple-element.100), channel_id=1, source_target_pairs={{0,0},{4,8},{8,16},{12,24},{16,4},{20,12},{24,20},{28,28},{1,1},{5... | collective-permute-start | bytes 2162696 | tf_op jit(solution)/shard_map/ppermute | solution.py:605
  145.9 26.0 %all-to-all-done.1.qkv_ref = bf16[16,32,1536]{2,1,0:T(8,128)(2,1)S(1)} async-done(((bf16[16,32,1536]{2,1,0:T(8,128)(2,1)}), bf16[16,32,1536]{2,1,0:T(8,128)(2,1)S(1)}, u32[]{:S(2)}, u32[]{:S(2)}) %all-to-all-start.1) | async-done | bytes 1572896 | tf_op jit(solution)/shard_map/all_to_all | solution.py:207
  176.0 8.0 %all-to-all-start.2 = ((bf16[16,32,512]{2,1,0:T(8,128)(2,1)}), bf16[16,32,512]{2,1,0:T(8,128)(2,1)}, u32[]{:S(2)}, u32[]{:S(2)}) async-start(bf16[16,32,512]{2,1,0:T(8,128)(2,1)} %copy-done.16), calls=%async_computation.2 | async-start | bytes 1048576 | tf_op jit(solution)/shard_map/all_to_all | solution.py:207
  188.1 5.5 %split_columns.5 = (bf16[4,128,2816]{2,1,0:T(8,128)(2,1)}, bf16[4,128,2816]{2,1,0:T(8,128)(2,1)}) custom-call(s32[5]{0:T(128)S(1)} %stack.55.scalars, bf16[128,7040]{1,0:T(8,128)(2,1)S(1)} %collect.2.refs_0_, bf16[128,2816]{1,0:T(8,128)(2,1)S(1)} %copy-done.8, bf16[128,7040]{1,0:T(8,128)(2,1)} %collective-permute-done.1.refs_1_.refs_2_, ...), custom_call_target="tpu_custom_call" | custom-call | bytes 1261568 | tf_op jit(solution)/shard_map/split_columns/pallas_call | solution.py:228
  200.8 4.2 collective-permute-start.14
  209.7 4.0 middle.1
  213.7 4.3 fusion.14
  218.0 4.3 convolution_add_fusion
  226.3 6.7 %multiply_convert_fusion.2 = (bf16[512,1408]{1,0:T(8,128)(2,1)S(1)}, bf16[512,1408]{1,0:T(8,128)(2,1)S(1)}, bf16[512,1408]{1,0:T(8,128)(2,1)S(1)}) fusion(f32[512,2816]{1,0:T(8,128)} %convolution_add_fusion, bf16[1408,1024]{1,0:T(8,128)(2,1)S(1)} %bitcast.146, bf16[256,1024]{1,0:T(8,128)(2,1)S(1)} %collective-permute-done.11.got_up, ...), kind=kOutput, calls=%fused_computation.11 | convolution fusion | flops 1490026496 | bytes 14024704 | tf_op jit(solution)/shard_map/dot_general | solution.py:183
  237.6 5.1 %collective-permute-start.17 = (bf16[352,1024]{1,0:T(8,128)(2,1)S(1)}, bf16[352,1024]{1,0:T(8,128)(2,1)S(1)}, u32[]{:S(2)}, u32[]{:S(2)}) collective-permute-start(bf16[352,1024]{1,0:T(8,128)(2,1)S(1)} %get-tuple-element.187), channel_id=1, source_target_pairs={{16,0},{24,4},{0,8},{8,12},{20,16},{28,20},{4,24},{12,28},{17,1},{... | collective-permute-start | bytes 2162696 | tf_op jit(solution)/shard_map/ppermute | solution.py:638
  248.8 7.3 %collective-permute-done.17.refs_2_ = bf16[352,1024]{1,0:T(8,128)(2,1)S(1)} collective-permute-done((bf16[352,1024]{1,0:T(8,128)(2,1)S(1)}, bf16[352,1024]{1,0:T(8,128)(2,1)S(1)}, u32[]{:S(2)}, u32[]{:S(2)}) %collective-permute-start.17) | collective-permute-done | bytes 720928 | tf_op jit(solution)/shard_map/ppermute | solution.py:638
  256.1 4.8 collective-permute-start.18
  268.5 4.8 middle_back.1
  276.3 5.4 %collective-permute-done.20.refs_3_ = bf16[352,1024]{1,0:T(8,128)(2,1)S(1)} collective-permute-done((bf16[352,1024]{1,0:T(8,128)(2,1)}, bf16[352,1024]{1,0:T(8,128)(2,1)S(1)}, u32[]{:S(2)}, u32[]{:S(2)}) %collective-permute-start.20) | collective-permute-done | bytes 720928 | tf_op jit(solution)/shard_map/ppermute | solution.py:638
  283.7 7.1 %all-to-all-start.3 = ((bf16[16,32,512]{2,1,0:T(8,128)(2,1)}), bf16[16,32,512]{2,1,0:T(8,128)(2,1)}, u32[]{:S(2)}, u32[]{:S(2)}) async-start(bf16[16,32,512]{2,1,0:T(8,128)(2,1)} %bitcast.162), calls=%async_computation.3 | async-start | bytes 1048576 | tf_op jit(solution)/shard_map/all_to_all | solution.py:207
  299.2 6.6 %all-to-all-done.3.grad_ref = bf16[16,32,512]{2,1,0:T(8,128)(2,1)} async-done(((bf16[16,32,512]{2,1,0:T(8,128)(2,1)}), bf16[16,32,512]{2,1,0:T(8,128)(2,1)}, u32[]{:S(2)}, u32[]{:S(2)}) %all-to-all-start.3) | async-done | bytes 524320 | tf_op jit(solution)/shard_map/all_to_all | solution.py:207
  305.8 10.3 %attend_back_kernel.1 = bf16[16,32,1536]{2,1,0:T(8,128)(2,1)S(1)} custom-call(bf16[16,32,1536]{2,1,0:T(8,128)(2,1)S(1)} %all-to-all-done.1.qkv_ref, bf16[16,32,512]{2,1,0:T(8,128)(2,1)} %all-to-all-done.3.grad_ref), custom_call_target="tpu_custom_call" | custom-call | flops 536870912 | bytes 3145728 | tf_op jit(solution)/shard_map/attend_back_kernel/pallas_call | solution.py:509
  317.3 5.6 %all-to-all-start.4 = ((bf16[16,32,1536]{2,1,0:T(8,128)(2,1)}), bf16[16,32,1536]{2,1,0:T(8,128)(2,1)}, u32[]{:S(2)}, u32[]{:S(2)}) async-start(bf16[16,32,1536]{2,1,0:T(8,128)(2,1)} %copy-done.3), calls=%async_computation.4 | async-start | bytes 3145728 | tf_op jit(solution)/shard_map/all_to_all | solution.py:207
  346.5 39.8 %collective-permute-done.24.refs_6_ = bf16[128,2816]{1,0:T(8,128)(2,1)S(1)} collective-permute-done((bf16[128,2816]{1,0:T(8,128)(2,1)}, bf16[128,2816]{1,0:T(8,128)(2,1)S(1)}, u32[]{:S(2)}, u32[]{:S(2)}) %collective-permute-start.24) | collective-permute-done | bytes 720928 | tf_op jit(solution)/shard_map/ppermute | solution.py:199
  393.7 6.0 %all-to-all-start.5 = ((bf16[16,16,1024]{2,1,0:T(8,128)(2,1)}), bf16[16,16,1024]{2,1,0:T(8,128)(2,1)}, u32[]{:S(2)}, u32[]{:S(2)}) async-start(bf16[16,16,1024]{2,1,0:T(8,128)(2,1)} %bitcast.159), calls=%async_computation.5 | async-start | bytes 1048576 | tf_op jit(solution)/shard_map/all_to_all | solution.py:207
  417.3 6.1 %collective-permute-done.29.refs_7_.refs_3_ = bf16[128,3840]{1,0:T(8,128)(2,1)} collective-permute-done((bf16[128,3840]{1,0:T(8,128)(2,1)}, bf16[128,3840]{1,0:T(8,128)(2,1)}, u32[]{:S(2)}, u32[]{:S(2)}) %collective-permute-start.29) | collective-permute-done | bytes 983072 | tf_op jit(solution)/shard_map/ppermute | solution.py:199
  424.4 16.5 %collective-permute-done.30.refs_2_.refs_3_ = bf16[256,1536]{1,0:T(8,128)(2,1)} collective-permute-done((bf16[256,1536]{1,0:T(8,128)(2,1)}, bf16[256,1536]{1,0:T(8,128)(2,1)}, u32[]{:S(2)}, u32[]{:S(2)}) %collective-permute-start.30) | collective-permute-done | bytes 786464 | tf_op jit(solution)/shard_map/ppermute | solution.py:199
  446.8 6.6 %all-to-all-start.6 = ((bf16[16,16,1024]{2,1,0:T(8,128)(2,1)}), bf16[16,16,1024]{2,1,0:T(8,128)(2,1)}, u32[]{:S(2)}, u32[]{:S(2)}) async-start(bf16[16,16,1024]{2,1,0:T(8,128)(2,1)} %bitcast.148), calls=%async_computation.6 | async-start | bytes 1048576 | tf_op jit(solution)/shard_map/all_to_all | solution.py:207
  455.6 4.0 place.8
  459.6 10.4 %place.7 = (f32[4,128,5632]{2,1,0:T(8,128)}, f32[4,128,1]{2,1,0:T(8,128)S(1)}) custom-call(s32[5]{0:T(128)S(1)} %stack.55.scalars, bf16[128,2816]{1,0:T(8,128)(2,1)S(1)} %copy-done.9, bf16[128,3840]{1,0:T(8,128)(2,1)S(1)} %pad_maximum_fusion.5.refs_1_.refs_0_, bf16[128,2816]{1,0:T(8,128)(2,1)} %collective-permute-done.21.refs_2_, ...), custom_call_target="tpu_custom_call" | custom-call | bytes 1572864 | tf_op jit(solution)/shard_map/place/pallas_call | solution.py:228
  470.1 6.8 %place.9 = (f32[4,128,3072]{2,1,0:T(8,128)}, f32[4,128,1]{2,1,0:T(8,128)S(1)}) custom-call(s32[5]{0:T(128)S(1)} %stack.55.scalars, bf16[256,1536]{1,0:T(8,128)(2,1)S(1)} %pad_maximum_fusion.9.refs_0_.refs_1_, bf16[256,1536]{1,0:T(8,128)(2,1)S(1)} %pad_maximum_fusion.9.refs_0_.refs_1_, bf16[256,1536]{1,0:T(8,128)(2,1)} %collective-permute-done.30.refs_2_.refs_3_, ...), custom_call_target="tpu_custom_call" | custom-call | bytes 1179648 | tf_op jit(solution)/shard_map/place/pallas_call | solution.py:228
  (256 shorter events, 163.1 us)
Async XLA Ops:
  9.9 51.8 %collective-permute-start.1 = (bf16[128,7040]{1,0:T(8,128)(2,1)}, bf16[128,7040]{1,0:T(8,128)(2,1)}, u32[]{:S(2)}, u32[]{:S(2)}) collective-permute-start(bf16[128,7040]{1,0:T(8,128)(2,1)} %get-tuple-element.85), channel_id=1, source_target_pairs={{0,8},{8,0},{16,24},{24,16},{1,9},{9,1},{17,25},{25,17},{2,10},{10... | collective-permute-start | bytes 5406728 | tf_op jit(solution)/shard_map/ppermute | solution.py:199
  12.8 90.2 %collective-permute-start.2 = (bf16[128,7040]{1,0:T(8,128)(2,1)}, bf16[128,7040]{1,0:T(8,128)(2,1)}, u32[]{:S(2)}, u32[]{:S(2)}) collective-permute-start(bf16[128,7040]{1,0:T(8,128)(2,1)} %get-tuple-element.86), channel_id=1, source_target_pairs={{0,16},{8,24},{16,0},{24,8},{1,17},{9,25},{17,1},{25,9},{2,18},{10... | collective-permute-start | bytes 5406728 | tf_op jit(solution)/shard_map/ppermute | solution.py:199
  14.3 88.7 %collective-permute-start.3 = (bf16[128,7040]{1,0:T(8,128)(2,1)}, bf16[128,7040]{1,0:T(8,128)(2,1)}, u32[]{:S(2)}, u32[]{:S(2)}) collective-permute-start(bf16[128,7040]{1,0:T(8,128)(2,1)} %get-tuple-element.87), channel_id=1, source_target_pairs={{0,24},{8,16},{16,8},{24,0},{1,25},{9,17},{17,9},{25,1},{2,26},{10... | collective-permute-start | bytes 5406728 | tf_op jit(solution)/shard_map/ppermute | solution.py:199
  16.7 96.6 %all-to-all-start = ((bf16[16,32,1024]{2,1,0:T(8,128)(2,1)}), bf16[16,32,1024]{2,1,0:T(8,128)(2,1)}, u32[]{:S(2)}, u32[]{:S(2)}) async-start(bf16[16,32,1024]{2,1,0:T(8,128)(2,1)} %pad_maximum_fusion.2), calls=%async_computation | async-start | bytes 2097152 | tf_op jit(solution)/shard_map/all_to_all | solution.py:207
  111.4 18.9 %collective-permute-start.6 = (bf16[128,2816]{1,0:T(8,128)(2,1)}, bf16[128,2816]{1,0:T(8,128)(2,1)}, u32[]{:S(2)}, u32[]{:S(2)}) collective-permute-start(bf16[128,2816]{1,0:T(8,128)(2,1)} %slice.70), channel_id=1, source_target_pairs={{0,8},{8,0},{16,24},{24,16},{1,9},{9,1},{17,25},{25,17},{2,10},{10... | collective-permute-start | bytes 2162696 | tf_op jit(solution)/shard_map/ppermute | solution.py:199
  111.7 18.6 %collective-permute-start.7 = (bf16[128,2816]{1,0:T(8,128)(2,1)}, bf16[128,2816]{1,0:T(8,128)(2,1)}, u32[]{:S(2)}, u32[]{:S(2)}) collective-permute-start(bf16[128,2816]{1,0:T(8,128)(2,1)} %slice.71), channel_id=1, source_target_pairs={{0,16},{8,24},{16,0},{24,8},{1,17},{9,25},{17,1},{25,9},{2,18},{10... | collective-permute-start | bytes 2162696 | tf_op jit(solution)/shard_map/ppermute | solution.py:199
  130.3 41.6 %all-to-all-start.1 = ((bf16[16,32,1536]{2,1,0:T(8,128)(2,1)}), bf16[16,32,1536]{2,1,0:T(8,128)(2,1)S(1)}, u32[]{:S(2)}, u32[]{:S(2)}) async-start(bf16[16,32,1536]{2,1,0:T(8,128)(2,1)} %bitcast.155), calls=%async_computation.1 | async-start | bytes 3145728 | tf_op jit(solution)/shard_map/all_to_all | solution.py:207
  137.4 38.6 %collective-permute-start.8 = (bf16[352,1024]{1,0:T(8,128)(2,1)}, bf16[352,1024]{1,0:T(8,128)(2,1)}, u32[]{:S(2)}, u32[]{:S(2)}) collective-permute-start(bf16[352,1024]{1,0:T(8,128)(2,1)} %get-tuple-element.100), channel_id=1, source_target_pairs={{0,0},{4,8},{8,16},{12,24},{16,4},{20,12},{24,20},{28,28},{1,1},{5... | collective-permute-start | bytes 2162696 | tf_op jit(solution)/shard_map/ppermute | solution.py:605
  144.2 31.8 %collective-permute-start.9 = (bf16[352,1024]{1,0:T(8,128)(2,1)}, bf16[352,1024]{1,0:T(8,128)(2,1)}, u32[]{:S(2)}, u32[]{:S(2)}) collective-permute-start(bf16[352,1024]{1,0:T(8,128)(2,1)} %get-tuple-element.101), channel_id=1, source_target_pairs={{0,8},{4,0},{8,24},{12,16},{16,12},{20,4},{24,28},{28,20},{1,9},{5... | collective-permute-start | bytes 2162696 | tf_op jit(solution)/shard_map/ppermute | solution.py:605
  144.2 42.7 %collective-permute-start.12 = (bf16[128,2816]{1,0:T(8,128)(2,1)}, bf16[128,2816]{1,0:T(8,128)(2,1)}, u32[]{:S(2)}, u32[]{:S(2)}) collective-permute-start(bf16[128,2816]{1,0:T(8,128)(2,1)} %slice.72), channel_id=1, source_target_pairs={{0,24},{8,16},{16,8},{24,0},{1,25},{9,17},{17,9},{25,1},{2,26},{10... | collective-permute-start | bytes 2162696 | tf_op jit(solution)/shard_map/ppermute | solution.py:199
  176.0 22.6 %all-to-all-start.2 = ((bf16[16,32,512]{2,1,0:T(8,128)(2,1)}), bf16[16,32,512]{2,1,0:T(8,128)(2,1)}, u32[]{:S(2)}, u32[]{:S(2)}) async-start(bf16[16,32,512]{2,1,0:T(8,128)(2,1)} %copy-done.16), calls=%async_computation.2 | async-start | bytes 1048576 | tf_op jit(solution)/shard_map/all_to_all | solution.py:207
  193.5 20.1 %collective-permute-start.13 = (bf16[512,2816]{1,0:T(8,128)(2,1)}, bf16[512,2816]{1,0:T(8,128)(2,1)}, u32[]{:S(2)}, u32[]{:S(2)}) collective-permute-start(bf16[512,2816]{1,0:T(8,128)(2,1)} %bitcast.166), channel_id=1, source_target_pairs={{0,4},{4,0},{1,5},{5,1},{2,6},{6,2},{3,7},{7,3},{8,12},{12,8},{9,1... | collective-permute-start | bytes 8650760 | tf_op jit(solution)/shard_map/ppermute | solution.py:203
  200.8 21.5 %collective-permute-start.14 = (bf16[352,1024]{1,0:T(8,128)(2,1)}, bf16[352,1024]{1,0:T(8,128)(2,1)S(1)}, u32[]{:S(2)}, u32[]{:S(2)}) collective-permute-start(bf16[352,1024]{1,0:T(8,128)(2,1)} %get-tuple-element.115), channel_id=1, source_target_pairs={{0,16},{4,24},{8,0},{12,8},{16,20},{20,28},{24,4},{28,12},{1,17},{... | collective-permute-start | bytes 2162696 | tf_op jit(solution)/shard_map/ppermute | solution.py:605
  205.0 19.1 %collective-permute-start.15 = (bf16[352,1024]{1,0:T(8,128)(2,1)}, bf16[352,1024]{1,0:T(8,128)(2,1)S(1)}, u32[]{:S(2)}, u32[]{:S(2)}) collective-permute-start(bf16[352,1024]{1,0:T(8,128)(2,1)} %get-tuple-element.116), channel_id=1, source_target_pairs={{0,24},{4,16},{8,8},{12,0},{16,28},{20,20},{24,12},{28,4},{1,25},{... | collective-permute-start | bytes 2162696 | tf_op jit(solution)/shard_map/ppermute | solution.py:605
  207.1 19.2 %collective-permute-start.11 = (bf16[256,1024]{1,0:T(8,128)(2,1)}, bf16[256,1024]{1,0:T(8,128)(2,1)S(1)}, u32[]{:S(2)}, u32[]{:S(2)}) collective-permute-start(bf16[256,1024]{1,0:T(8,128)(2,1)} %bitcast.25.own_up), channel_id=1, source_target_pairs={{0,4},{4,0},{1,5},{5,1},{2,6},{6,2},{3,7},{7,3},{8,12},{12,8},{9,1... | collective-permute-start | bytes 1572872 | tf_op jit(solution)/shard_map/ppermute | solution.py:203
  237.6 18.5 %collective-permute-start.17 = (bf16[352,1024]{1,0:T(8,128)(2,1)S(1)}, bf16[352,1024]{1,0:T(8,128)(2,1)S(1)}, u32[]{:S(2)}, u32[]{:S(2)}) collective-permute-start(bf16[352,1024]{1,0:T(8,128)(2,1)S(1)} %get-tuple-element.187), channel_id=1, source_target_pairs={{16,0},{24,4},{0,8},{8,12},{20,16},{28,20},{4,24},{12,28},{17,1},{... | collective-permute-start | bytes 2162696 | tf_op jit(solution)/shard_map/ppermute | solution.py:638
  260.9 20.8 %collective-permute-start.20 = (bf16[352,1024]{1,0:T(8,128)(2,1)}, bf16[352,1024]{1,0:T(8,128)(2,1)S(1)}, u32[]{:S(2)}, u32[]{:S(2)}) collective-permute-start(bf16[352,1024]{1,0:T(8,128)(2,1)} %get-tuple-element.185), channel_id=1, source_target_pairs={{24,0},{16,4},{8,8},{0,12},{28,16},{20,20},{12,24},{4,28},{25,1},{... | collective-permute-start | bytes 2162696 | tf_op jit(solution)/shard_map/ppermute | solution.py:638
  264.7 18.1 %collective-permute-start.19 = (bf16[352,1024]{1,0:T(8,128)(2,1)}, bf16[352,1024]{1,0:T(8,128)(2,1)S(1)}, u32[]{:S(2)}, u32[]{:S(2)}) collective-permute-start(bf16[352,1024]{1,0:T(8,128)(2,1)} %get-tuple-element.186), channel_id=1, source_target_pairs={{8,0},{0,4},{24,8},{16,12},{12,16},{4,20},{28,24},{20,28},{9,1},{1... | collective-permute-start | bytes 2162696 | tf_op jit(solution)/shard_map/ppermute | solution.py:638
  268.5 62.7 %collective-permute-start.25 = (bf16[512,2816]{1,0:T(8,128)(2,1)}, bf16[512,2816]{1,0:T(8,128)(2,1)}, u32[]{:S(2)}, u32[]{:S(2)}) collective-permute-start(bf16[512,2816]{1,0:T(8,128)(2,1)} %convolution_convert_fusion), channel_id=1, source_target_pairs={{0,4},{4,0},{1,5},{5,1},{2,6},{6,2},{3,7},{7,3},{8,12},{12,8},{9,1... | collective-permute-start | bytes 8650760 | tf_op jit(solution)/shard_map/ppermute | solution.py:203
  283.7 22.2 %all-to-all-start.3 = ((bf16[16,32,512]{2,1,0:T(8,128)(2,1)}), bf16[16,32,512]{2,1,0:T(8,128)(2,1)}, u32[]{:S(2)}, u32[]{:S(2)}) async-start(bf16[16,32,512]{2,1,0:T(8,128)(2,1)} %bitcast.162), calls=%async_computation.3 | async-start | bytes 1048576 | tf_op jit(solution)/shard_map/all_to_all | solution.py:207
  295.9 20.2 %collective-permute-start.22 = (bf16[128,2816]{1,0:T(8,128)(2,1)}, bf16[128,2816]{1,0:T(8,128)(2,1)S(1)}, u32[]{:S(2)}, u32[]{:S(2)}) collective-permute-start(bf16[128,2816]{1,0:T(8,128)(2,1)} %get-tuple-element.182), channel_id=1, source_target_pairs={{0,16},{8,24},{16,0},{24,8},{1,17},{9,25},{17,1},{25,9},{2,18},{10... | collective-permute-start | bytes 2162696 | tf_op jit(solution)/shard_map/ppermute | solution.py:199
  297.8 19.4 %collective-permute-start.21 = (bf16[128,2816]{1,0:T(8,128)(2,1)}, bf16[128,2816]{1,0:T(8,128)(2,1)}, u32[]{:S(2)}, u32[]{:S(2)}) collective-permute-start(bf16[128,2816]{1,0:T(8,128)(2,1)} %get-tuple-element.183), channel_id=1, source_target_pairs={{0,8},{8,0},{16,24},{24,16},{1,9},{9,1},{17,25},{25,17},{2,10},{10... | collective-permute-start | bytes 2162696 | tf_op jit(solution)/shard_map/ppermute | solution.py:199
  317.3 70.0 %all-to-all-start.4 = ((bf16[16,32,1536]{2,1,0:T(8,128)(2,1)}), bf16[16,32,1536]{2,1,0:T(8,128)(2,1)}, u32[]{:S(2)}, u32[]{:S(2)}) async-start(bf16[16,32,1536]{2,1,0:T(8,128)(2,1)} %copy-done.3), calls=%async_computation.4 | async-start | bytes 3145728 | tf_op jit(solution)/shard_map/all_to_all | solution.py:207
  335.3 51.9 %collective-permute-start.26 = (bf16[128,3840]{1,0:T(8,128)(2,1)}, bf16[128,3840]{1,0:T(8,128)(2,1)S(1)}, u32[]{:S(2)}, u32[]{:S(2)}) collective-permute-start(bf16[128,3840]{1,0:T(8,128)(2,1)} %pad_maximum_fusion.6), channel_id=1, source_target_pairs={{0,8},{8,0},{16,24},{24,16},{1,9},{9,1},{17,25},{25,17},{2,10},{10... | collective-permute-start | bytes 2949128 | tf_op jit(solution)/shard_map/ppermute | solution.py:199
  338.4 48.9 %collective-permute-start.27 = (bf16[128,3840]{1,0:T(8,128)(2,1)}, bf16[128,3840]{1,0:T(8,128)(2,1)}, u32[]{:S(2)}, u32[]{:S(2)}) collective-permute-start(bf16[128,3840]{1,0:T(8,128)(2,1)} %pad_maximum_fusion.7), channel_id=1, source_target_pairs={{0,16},{8,24},{16,0},{24,8},{1,17},{9,25},{17,1},{25,9},{2,18},{10... | collective-permute-start | bytes 2949128 | tf_op jit(solution)/shard_map/ppermute | solution.py:199
  339.9 46.4 %collective-permute-start.24 = (bf16[128,2816]{1,0:T(8,128)(2,1)}, bf16[128,2816]{1,0:T(8,128)(2,1)S(1)}, u32[]{:S(2)}, u32[]{:S(2)}) collective-permute-start(bf16[128,2816]{1,0:T(8,128)(2,1)} %get-tuple-element.181), channel_id=1, source_target_pairs={{0,24},{8,16},{16,8},{24,0},{1,25},{9,17},{17,9},{25,1},{2,26},{10... | collective-permute-start | bytes 2162696 | tf_op jit(solution)/shard_map/ppermute | solution.py:199
  392.1 31.3 %collective-permute-start.29 = (bf16[128,3840]{1,0:T(8,128)(2,1)}, bf16[128,3840]{1,0:T(8,128)(2,1)}, u32[]{:S(2)}, u32[]{:S(2)}) collective-permute-start(bf16[128,3840]{1,0:T(8,128)(2,1)} %pad_maximum_fusion.8), channel_id=1, source_target_pairs={{0,24},{8,16},{16,8},{24,0},{1,25},{9,17},{17,9},{25,1},{2,26},{10... | collective-permute-start | bytes 2949128 | tf_op jit(solution)/shard_map/ppermute | solution.py:199
  393.7 30.7 %all-to-all-start.5 = ((bf16[16,16,1024]{2,1,0:T(8,128)(2,1)}), bf16[16,16,1024]{2,1,0:T(8,128)(2,1)}, u32[]{:S(2)}, u32[]{:S(2)}) async-start(bf16[16,16,1024]{2,1,0:T(8,128)(2,1)} %bitcast.159), calls=%async_computation.5 | async-start | bytes 1048576 | tf_op jit(solution)/shard_map/all_to_all | solution.py:207
  406.6 34.2 %collective-permute-start.30 = (bf16[256,1536]{1,0:T(8,128)(2,1)}, bf16[256,1536]{1,0:T(8,128)(2,1)}, u32[]{:S(2)}, u32[]{:S(2)}) collective-permute-start(bf16[256,1536]{1,0:T(8,128)(2,1)} %pad_maximum_fusion.10), channel_id=1, source_target_pairs={{0,8},{8,0},{16,24},{24,16},{1,9},{9,1},{17,25},{25,17},{2,10},{10... | collective-permute-start | bytes 2359304 | tf_op jit(solution)/shard_map/ppermute | solution.py:199
  408.6 32.3 %collective-permute-start.31 = (bf16[256,1536]{1,0:T(8,128)(2,1)}, bf16[256,1536]{1,0:T(8,128)(2,1)}, u32[]{:S(2)}, u32[]{:S(2)}) collective-permute-start(bf16[256,1536]{1,0:T(8,128)(2,1)} %pad_maximum_fusion.11), channel_id=1, source_target_pairs={{0,16},{8,24},{16,0},{24,8},{1,17},{9,25},{17,1},{25,9},{2,18},{10... | collective-permute-start | bytes 2359304 | tf_op jit(solution)/shard_map/ppermute | solution.py:199
  441.0 29.0 %collective-permute-start.33 = (bf16[256,1536]{1,0:T(8,128)(2,1)}, bf16[256,1536]{1,0:T(8,128)(2,1)}, u32[]{:S(2)}, u32[]{:S(2)}) collective-permute-start(bf16[256,1536]{1,0:T(8,128)(2,1)} %pad_maximum_fusion.12), channel_id=1, source_target_pairs={{0,24},{8,16},{16,8},{24,0},{1,25},{9,17},{17,9},{25,1},{2,26},{10... | collective-permute-start | bytes 2359304 | tf_op jit(solution)/shard_map/ppermute | solution.py:199
  446.8 31.5 %all-to-all-start.6 = ((bf16[16,16,1024]{2,1,0:T(8,128)(2,1)}), bf16[16,16,1024]{2,1,0:T(8,128)(2,1)}, u32[]{:S(2)}, u32[]{:S(2)}) async-start(bf16[16,16,1024]{2,1,0:T(8,128)(2,1)} %bitcast.148), calls=%async_computation.6 | async-start | bytes 1048576 | tf_op jit(solution)/shard_map/all_to_all | solution.py:207
  (69 other events, 393.6 us)
